TPU v7x, 32 devices: a whole 2x2x4 slice. The times are simulated.
32 devices in a mesh: sx: 8 (over z, x), sy: 4 (over y, core).
Axes of the slice: x: 2, y: 2, z: 4, core: 2. Of those that a mesh axis runs over, the one named last changes fastest.
Arguments:
- charges: bfloat16 [2048, 64, 128], P(('sx', 'sy')), may hold values from -6 to 6
- near_blocks: bfloat16 [2048, 6, 128, 128], P(('sx', 'sy')), may hold values from -0.21875 to 0.21875
- near_list: int32 [2048, 6], P(('sx', 'sy')), may hold values from 0 to 2047, as said below
- leaf_basis: bfloat16 [2048, 64, 128], P(('sx', 'sy')), may hold values from -0.5 to 0.5
- child_transfer: bfloat16 [2048, 64, 64], P(('sx', 'sy')), may hold values from -0.5 to 0.5
- parent_transfer: bfloat16 [256, 64, 64], P(('sx', 'sy')), may hold values from -0.5 to 0.5
- m2l_ops: bfloat16 [2, 316, 64, 64], replicated, may hold values from -0.15625 to 0.15625
- far_list0: int32 [2048, 24], P(('sx', 'sy')), may hold values from 0 to 2047, as said below
- far_op0: int32 [2048, 24], P(('sx', 'sy')), may hold values from 0 to 315
- far_list1: int32 [256, 24], P(('sx', 'sy')), may hold values from 0 to 255, as said below
- far_op1: int32 [256, 24], P(('sx', 'sy')), may hold values from 0 to 315
- top_transfer: float32 [64, 64], replicated, may hold values from -0.5 to 0.5
- top_couple: float32 [64, 64], replicated, may hold values from -0.75 to 0.75
Outputs:
- product: float32 [2048, 64, 128], P(('sx', 'sy'))
Inputs may be any that keep to these rules, and one draw needn't show every extreme that they name: `near_list`: each entry is a leaf id whose distance from its own row's leaf id is at most 64; entry 0 is the row's own leaf; the distance 64 is taken. `far_list0`: each entry is a leaf id whose distance from its own row's leaf id is at most 64; the distance 64 is taken. `far_list1`: each entry is a parent id whose distance from its own row's parent id is at most 8; the distance 8 is taken.
All inputs are finite; a program needn't handle non-finite values.
Results may differ from a plain program's by a relative error of at most 0.008.
Values may be sent and summed in bfloat16 or wider, within the bound.
No kernel may reach another device: no remote copies, remote signals or barrier semaphores. Data moves between devices by JAX's collectives and lax.ppermute only.
A program may use at most 192 MiB of HBM per device.

v0:
```python
import jax
import jax.numpy as jnp
from jax import lax
from jax.sharding import PartitionSpec as P

highest = lax.Precision.HIGHEST


def extended_2(cells, sides, width):
    for axis, dim in sides:
        count = lax.axis_size(axis)
        ends = count - 1
        head = lax.slice_in_dim(cells, 0, width, axis=dim)
        tail = lax.slice_in_dim(cells, cells.shape[dim] - width, cells.shape[dim], axis=dim)
        cells = jnp.concatenate(
            [
                lax.ppermute(tail, axis, [(i, (i + 1) % count) for i in range(ends)]),
                cells,
                lax.ppermute(head, axis, [((i + 1) % count, i) for i in range(ends)]),
            ],
            axis=dim,
        )
    return cells


def from_partner(block, axis, apart):
    count = lax.axis_size(axis)
    route = []
    for low in range(count):
        high = low | 1 << apart
        if high != low and high < count:
            route += [(low, high), (high, low)]
    return lax.ppermute(block, axis, route)


def translate(extended, local_ids, op_ids, table):
    picked = jnp.take(extended, local_ids, axis=0)
    matrices = jnp.take(table, op_ids, axis=0)
    return jnp.einsum("nerk,nekj->nrj", picked, matrices, preferred_element_type=jnp.float32)


def local(
    charges,
    near_blocks,
    near_list,
    leaf_basis,
    child_transfer,
    parent_transfer,
    m2l_ops,
    far_list0,
    far_op0,
    far_list1,
    far_op1,
    top_transfer,
    top_couple,
):
    leaf_count = charges.shape[0]
    parent_count = parent_transfer.shape[0]
    columns = charges.shape[1]
    rank = leaf_basis.shape[1]
    device = lax.axis_index(("sx", "sy"))
    moments = jnp.einsum(
        "lrp,lkp->lrk", charges, leaf_basis, preferred_element_type=jnp.float32
    ).astype(jnp.bfloat16)
    charge_ext = extended_2(charges, ((("sx", "sy"), 0),), leaf_count)
    moment_ext = extended_2(moments, ((("sx", "sy"), 0),), leaf_count)
    child_groups = child_transfer.reshape(parent_count, 8, rank, rank)
    parent_moments = jnp.einsum(
        "pcrk,pckj->prj",
        moments.reshape(parent_count, 8, columns, rank),
        child_groups,
        preferred_element_type=jnp.float32,
    ).astype(jnp.bfloat16)
    box_moment = jnp.einsum(
        "prk,pkj->rj", parent_moments, parent_transfer, preferred_element_type=jnp.float32
    )
    height = lax.axis_size(("sx", "sy")).bit_length() - 1
    siblings = []
    current = box_moment
    for level_bit in range(height):
        partner = from_partner(current, ("sx", "sy"), level_bit)
        siblings.append(partner)
        if level_bit + 1 < height:
            current = jnp.einsum("rk,kj->rj", current + partner, top_transfer, precision=highest)
    local_field = jnp.zeros_like(box_moment)
    for level_bit in reversed(range(height)):
        local_field = jnp.einsum(
            "rj,kj->rk", local_field, top_transfer, precision=highest
        ) + jnp.einsum("rk,kj->rj", siblings[level_bit], top_couple, precision=highest)
    box_local = local_field.astype(jnp.bfloat16)
    parent_ext = extended_2(parent_moments, ((("sx", "sy"), 0),), parent_count)
    parent_local = jnp.einsum(
        "rj,pkj->prk", box_local, parent_transfer, preferred_element_type=jnp.float32
    )
    parent_local = parent_local + translate(
        parent_ext, far_list1 - device * parent_count + parent_count, far_op1, m2l_ops[1]
    )
    parent_local = parent_local.astype(jnp.bfloat16)
    leaf_local = jnp.einsum(
        "prj,pckj->pcrk", parent_local, child_groups, preferred_element_type=jnp.float32
    ).reshape(leaf_count, columns, rank)
    leaf_local = leaf_local + translate(
        moment_ext, far_list0 - device * leaf_count + leaf_count, far_op0, m2l_ops[0]
    )
    leaf_local = leaf_local.astype(jnp.bfloat16)
    far_part = jnp.einsum(
        "lrk,lkp->lrp", leaf_local, leaf_basis, preferred_element_type=jnp.float32
    )
    local_near = near_list - device * leaf_count + leaf_count
    near_sources = jnp.take(charge_ext, local_near, axis=0)
    near_part = jnp.einsum(
        "lnrq,lnpq->lrp", near_sources, near_blocks, preferred_element_type=jnp.float32
    )
    return far_part + near_part


def solution(mesh):
    placed = (
        P(("sx", "sy"), None, None),
        P(("sx", "sy"), None, None, None),
        P(("sx", "sy"), None),
        P(("sx", "sy"), None, None),
        P(("sx", "sy"), None, None),
        P(("sx", "sy"), None, None),
        P(),
        P(("sx", "sy"), None),
        P(("sx", "sy"), None),
        P(("sx", "sy"), None),
        P(("sx", "sy"), None),
        P(),
        P(),
    )
    return jax.shard_map(
        local, mesh=mesh, in_specs=placed, out_specs=P(("sx", "sy"), None, None), check_vma=False
    )
```

profile of v0, /device:TPU:0, one launch (start us, length us, event | category | flops | bytes accessed | tf_op | source)
XLA Modules:
  0.0 214.5 jit_solution(2745351473095102526)
XLA Ops:
  1.2 1.9 convolution_convert_fusion
  4.8 3.0 %collective-permute-start.5 = (bf16[8,64,64]{2,1,0:T(8,128)(2,1)S(1)}, bf16[8,64,64]{2,1,0:T(8,128)(2,1)S(1)}, u32[]{:S(2)}, u32[]{:S(2)}) collective-permute-start(bf16[8,64,64]{2,1,0:T(8,128)(2,1)S(1)} %fusion.38), channel_id=1, source_target_pairs={{0,1},{1,2},{2,3},{3,4},{4,5},{5,6},{6,7},{7,8},{8,9},{9,10},{10,1... | collective-permute-start | bytes 196616 | tf_op jit(solution)/shard_map/ppermute | solution.py:17
  9.2 6.1 %collective-permute-start.7 = (bf16[64,64,64]{2,1,0:T(8,128)(2,1)S(1)}, bf16[64,64,64]{2,1,0:T(8,128)(2,1)}, u32[]{:S(2)}, u32[]{:S(2)}) collective-permute-start(bf16[64,64,64]{2,1,0:T(8,128)(2,1)S(1)} %convolution_convert_fusion), channel_id=1, source_target_pairs={{0,1},{1,2},{2,3},{3,4},{4,5},{5,6},{6,7},{7,8},{8,9},{9,10},{10,1... | collective-permute-start | bytes 1572872 | tf_op jit(solution)/shard_map/ppermute | solution.py:17
  16.6 6.2 %fusion.66 = (bf16[1,316,64,64]{1,3,2,0:T(8,128)(2,1)}, bf16[1,316,64,64]{1,3,2,0:T(8,128)(2,1)}) fusion(bf16[2,316,64,64]{1,3,2,0:T(8,128)(2,1)} %param.19), kind=kLoop, calls=%fused_computation.73 | loop fusion | bytes 10354688 | tf_op jit(solution)/shard_map/slice | solution.py:103
  23.6 3.3 %collective-permute-start.1 = (f32[64,64]{1,0:T(8,128)S(1)}, f32[64,64]{1,0:T(8,128)S(1)}, u32[]{:S(2)}, u32[]{:S(2)}) collective-permute-start(f32[64,64]{1,0:T(8,128)S(1)} %fusion.57), channel_id=1, source_target_pairs={{0,2},{2,0},{1,3},{3,1},{4,6},{6,4},{5,7},{7,5},{8,10},{10,8},{9,1... | collective-permute-start | bytes 49160 | tf_op jit(solution)/shard_map/ppermute | solution.py:33
  27.0 1.8 collective-permute-done.1
  28.9 11.5 %collective-permute-start.2 = (f32[64,64]{1,0:T(8,128)S(1)}, f32[64,64]{1,0:T(8,128)S(1)}, u32[]{:S(2)}, u32[]{:S(2)}) collective-permute-start(f32[64,64]{1,0:T(8,128)S(1)} %fusion.55), channel_id=1, source_target_pairs={{0,4},{4,0},{1,5},{5,1},{2,6},{6,2},{3,7},{7,3},{8,12},{12,8},{9,1... | collective-permute-start | bytes 49160 | tf_op jit(solution)/shard_map/ppermute | solution.py:33
  40.6 1.7 collective-permute-done.2
  42.5 3.4 %collective-permute-start.3 = (f32[64,64]{1,0:T(8,128)S(1)}, f32[64,64]{1,0:T(8,128)S(1)}, u32[]{:S(2)}, u32[]{:S(2)}) collective-permute-start(f32[64,64]{1,0:T(8,128)S(1)} %fusion.53), channel_id=1, source_target_pairs={{0,8},{8,0},{1,9},{9,1},{2,10},{10,2},{3,11},{11,3},{4,12},{12,4},... | collective-permute-start | bytes 49160 | tf_op jit(solution)/shard_map/ppermute | solution.py:33
  45.9 10.0 %copy.32 = bf16[1,316,64,64]{3,2,1,0:T(8,128)(2,1)} copy(bf16[1,316,64,64]{1,3,2,0:T(8,128)(2,1)} %get-tuple-element.12) | data formatting | bytes 5177344
  55.9 10.0 %copy.33 = bf16[1,316,64,64]{3,2,1,0:T(8,128)(2,1)} copy(bf16[1,316,64,64]{1,3,2,0:T(8,128)(2,1)} %get-tuple-element.11) | data formatting | bytes 5177344
  66.2 5.2 %gather_fusion.1 = bf16[192,64,64]{2,1,0:T(8,128)(2,1)} fusion(bf16[316,64,64]{2,1,0:T(8,128)(2,1)} %bitcast.88, s32[1024]{0:T(1024)S(1)} %pad_clamp_fusion.3), kind=kCustom, calls=%fused_computation.1 | custom fusion | bytes 3146496 | tf_op jit(solution)/shard_map/jit(_take)/gather | solution.py:38
  71.4 36.2 %gather_fusion.3 = bf16[1536,64,64]{2,1,0:T(8,128)(2,1)} fusion(bf16[316,64,64]{2,1,0:T(8,128)(2,1)} %bitcast.84, s32[2048]{0:T(1024)S(1)} %pad_clamp_fusion), kind=kCustom, calls=%fused_computation.3 | custom fusion | bytes 25171968 | tf_op jit(solution)/shard_map/jit(_take)/gather | solution.py:38
  109.1 4.0 %collective-permute-start.9 = (bf16[64,64,128]{2,1,0:T(8,128)(2,1)}, bf16[64,64,128]{2,1,0:T(8,128)(2,1)}, u32[]{:S(2)}, u32[]{:S(2)}) collective-permute-start(bf16[64,64,128]{2,1,0:T(8,128)(2,1)} %param.13), channel_id=1, source_target_pairs={{0,1},{1,2},{2,3},{3,4},{4,5},{5,6},{6,7},{7,8},{8,9},{9,10},{10,1... | collective-permute-start | bytes 3145736 | tf_op jit(solution)/shard_map/ppermute | solution.py:17
  113.1 1.8 collective-permute-start.4
  115.1 2.8 %gather_fusion = bf16[192,64,64]{2,1,0:T(8,128)(2,1)} fusion(bf16[24,64,64]{2,1,0:T(8,128)(2,1)S(1)} %pad_maximum_fusion.2, s32[1024]{0:T(1024)S(1)} %pad_clamp_fusion.4), kind=kCustom, calls=%fused_computation | custom fusion | bytes 3146496 | tf_op jit(solution)/shard_map/jit(_take)/gather | solution.py:37
  117.8 8.4 %collective-permute-done.4 = f32[64,64]{1,0:T(8,128)S(1)} collective-permute-done((f32[64,64]{1,0:T(8,128)S(1)}, f32[64,64]{1,0:T(8,128)S(1)}, u32[]{:S(2)}, u32[]{:S(2)}) %collective-permute-start.4) | collective-permute-done | bytes 16416 | tf_op jit(solution)/shard_map/ppermute | solution.py:33
  128.1 6.9 %fusion.46 = f32[8,64,8,64]{3,1,2,0:T(8,128)} fusion(bf16[8,8,64,64]{3,2,1,0:T(8,128)(2,1)} %bitcast.92, f32[8,64,64]{2,1,0:T(8,128)S(1)} %convolution_bitcast_fusion, bf16[8,24,64,64]{3,2,1,0:T(8,128)(2,1)} %bitcast.90, pred[8,24]{1,0:T(8,128)(4,1)S(1)} %compare_and_fusion.3, bf16[8,24,64,64]{3,2,1,0:T(8,128)(2,1)} %bitcast.91, ...), kind=kOutput, calls=%fused_computation.34 | convolution fusion | flops 135856128 | bytes 4850048 | tf_op jit(solution)/shard_map/prj,pckj->pcrk/dot_general | solution.py:99
  135.0 3.2 %pad_maximum_fusion = bf16[192,64,64]{2,1,0:T(8,128)(2,1)} fusion(bf16[64,64,64]{2,1,0:T(8,128)(2,1)} %collective-permute-done.8, bf16[64,64,64]{2,1,0:T(8,128)(2,1)S(1)} %convolution_convert_fusion, bf16[64,64,64]{2,1,0:T(8,128)(2,1)} %collective-permute-done.7), kind=kLoop, calls=%fused_computation.14 | loop fusion | flops 1572864 | bytes 3145728 | tf_op jit(solution)/shard_map/concatenate | solution.py:15
  138.2 35.4 %gather_fusion.2 = bf16[1536,64,64]{2,1,0:T(8,128)(2,1)} fusion(bf16[192,64,64]{2,1,0:T(8,128)(2,1)} %pad_maximum_fusion, s32[2048]{0:T(1024)S(1)} %pad_clamp_fusion.1), kind=kCustom, calls=%fused_computation.2 | custom fusion | bytes 25171968 | tf_op jit(solution)/shard_map/jit(_take)/gather | solution.py:37
  173.6 18.9 %fusion.15 = bf16[64,64,64]{2,1,0:T(8,128)(2,1)S(1)} fusion(f32[8,64,8,64]{3,1,2,0:T(8,128)} %fusion.46, bf16[64,24,64,64]{3,2,1,0:T(8,128)(2,1)} %bitcast.86, pred[64,24]{1,0:T(8,128)(4,1)S(1)} %copy.22, bf16[64,24,64,64]{3,2,1,0:T(8,128)(2,1)} %bitcast.87, pred[64,24]{1,0:T(8,128)(4,1)S(1)} %copy.20), kind=kOutput, calls=%fused_computation.23 | convolution fusion | flops 818413568 | bytes 26741760 | tf_op jit(solution)/shard_map/nerk,nekj->nrj/dot_general | solution.py:39
  193.0 3.3 %pad_maximum_fusion.1 = bf16[192,64,128]{2,1,0:T(8,128)(2,1)} fusion(bf16[64,64,128]{2,1,0:T(8,128)(2,1)} %collective-permute-done.10, bf16[64,64,128]{2,1,0:T(8,128)(2,1)} %param.13, bf16[64,64,128]{2,1,0:T(8,128)(2,1)} %collective-permute-done.9), kind=kLoop, calls=%fused_computation.15 | loop fusion | flops 3145728 | bytes 6291456 | tf_op jit(solution)/shard_map/concatenate | solution.py:15
  196.3 5.9 %gather_fusion.4 = bf16[384,64,128]{2,1,0:T(8,128)(2,1)} fusion(bf16[192,64,128]{2,1,0:T(8,128)(2,1)} %pad_maximum_fusion.1, s32[1024]{0:T(1024)S(1)} %pad_clamp_fusion.2), kind=kCustom, calls=%fused_computation.4 | custom fusion | bytes 12584448 | tf_op jit(solution)/shard_map/jit(_take)/gather | solution.py:110
  202.2 12.3 %bitcast_add_fusion.1 = f32[64,64,128]{2,1,0:T(8,128)} fusion(f32[64,64,128]{2,1,0:T(8,128)S(1)} %fusion.71, bf16[64,6,128,128]{3,2,1,0:T(8,128)(2,1)} %param.14, bf16[64,6,64,128]{3,2,1,0:T(8,128)(2,1)} %bitcast.85, pred[64,6]{1,0:T(8,128)(4,1)S(1)} %copy.25), kind=kOutput, calls=%fused_computation.24 | convolution fusion | flops 808976384 | bytes 23069056 | tf_op jit(solution)/shard_map/lnrq,lnpq->lrp/dot_general | solution.py:111
  (74 shorter events, 10.8 us)
Async XLA Ops:
  0.0 1.2 copy-start
  0.0 3.1 %copy-start.2 = (bf16[64,64,64]{2,1,0:T(8,128)(2,1)S(1)}, bf16[64,64,64]{2,1,0:T(8,128)(2,1)}, u32[]{:S(2)}) copy-start(bf16[64,64,64]{2,1,0:T(8,128)(2,1)} %param.17) | copy-start | bytes 1572868
  0.0 15.3 %copy-start.4 = (bf16[8,64,64]{2,1,0:T(8,128)(2,1)S(1)}, bf16[8,64,64]{2,1,0:T(8,128)(2,1)}, u32[]{:S(2)}) copy-start(bf16[8,64,64]{2,1,0:T(8,128)(2,1)} %param.18) | copy-start | bytes 196612
  0.0 16.3 %copy-start.6 = (s32[8,24]{1,0:T(8,128)S(1)}, s32[8,24]{1,0:T(8,128)}, u32[]{:S(2)}) copy-start(s32[8,24]{1,0:T(8,128)} %param.23) | copy-start | bytes 2308
  0.0 16.3 %copy-start.5 = (s32[64,24]{0,1:T(8,128)S(1)}, s32[64,24]{0,1:T(8,128)}, u32[]{:S(2)}) copy-start(s32[64,24]{0,1:T(8,128)} %param.21) | copy-start | bytes 18436
  0.0 16.3 %copy-start.1 = (f32[64,64]{1,0:T(8,128)S(1)}, f32[64,64]{1,0:T(8,128)}, u32[]{:S(2)}) copy-start(f32[64,64]{1,0:T(8,128)} %param.24) | copy-start | bytes 49156
  3.5 105.5 %collective-permute-start.6 = (bf16[8,64,64]{2,1,0:T(8,128)(2,1)S(1)}, bf16[8,64,64]{2,1,0:T(8,128)(2,1)S(1)}, u32[]{:S(2)}, u32[]{:S(2)}) collective-permute-start(bf16[8,64,64]{2,1,0:T(8,128)(2,1)S(1)} %fusion.38), channel_id=1, source_target_pairs={{1,0},{2,1},{3,2},{4,3},{5,4},{6,5},{7,6},{8,7},{9,8},{10,9},{11,1... | collective-permute-start | bytes 196616 | tf_op jit(solution)/shard_map/ppermute | solution.py:19
  4.8 108.3 %collective-permute-start.5 = (bf16[8,64,64]{2,1,0:T(8,128)(2,1)S(1)}, bf16[8,64,64]{2,1,0:T(8,128)(2,1)S(1)}, u32[]{:S(2)}, u32[]{:S(2)}) collective-permute-start(bf16[8,64,64]{2,1,0:T(8,128)(2,1)S(1)} %fusion.38), channel_id=1, source_target_pairs={{0,1},{1,2},{2,3},{3,4},{4,5},{5,6},{6,7},{7,8},{8,9},{9,10},{10,1... | collective-permute-start | bytes 196616 | tf_op jit(solution)/shard_map/ppermute | solution.py:17
  7.9 127.1 %collective-permute-start.8 = (bf16[64,64,64]{2,1,0:T(8,128)(2,1)S(1)}, bf16[64,64,64]{2,1,0:T(8,128)(2,1)}, u32[]{:S(2)}, u32[]{:S(2)}) collective-permute-start(bf16[64,64,64]{2,1,0:T(8,128)(2,1)S(1)} %convolution_convert_fusion), channel_id=1, source_target_pairs={{1,0},{2,1},{3,2},{4,3},{5,4},{6,5},{7,6},{8,7},{9,8},{10,9},{11,1... | collective-permute-start | bytes 1572872 | tf_op jit(solution)/shard_map/ppermute | solution.py:19
  9.2 125.8 %collective-permute-start.7 = (bf16[64,64,64]{2,1,0:T(8,128)(2,1)S(1)}, bf16[64,64,64]{2,1,0:T(8,128)(2,1)}, u32[]{:S(2)}, u32[]{:S(2)}) collective-permute-start(bf16[64,64,64]{2,1,0:T(8,128)(2,1)S(1)} %convolution_convert_fusion), channel_id=1, source_target_pairs={{0,1},{1,2},{2,3},{3,4},{4,5},{5,6},{6,7},{7,8},{8,9},{9,10},{10,1... | collective-permute-start | bytes 1572872 | tf_op jit(solution)/shard_map/ppermute | solution.py:17
  15.5 7.9 %collective-permute-start = (f32[64,64]{1,0:T(8,128)S(1)}, f32[64,64]{1,0:T(8,128)S(1)}, u32[]{:S(2)}, u32[]{:S(2)}) collective-permute-start(f32[64,64]{1,0:T(8,128)S(1)} %convolution_bitcast_fusion.2), channel_id=1, source_target_pairs={{0,1},{1,0},{2,3},{3,2},{4,5},{5,4},{6,7},{7,6},{8,9},{9,8},{10,11... | collective-permute-start | bytes 49160 | tf_op jit(solution)/shard_map/ppermute | solution.py:33
  16.6 6.5 %copy-start.7 = (s32[64,24]{0,1:T(8,128)S(1)}, s32[64,24]{0,1:T(8,128)}, u32[]{:S(2)}) copy-start(s32[64,24]{0,1:T(8,128)} %param.20) | copy-start | bytes 18436
  16.6 6.7 %copy-start.8 = (s32[64,6]{0,1:T(8,128)S(1)}, s32[64,6]{0,1:T(8,128)}, u32[]{:S(2)}) copy-start(s32[64,6]{0,1:T(8,128)} %param.15) | copy-start | bytes 4612
  16.6 6.7 %copy-start.9 = (s32[8,24]{1,0:T(8,128)S(1)}, s32[8,24]{1,0:T(8,128)}, u32[]{:S(2)}) copy-start(s32[8,24]{1,0:T(8,128)} %param.22) | copy-start | bytes 2308
  23.6 5.2 %collective-permute-start.1 = (f32[64,64]{1,0:T(8,128)S(1)}, f32[64,64]{1,0:T(8,128)S(1)}, u32[]{:S(2)}, u32[]{:S(2)}) collective-permute-start(f32[64,64]{1,0:T(8,128)S(1)} %fusion.57), channel_id=1, source_target_pairs={{0,2},{2,0},{1,3},{3,1},{4,6},{6,4},{5,7},{7,5},{8,10},{10,8},{9,1... | collective-permute-start | bytes 49160 | tf_op jit(solution)/shard_map/ppermute | solution.py:33
  28.9 13.4 %collective-permute-start.2 = (f32[64,64]{1,0:T(8,128)S(1)}, f32[64,64]{1,0:T(8,128)S(1)}, u32[]{:S(2)}, u32[]{:S(2)}) collective-permute-start(f32[64,64]{1,0:T(8,128)S(1)} %fusion.55), channel_id=1, source_target_pairs={{0,4},{4,0},{1,5},{5,1},{2,6},{6,2},{3,7},{7,3},{8,12},{12,8},{9,1... | collective-permute-start | bytes 49160 | tf_op jit(solution)/shard_map/ppermute | solution.py:33
  42.5 65.1 %collective-permute-start.3 = (f32[64,64]{1,0:T(8,128)S(1)}, f32[64,64]{1,0:T(8,128)S(1)}, u32[]{:S(2)}, u32[]{:S(2)}) collective-permute-start(f32[64,64]{1,0:T(8,128)S(1)} %fusion.53), channel_id=1, source_target_pairs={{0,8},{8,0},{1,9},{9,1},{2,10},{10,2},{3,11},{11,3},{4,12},{12,4},... | collective-permute-start | bytes 49160 | tf_op jit(solution)/shard_map/ppermute | solution.py:33
  107.6 85.4 %collective-permute-start.10 = (bf16[64,64,128]{2,1,0:T(8,128)(2,1)}, bf16[64,64,128]{2,1,0:T(8,128)(2,1)}, u32[]{:S(2)}, u32[]{:S(2)}) collective-permute-start(bf16[64,64,128]{2,1,0:T(8,128)(2,1)} %param.13), channel_id=1, source_target_pairs={{1,0},{2,1},{3,2},{4,3},{5,4},{6,5},{7,6},{8,7},{9,8},{10,9},{11,1... | collective-permute-start | bytes 3145736 | tf_op jit(solution)/shard_map/ppermute | solution.py:19
  109.1 83.9 %collective-permute-start.9 = (bf16[64,64,128]{2,1,0:T(8,128)(2,1)}, bf16[64,64,128]{2,1,0:T(8,128)(2,1)}, u32[]{:S(2)}, u32[]{:S(2)}) collective-permute-start(bf16[64,64,128]{2,1,0:T(8,128)(2,1)} %param.13), channel_id=1, source_target_pairs={{0,1},{1,2},{2,3},{3,4},{4,5},{5,6},{6,7},{7,8},{8,9},{9,10},{10,1... | collective-permute-start | bytes 3145736 | tf_op jit(solution)/shard_map/ppermute | solution.py:17
  113.1 13.1 %collective-permute-start.4 = (f32[64,64]{1,0:T(8,128)S(1)}, f32[64,64]{1,0:T(8,128)S(1)}, u32[]{:S(2)}, u32[]{:S(2)}) collective-permute-start(f32[64,64]{1,0:T(8,128)S(1)} %fusion.51), channel_id=1, source_target_pairs={{0,16},{16,0},{1,17},{17,1},{2,18},{18,2},{3,19},{19,3},{4,20},{20... | collective-permute-start | bytes 49160 | tf_op jit(solution)/shard_map/ppermute | solution.py:33
  115.1 11.2 %copy-start.3 = (f32[64,64]{1,0:T(8,128)S(1)}, f32[64,64]{1,0:T(8,128)}, u32[]{:S(2)}) copy-start(f32[64,64]{1,0:T(8,128)} %param.25) | copy-start | bytes 49156
where the time goes:
time: 215 us; the launch traced here: 214 us
  local copies, waits for them, and re-layouts  114 us (53%)
  matrix products  43.6 us (20%)
  starting transfers between devices  37.9 us (18%)
  waiting for transfers between devices  11.9 us (6%)
  other arithmetic  6.72 us (3%)
    gather x2, local copies, waits for them, and re-layouts, translate(): matrices = jnp.take(table, op_ids, axis=0)  41.3 us
    gather x2, local copies, waits for them, and re-layouts, translate(): picked = jnp.take(extended, local_ids, axis=0)  38.1 us
    unnamed x22, local copies, waits for them, and re-layouts  21.3 us
    ppermute x5, starting transfers between devices, from_partner(): return lax.ppermute(block, axis, route)  20.9 us
    dot_general x1, matrix products, translate(): jnp.einsum('nerk,nekj->nrj', picked, matrices, preferred_element_type=jnp...  18.9 us
    ppermute x3, starting transfers between devices, extended_2(): lax.ppermute(tail, axis, [(i, (i + 1) % count) for i in range(ends)])  13.2 us
    dot_general x1, matrix products, local(): jnp.einsum('lnrq,lnpq->lrp', near_sources, near_blocks, preferred_element...  12.3 us
    ppermute x5, waiting for transfers between devices, from_partner(): return lax.ppermute(block, axis, route)  11.9 us
  transfers between devices with their start and end apart: 11, of which 3 were waited for; matrix products, arithmetic and copies ran while one was open for 65% of the time, Pallas kernels for 0%

commit v1 on v0

v1 whole, which is shorter than its diff:
```python
import functools

import jax
import jax.numpy as jnp
from jax import lax
from jax.experimental import pallas as pl
from jax.experimental.pallas import tpu as pltpu
from jax.sharding import PartitionSpec as P

highest = lax.Precision.HIGHEST
AXES = ("sx", "sy")
f32 = jnp.float32
bf16 = jnp.bfloat16
NN = (((1,), (0,)), ((), ()))
NT = (((1,), (1,)), ((), ()))


def mm(a, b, dims=NN, precision=None):
    return lax.dot_general(a, b, dims, precision=precision, preferred_element_type=f32)


def params(mib):
    return pltpu.CompilerParams(
        dimension_semantics=("arbitrary",), vmem_limit_bytes=mib * 1024 * 1024
    )


def moments_kernel(charges, basis, child, parent, send, box):
    step = pl.program_id(0)
    leaf_pairs = 8 * pl.num_programs(0)
    rank = basis.shape[1]
    parents = []
    for p in range(2):
        acc = None
        for i in range(4):
            c = 8 * p + 2 * i
            pair = jnp.concatenate(
                [mm(charges[c], basis[c], NT), mm(charges[c + 1], basis[c + 1], NT)], axis=1
            ).astype(bf16)
            send[step * 8 + p * 4 + i] = pair
            term = mm(pair, child[c : c + 2].reshape(2 * rank, rank))
            acc = term if acc is None else acc + term
        parents.append(acc)
    both = jnp.concatenate(parents, axis=1).astype(bf16)
    send[leaf_pairs + step] = both
    part = mm(both, parent[...].reshape(2 * rank, rank))

    @pl.when(step == 0)
    def _():
        box[...] = part

    @pl.when(step > 0)
    def _():
        box[...] += part


def moments_call(charges, basis, child, parent):
    leaves, columns, points = charges.shape
    rank = basis.shape[1]
    parents = parent.shape[0]
    steps = parents // 2
    pairs = leaves // 2 + parents // 2
    return pl.pallas_call(
        moments_kernel,
        grid=(steps,),
        in_specs=[
            pl.BlockSpec((16, columns, points), lambda i: (i, 0, 0)),
            pl.BlockSpec((16, rank, points), lambda i: (i, 0, 0)),
            pl.BlockSpec((16, rank, rank), lambda i: (i, 0, 0)),
            pl.BlockSpec((2, rank, rank), lambda i: (i, 0, 0)),
        ],
        out_specs=[
            pl.BlockSpec((pairs, columns, 2 * rank), lambda i: (0, 0, 0)),
            pl.BlockSpec((columns, rank), lambda i: (0, 0)),
        ],
        out_shape=[
            jax.ShapeDtypeStruct((pairs, columns, 2 * rank), bf16),
            jax.ShapeDtypeStruct((columns, rank), f32),
        ],
        compiler_params=params(32),
        name="moments",
    )(charges, basis, child, parent)


OPS_BLOCK = 128


def table_kernel(ops, table, turned):
    rank = ops.shape[1]
    half = rank // 2
    stride = turned.shape[0] // half
    for k in range(half):
        both = jnp.concatenate([ops[0, k], ops[0, k + half]], axis=0).astype(f32)
        turned[k * stride : k * stride + OPS_BLOCK, :] = both.T
    for o in range(OPS_BLOCK):
        rows = turned[pl.ds(o, half, stride=stride), :]
        table[0, o] = jnp.concatenate([rows[:, :rank], rows[:, rank:]], axis=0).astype(bf16)


def table_call(ops):
    levels, count, rank, _ = ops.shape
    blocks = pl.cdiv(count, OPS_BLOCK)
    turned_view = jnp.transpose(ops, (0, 2, 3, 1))
    return pl.pallas_call(
        table_kernel,
        grid=(levels, blocks),
        in_specs=[pl.BlockSpec((1, rank, rank, OPS_BLOCK), lambda t, i: (t, 0, 0, i))],
        out_specs=pl.BlockSpec((1, OPS_BLOCK, rank, rank), lambda t, i: (t, i, 0, 0)),
        out_shape=jax.ShapeDtypeStruct((levels, blocks * OPS_BLOCK, rank, rank), bf16),
        scratch_shapes=[pltpu.VMEM((rank // 2 * (OPS_BLOCK + 8), 2 * rank), f32)],
        compiler_params=pltpu.CompilerParams(
            dimension_semantics=("arbitrary", "arbitrary"), vmem_limit_bytes=32 * 1024 * 1024
        ),
        name="operator_table",
    )(turned_view)


NEAR_LEAVES = 8


def near_kernel(base, near, left, own, right, blocks, out, sources, sems):
    step = pl.program_id(0)
    leaves = own.shape[0]

    @pl.when(step == 0)
    def _():
        copies = [
            pltpu.make_async_copy(ref, sources.at[pl.ds(i * leaves, leaves)], sems.at[i])
            for i, ref in enumerate((left, own, right))
        ]
        for copy in copies:
            copy.start()
        for copy in copies:
            copy.wait()

    count = blocks.shape[1]
    for i in range(NEAR_LEAVES):
        row = step * NEAR_LEAVES + i
        acc = None
        for n in range(0, count, 2):
            lhs = jnp.concatenate(
                [sources[near[n, row] - base[0]], sources[near[n + 1, row] - base[0]]], axis=1
            )
            rhs = jnp.concatenate([blocks[i, n], blocks[i, n + 1]], axis=1)
            term = mm(lhs, rhs, NT)
            acc = term if acc is None else acc + term
        out[i] = acc


def near_call(base, near_rows, left, own, right, blocks):
    leaves, columns, points = own.shape
    count = blocks.shape[1]
    hbm = pl.BlockSpec(memory_space=pl.ANY)
    return pl.pallas_call(
        near_kernel,
        grid_spec=pltpu.PrefetchScalarGridSpec(
            num_scalar_prefetch=2,
            grid=(leaves // NEAR_LEAVES,),
            in_specs=[
                hbm,
                hbm,
                hbm,
                pl.BlockSpec((NEAR_LEAVES, count, points, points), lambda i, *_: (i, 0, 0, 0)),
            ],
            out_specs=pl.BlockSpec((NEAR_LEAVES, columns, points), lambda i, *_: (i, 0, 0)),
            scratch_shapes=[
                pltpu.VMEM((3 * leaves, columns, points), bf16),
                pltpu.SemaphoreType.DMA((3,)),
            ],
        ),
        out_shape=jax.ShapeDtypeStruct((leaves, columns, points), f32),
        compiler_params=params(32),
        name="near",
    )(base, near_rows, left, own, right, blocks)


def doubled(pair, low):
    rank = pair.shape[1] // 2
    swapped = jnp.concatenate([pair[:, rank:], pair[:, :rank]], axis=1)
    return jnp.where(low, pair, swapped), jnp.where(low, swapped, pair)


def translated(acc, sources, table, level, lists, ops, base, row, low):
    count = lists.shape[0]
    for e in range(0, count, 4):
        picked = [sources[lists[e + i, row] - base] for i in range(4)]
        lhs = jnp.concatenate(
            [jnp.where(low, picked[0], picked[1]), jnp.where(low, picked[2], picked[3])], axis=1
        )
        rhs = jnp.concatenate([table[level, ops[e + i, row]] for i in range(4)], axis=0)
        acc = acc + mm(lhs, rhs)
    return acc


def far_kernel(
    base, list0, op0, list1, op1,
    left, own, right, table, siblings, transfer, couple, parent, child, basis, near,
    out, leaf_sources, parent_sources, parent_locals,
):
    step = pl.program_id(0)
    parents = pl.num_programs(0)
    leaves = 8 * parents
    columns = own.shape[1]
    rank = own.shape[2] // 2
    low = lax.broadcasted_iota(jnp.int32, (columns, 2 * rank), 1) < rank

    @pl.when(step == 0)
    def _():
        for i, ref in enumerate((left, own, right)):
            def leaf_pair(n, _, i=i, ref=ref):
                a, b = doubled(ref[n], low)
                leaf_sources[i * leaves + 2 * n] = a
                leaf_sources[i * leaves + 2 * n + 1] = b
                return 0

            lax.fori_loop(0, leaves // 2, leaf_pair, 0)

            def parent_pair(n, _, i=i, ref=ref):
                a, b = doubled(ref[leaves // 2 + n], low)
                parent_sources[i * parents + 2 * n] = a
                parent_sources[i * parents + 2 * n + 1] = b
                return 0

            lax.fori_loop(0, parents // 2, parent_pair, 0)
        field = None
        for j in reversed(range(siblings.shape[0])):
            term = mm(siblings[j], couple[...], precision=highest)
            if field is not None:
                term = term + mm(field, transfer[...], NT, precision=highest)
            field = term
        box_local = field.astype(bf16)

        def one_parent(q, _):
            acc = mm(box_local, parent[q], NT)
            acc = translated(acc, parent_sources, table, 1, list1, op1, base[1], q, low)
            parent_locals[q] = acc.astype(bf16)
            return 0

        lax.fori_loop(0, parents, one_parent, 0)

    parent_local = parent_locals[step]
    for c in range(8):
        row = step * 8 + c
        acc = mm(parent_local, child[c], NT)
        acc = translated(acc, leaf_sources, table, 0, list0, op0, base[0], row, low)
        out[c] = near[c] + mm(acc.astype(bf16), basis[c])


def far_call(base, list0, op0, list1, op1, left, own, right, table, siblings, transfer, couple, parent, child, basis, near):
    leaves, rank, points = basis.shape
    parents = parent.shape[0]
    columns = near.shape[1]

    def whole(x):
        return pl.BlockSpec(x.shape, lambda i, *_: (0,) * x.ndim)

    def rows(x):
        return pl.BlockSpec((8,) + x.shape[1:], lambda i, *_: (i,) + (0,) * (x.ndim - 1))

    return pl.pallas_call(
        far_kernel,
        grid_spec=pltpu.PrefetchScalarGridSpec(
            num_scalar_prefetch=5,
            grid=(parents,),
            in_specs=[whole(x) for x in (left, own, right, table, siblings, transfer, couple, parent)]
            + [rows(x) for x in (child, basis, near)],
            out_specs=rows(near),
            scratch_shapes=[
                pltpu.VMEM((3 * leaves, columns, 2 * rank), bf16),
                pltpu.VMEM((3 * parents, columns, 2 * rank), bf16),
                pltpu.VMEM((parents, columns, rank), bf16),
            ],
        ),
        out_shape=jax.ShapeDtypeStruct((leaves, columns, points), f32),
        compiler_params=params(56),
        name="far",
    )(base, list0, op0, list1, op1, left, own, right, table, siblings, transfer, couple, parent, child, basis, near)


def to_right(block):
    count = lax.axis_size(AXES)
    return lax.ppermute(block, AXES, [(i, i + 1) for i in range(count - 1)])


def to_left(block):
    count = lax.axis_size(AXES)
    return lax.ppermute(block, AXES, [(i + 1, i) for i in range(count - 1)])


def from_partner(block, apart):
    count = lax.axis_size(AXES)
    return lax.ppermute(block, AXES, [(i, i ^ (1 << apart)) for i in range(count)])


def local(
    charges, near_blocks, near_list, leaf_basis, child_transfer, parent_transfer, m2l_ops,
    far_list0, far_op0, far_list1, far_op1, top_transfer, top_couple,
):
    leaves = charges.shape[0]
    parents = parent_transfer.shape[0]
    device = lax.axis_index(AXES)
    base = jnp.stack([(device - 1) * leaves, (device - 1) * parents]).astype(jnp.int32)
    charges_left = to_right(charges)
    charges_right = to_left(charges)
    send, box = moments_call(charges, leaf_basis, child_transfer, parent_transfer)
    moments_left = to_right(send)
    moments_right = to_left(send)
    height = lax.axis_size(AXES).bit_length() - 1
    siblings = []
    current = box
    for level_bit in range(height):
        partner = from_partner(current, level_bit)
        siblings.append(partner)
        if level_bit + 1 < height:
            current = mm(current + partner, top_transfer, precision=highest)
    table = table_call(m2l_ops)
    near = near_call(base, near_list.T, charges_left, charges, charges_right, near_blocks)
    return far_call(
        base, far_list0.T, far_op0.T, far_list1.T, far_op1.T,
        moments_left, send, moments_right, table, jnp.stack(siblings),
        top_transfer, top_couple, parent_transfer, child_transfer, leaf_basis, near,
    )


def solution(mesh):
    split = P(AXES)
    placed = (split,) * 6 + (P(),) + (split,) * 4 + (P(), P())
    return jax.shard_map(local, mesh=mesh, in_specs=placed, out_specs=split, check_vma=False)
```

time: 215 us -> 105 us (0.49)
  local copies, waits for them, and re-layouts: 114 us -> 14.7 us
  Pallas kernels: 0 us -> 50.6 us
  matrix products: 43.6 us -> 0.64 us
  starting transfers between devices: 37.9 us -> 30.4 us
  other arithmetic: 6.72 us -> 0.07 us
  waiting for transfers between devices: 11.9 us -> 7.78 us
    gather x5 -> x0, local copies, waits for them, and re-layouts: 85.4 us -> none  [the longest x2 41.3 us: translate(): matrices = jnp.take(table, op_ids, axis=0)]
    pallas_call x0 -> x4, Pallas kernels: none -> 50.6 us  [the longest x1 31.3 us: far_call(): pl.pallas_call(far_kernel, grid_spec=pltpu.PrefetchScalarGridSpec(num_sca...]
    dot_general x22 -> x4, matrix products: 43.6 us -> 0.64 us  [mm(): lax.dot_general(a, b, dims, precision=precision, preferred_element_type=f32)]
    ppermute x11 -> x9, starting transfers between devices: 37.9 us -> 30.4 us  [the longest x5 20.2 us: from_partner(): lax.ppermute(block, AXES, [(i, i ^ 1 << apart) for i in range(count)])]
    concatenate x3 -> x0, other arithmetic: 6.63 us -> none  [extended_2(): jnp.concatenate([lax.ppermute(tail, axis, [(i, (i + 1) % count) for i in...]
    unnamed x22 -> x30, local copies, waits for them, and re-layouts: 21.3 us -> 14.7 us
    slice x1 -> x0, local copies, waits for them, and re-layouts: 6.23 us -> none  [local(): m2l_ops[0]]
    ppermute x11 -> x9, waiting for transfers between devices: 11.9 us -> 7.78 us  [the longest x5 7.77 us: from_partner(): lax.ppermute(block, AXES, [(i, i ^ 1 << apart) for i in range(count)])]
  transfers between devices with their start and end apart: 11 -> 9, of which waited for: 3 -> 4; matrix products, arithmetic and copies ran while one was open for 65% -> 3% of each run, Pallas kernels for 0% -> 13%
where the time goes in v1:
time: 105 us; the launch traced here: 104 us
  Pallas kernels  50.6 us (48%)
  starting transfers between devices  30.4 us (29%)
  local copies, waits for them, and re-layouts  14.7 us (14%)
  waiting for transfers between devices  7.78 us (7%)
    pallas_call x1, Pallas kernels, far_call(): pl.pallas_call(far_kernel, grid_spec=pltpu.PrefetchScalarGridSpec(num_sca...  31.3 us
    ppermute x5, starting transfers between devices, from_partner(): lax.ppermute(block, AXES, [(i, i ^ 1 << apart) for i in range(count)])  20.2 us
    unnamed x30, local copies, waits for them, and re-layouts  14.7 us
    ppermute x5, waiting for transfers between devices, from_partner(): lax.ppermute(block, AXES, [(i, i ^ 1 << apart) for i in range(count)])  7.77 us
    ppermute x2, starting transfers between devices, to_right(): return lax.ppermute(block, AXES, [(i, i + 1) for i in range(count - 1)])  7.6 us
    pallas_call x1, Pallas kernels, near_call(): pl.pallas_call(near_kernel, grid_spec=pltpu.PrefetchScalarGridSpec(num_sc...  7.52 us
    pallas_call x1, Pallas kernels, table_call(): pl.pallas_call(table_kernel, grid=(levels, blocks), in_specs=[pl.BlockSpe...  6.28 us
    pallas_call x1, Pallas kernels, moments_call(): pl.pallas_call(moments_kernel, grid=(steps,), in_specs=[pl.BlockSpec((16,...  5.58 us
  transfers between devices with their start and end apart: 9, of which 4 were waited for; matrix products, arithmetic and copies ran while one was open for 3% of the time, Pallas kernels for 13%

profile of v1, /device:TPU:0, one launch (start us, length us, event | category | flops | bytes accessed | tf_op | source)
XLA Modules:
  0.0 104.4 jit_solution(13266558946508320985)
XLA Ops:
  0.0 1.2 %copy-done.4 = bf16[64,64,128]{2,1,0:T(8,128)(2,1)S(1)} copy-done((bf16[64,64,128]{2,1,0:T(8,128)(2,1)S(1)}, bf16[64,64,128]{2,1,0:T(8,128)(2,1)}, u32[]{:S(2)}) %copy-start.4) | copy-done | bytes 1048600
  1.2 1.2 %copy-done.5 = bf16[64,64,64]{2,1,0:T(8,128)(2,1)S(1)} copy-done((bf16[64,64,64]{2,1,0:T(8,128)(2,1)S(1)}, bf16[64,64,64]{2,1,0:T(8,128)(2,1)}, u32[]{:S(2)}) %copy-start.5) | copy-done | bytes 524312
  3.4 5.6 %moments.1 = (bf16[36,64,128]{2,1,0:T(8,128)(2,1)S(1)}, f32[64,64]{1,0:T(8,128)S(1)}) custom-call(bf16[64,64,128]{2,1,0:T(8,128)(2,1)} %own.1, bf16[64,64,128]{2,1,0:T(8,128)(2,1)S(1)} %copy-done.4, bf16[64,64,64]{2,1,0:T(8,128)(2,1)S(1)} %copy-done.5, bf16[8,64,64]{2,1,0:T(8,128)(2,1)S(1)} %copy-done.7), custom_call_target="tpu_custom_call" | custom-call | tf_op jit(solution)/shard_map/moments/pallas_call | solution.py:63
  9.0 1.3 %collective-permute-start.1 = (bf16[36,64,128]{2,1,0:T(8,128)(2,1)S(1)}, bf16[36,64,128]{2,1,0:T(8,128)(2,1)}, u32[]{:S(2)}, u32[]{:S(2)}) collective-permute-start(bf16[36,64,128]{2,1,0:T(8,128)(2,1)S(1)} %get-tuple-element.7.own), channel_id=1, source_target_pairs={{1,0},{2,1},{3,2},{4,3},{5,4},{6,5},{7,6},{8,7},{9,8},{10,9},{11,1... | collective-permute-start | bytes 1769480 | tf_op jit(solution)/shard_map/ppermute | solution.py:287
  10.3 3.8 %collective-permute-start = (bf16[36,64,128]{2,1,0:T(8,128)(2,1)S(1)}, bf16[36,64,128]{2,1,0:T(8,128)(2,1)}, u32[]{:S(2)}, u32[]{:S(2)}) collective-permute-start(bf16[36,64,128]{2,1,0:T(8,128)(2,1)S(1)} %get-tuple-element.7.own), channel_id=1, source_target_pairs={{0,1},{1,2},{2,3},{3,4},{4,5},{5,6},{6,7},{7,8},{8,9},{9,10},{10,1... | collective-permute-start | bytes 1769480 | tf_op jit(solution)/shard_map/ppermute | solution.py:282
  14.1 3.8 %collective-permute-start.7 = (bf16[64,64,128]{2,1,0:T(8,128)(2,1)}, bf16[64,64,128]{2,1,0:T(8,128)(2,1)S(1)}, u32[]{:S(2)}, u32[]{:S(2)}) collective-permute-start(bf16[64,64,128]{2,1,0:T(8,128)(2,1)} %own.1), channel_id=1, source_target_pairs={{0,1},{1,2},{2,3},{3,4},{4,5},{5,6},{6,7},{7,8},{8,9},{9,10},{10,1... | collective-permute-start | bytes 3145736 | tf_op jit(solution)/shard_map/ppermute | solution.py:282
  17.9 1.3 %collective-permute-start.8 = (bf16[64,64,128]{2,1,0:T(8,128)(2,1)}, bf16[64,64,128]{2,1,0:T(8,128)(2,1)}, u32[]{:S(2)}, u32[]{:S(2)}) collective-permute-start(bf16[64,64,128]{2,1,0:T(8,128)(2,1)} %own.1), channel_id=1, source_target_pairs={{1,0},{2,1},{3,2},{4,3},{5,4},{6,5},{7,6},{8,7},{9,8},{10,9},{11,1... | collective-permute-start | bytes 3145736 | tf_op jit(solution)/shard_map/ppermute | solution.py:287
  19.2 1.2 %collective-permute-start.2 = (f32[64,64]{1,0:T(8,128)S(1)}, f32[64,64]{1,0:T(8,128)S(1)}, u32[]{:S(2)}, u32[]{:S(2)}) collective-permute-start(f32[64,64]{1,0:T(8,128)S(1)} %get-tuple-element.8), channel_id=1, source_target_pairs={{0,1},{1,0},{2,3},{3,2},{4,5},{5,4},{6,7},{7,6},{8,9},{9,8},{10,11... | collective-permute-start | bytes 49160 | tf_op jit(solution)/shard_map/ppermute | solution.py:292
  20.4 1.4 %copy.14 = s32[8,24]{0,1:T(8,128)} copy(s32[8,24]{1,0:T(8,128)} %param.22) | data formatting | bytes 1536 | tf_op args[9]
  21.8 1.4 %copy.15 = s32[8,24]{0,1:T(8,128)} copy(s32[8,24]{1,0:T(8,128)} %param.23) | data formatting | bytes 1536 | tf_op args[10]
  23.1 2.8 %copy-done.3 = bf16[2,316,64,64]{1,3,2,0:T(8,128)(2,1)S(1)} copy-done((bf16[2,316,64,64]{1,3,2,0:T(8,128)(2,1)S(1)}, bf16[2,316,64,64]{1,3,2,0:T(8,128)(2,1)}, u32[]{:S(2)}) %copy-start.3) | copy-done | bytes 5177368
  25.9 6.3 %operator_table.1.table = bf16[2,384,64,64]{3,2,1,0:T(8,128)(2,1)S(1)} custom-call(bf16[2,64,64,316]{3,2,1,0:T(8,128)(2,1)S(1)} %bitcast.22), custom_call_target="tpu_custom_call" | custom-call | tf_op jit(solution)/shard_map/operator_table/pallas_call | solution.py:104
  32.2 4.5 %copy-done = bf16[2,384,64,64]{3,2,1,0:T(8,128)(2,1)} copy-done((bf16[2,384,64,64]{3,2,1,0:T(8,128)(2,1)}, bf16[2,384,64,64]{3,2,1,0:T(8,128)(2,1)S(1)}, u32[]{:S(2)}) %copy-start) | copy-done | bytes 6291480
  36.9 2.4 %collective-permute-start.3 = (f32[64,64]{1,0:T(8,128)S(1)}, f32[64,64]{1,0:T(8,128)S(1)}, u32[]{:S(2)}, u32[]{:S(2)}) collective-permute-start(f32[64,64]{1,0:T(8,128)S(1)} %fusion.6), channel_id=1, source_target_pairs={{0,2},{1,3},{2,0},{3,1},{4,6},{5,7},{6,4},{7,5},{8,10},{9,11},{10,... | collective-permute-start | bytes 49160 | tf_op jit(solution)/shard_map/ppermute | solution.py:292
  39.3 1.9 %collective-permute-done.3 = f32[64,64]{1,0:T(8,128)S(1)} collective-permute-done((f32[64,64]{1,0:T(8,128)S(1)}, f32[64,64]{1,0:T(8,128)S(1)}, u32[]{:S(2)}, u32[]{:S(2)}) %collective-permute-start.3) | collective-permute-done | bytes 16416 | tf_op jit(solution)/shard_map/ppermute | solution.py:292
  41.4 11.5 %collective-permute-start.4 = (f32[64,64]{1,0:T(8,128)S(1)}, f32[64,64]{1,0:T(8,128)S(1)}, u32[]{:S(2)}, u32[]{:S(2)}) collective-permute-start(f32[64,64]{1,0:T(8,128)S(1)} %fusion.4), channel_id=1, source_target_pairs={{0,4},{1,5},{2,6},{3,7},{4,0},{5,1},{6,2},{7,3},{8,12},{9,13},{10,... | collective-permute-start | bytes 49160 | tf_op jit(solution)/shard_map/ppermute | solution.py:292
  52.9 2.0 %collective-permute-done.4 = f32[64,64]{1,0:T(8,128)S(1)} collective-permute-done((f32[64,64]{1,0:T(8,128)S(1)}, f32[64,64]{1,0:T(8,128)S(1)}, u32[]{:S(2)}, u32[]{:S(2)}) %collective-permute-start.4) | collective-permute-done | bytes 16416 | tf_op jit(solution)/shard_map/ppermute | solution.py:292
  55.1 2.0 %collective-permute-start.5 = (f32[64,64]{1,0:T(8,128)S(1)}, f32[64,64]{1,0:T(8,128)S(1)}, u32[]{:S(2)}, u32[]{:S(2)}) collective-permute-start(f32[64,64]{1,0:T(8,128)S(1)} %fusion.2), channel_id=1, source_target_pairs={{0,8},{1,9},{2,10},{3,11},{4,12},{5,13},{6,14},{7,15},{8,0},{9,1},... | collective-permute-start | bytes 49160 | tf_op jit(solution)/shard_map/ppermute | solution.py:292
  57.2 1.9 %collective-permute-done.5 = f32[64,64]{1,0:T(8,128)S(1)} collective-permute-done((f32[64,64]{1,0:T(8,128)S(1)}, f32[64,64]{1,0:T(8,128)S(1)}, u32[]{:S(2)}, u32[]{:S(2)}) %collective-permute-start.5) | collective-permute-done | bytes 16416 | tf_op jit(solution)/shard_map/ppermute | solution.py:292
  59.3 3.0 %collective-permute-start.6 = (f32[64,64]{1,0:T(8,128)S(1)}, f32[64,64]{1,0:T(8,128)S(1)}, u32[]{:S(2)}, u32[]{:S(2)}) collective-permute-start(f32[64,64]{1,0:T(8,128)S(1)} %fusion), channel_id=1, source_target_pairs={{0,16},{1,17},{2,18},{3,19},{4,20},{5,21},{6,22},{7,23},{8,24},{9,... | collective-permute-start | bytes 49160 | tf_op jit(solution)/shard_map/ppermute | solution.py:292
  62.3 1.9 %collective-permute-done.6 = f32[64,64]{1,0:T(8,128)S(1)} collective-permute-done((f32[64,64]{1,0:T(8,128)S(1)}, f32[64,64]{1,0:T(8,128)S(1)}, u32[]{:S(2)}, u32[]{:S(2)}) %collective-permute-start.6) | collective-permute-done | bytes 16416 | tf_op jit(solution)/shard_map/ppermute | solution.py:292
  64.3 7.5 %near.1 = f32[64,64,128]{2,1,0:T(8,128)S(1)} custom-call(s32[2]{0:T(128)S(1)} %pad_add_fusion.base, s32[6,64]{1,0:T(8,128)S(1)} %bitcast.23, bf16[64,64,128]{2,1,0:T(8,128)(2,1)S(1)} %collective-permute-done.7.left, bf16[64,64,128]{2,1,0:T(8,128)(2,1)} %own.1, bf16[64,64,128]{2,1,0:T(8,128)(2,1)} %collective-permute-done.8.right, ...), custom_call_target="tpu_custom_call" | custom-call | tf_op jit(solution)/shard_map/near/pallas_call | solution.py:154
  71.8 1.3 %copy-done.2 = f32[64,64,128]{2,1,0:T(8,128)} copy-done((f32[64,64,128]{2,1,0:T(8,128)}, f32[64,64,128]{2,1,0:T(8,128)S(1)}, u32[]{:S(2)}) %copy-start.2) | copy-done | bytes 2097176
  73.2 31.3 %far.1 = f32[64,64,128]{2,1,0:T(8,128)} custom-call(s32[2]{0:T(128)} %copy-done.9, s32[24,64]{1,0:T(8,128)} %bitcast.26, s32[24,64]{1,0:T(8,128)} %bitcast.27, s32[24,8]{1,0:T(8,128)} %bitcast.24, s32[24,8]{1,0:T(8,128)} %bitcast.25, bf16[36,64,128]{2,1,0:T(8,128)(2,1)} %collective-permute-done.left, bf16[36,64,128]{2,1,0:T(8,128)(2,1)} %copy-done.6, ...), custom_call_target="tpu_custom_call" | custom-call | tf_op jit(solution)/shard_map/far/pallas_call | solution.py:260
  (34 shorter events, 1.7 us)
Async XLA Ops:
  0.0 1.2 %copy-start.4 = (bf16[64,64,128]{2,1,0:T(8,128)(2,1)S(1)}, bf16[64,64,128]{2,1,0:T(8,128)(2,1)}, u32[]{:S(2)}) copy-start(bf16[64,64,128]{2,1,0:T(8,128)(2,1)} %basis.3) | copy-start | bytes 3145732
  1.2 1.2 %copy-start.5 = (bf16[64,64,64]{2,1,0:T(8,128)(2,1)S(1)}, bf16[64,64,64]{2,1,0:T(8,128)(2,1)}, u32[]{:S(2)}) copy-start(bf16[64,64,64]{2,1,0:T(8,128)(2,1)} %child.3) | copy-start | bytes 1572868
  2.5 0.9 copy-start.7
  8.9 23.3 %copy-start.6 = (bf16[36,64,128]{2,1,0:T(8,128)(2,1)}, bf16[36,64,128]{2,1,0:T(8,128)(2,1)S(1)}, u32[]{:S(2)}) copy-start(bf16[36,64,128]{2,1,0:T(8,128)(2,1)S(1)} %get-tuple-element.7.own) | copy-start | bytes 1769476
  9.0 64.2 %collective-permute-start.1 = (bf16[36,64,128]{2,1,0:T(8,128)(2,1)S(1)}, bf16[36,64,128]{2,1,0:T(8,128)(2,1)}, u32[]{:S(2)}, u32[]{:S(2)}) collective-permute-start(bf16[36,64,128]{2,1,0:T(8,128)(2,1)S(1)} %get-tuple-element.7.own), channel_id=1, source_target_pairs={{1,0},{2,1},{3,2},{4,3},{5,4},{6,5},{7,6},{8,7},{9,8},{10,9},{11,1... | collective-permute-start | bytes 1769480 | tf_op jit(solution)/shard_map/ppermute | solution.py:287
  10.3 62.9 %collective-permute-start = (bf16[36,64,128]{2,1,0:T(8,128)(2,1)S(1)}, bf16[36,64,128]{2,1,0:T(8,128)(2,1)}, u32[]{:S(2)}, u32[]{:S(2)}) collective-permute-start(bf16[36,64,128]{2,1,0:T(8,128)(2,1)S(1)} %get-tuple-element.7.own), channel_id=1, source_target_pairs={{0,1},{1,2},{2,3},{3,4},{4,5},{5,6},{6,7},{7,8},{8,9},{9,10},{10,1... | collective-permute-start | bytes 1769480 | tf_op jit(solution)/shard_map/ppermute | solution.py:282
  14.1 50.1 %collective-permute-start.7 = (bf16[64,64,128]{2,1,0:T(8,128)(2,1)}, bf16[64,64,128]{2,1,0:T(8,128)(2,1)S(1)}, u32[]{:S(2)}, u32[]{:S(2)}) collective-permute-start(bf16[64,64,128]{2,1,0:T(8,128)(2,1)} %own.1), channel_id=1, source_target_pairs={{0,1},{1,2},{2,3},{3,4},{4,5},{5,6},{6,7},{7,8},{8,9},{9,10},{10,1... | collective-permute-start | bytes 3145736 | tf_op jit(solution)/shard_map/ppermute | solution.py:282
  17.9 46.4 %collective-permute-start.8 = (bf16[64,64,128]{2,1,0:T(8,128)(2,1)}, bf16[64,64,128]{2,1,0:T(8,128)(2,1)}, u32[]{:S(2)}, u32[]{:S(2)}) collective-permute-start(bf16[64,64,128]{2,1,0:T(8,128)(2,1)} %own.1), channel_id=1, source_target_pairs={{1,0},{2,1},{3,2},{4,3},{5,4},{6,5},{7,6},{8,7},{9,8},{10,9},{11,1... | collective-permute-start | bytes 3145736 | tf_op jit(solution)/shard_map/ppermute | solution.py:287
  19.2 17.6 %collective-permute-start.2 = (f32[64,64]{1,0:T(8,128)S(1)}, f32[64,64]{1,0:T(8,128)S(1)}, u32[]{:S(2)}, u32[]{:S(2)}) collective-permute-start(f32[64,64]{1,0:T(8,128)S(1)} %get-tuple-element.8), channel_id=1, source_target_pairs={{0,1},{1,0},{2,3},{3,2},{4,5},{5,4},{6,7},{7,6},{8,9},{9,8},{10,11... | collective-permute-start | bytes 49160 | tf_op jit(solution)/shard_map/ppermute | solution.py:292
  20.4 43.8 %copy-start.9 = (s32[2]{0:T(128)}, s32[2]{0:T(128)S(1)}, u32[]{:S(2)}) copy-start(s32[2]{0:T(128)S(1)} %pad_add_fusion.base) | copy-start | bytes 28
  23.1 2.8 %copy-start.3 = (bf16[2,316,64,64]{1,3,2,0:T(8,128)(2,1)S(1)}, bf16[2,316,64,64]{1,3,2,0:T(8,128)(2,1)}, u32[]{:S(2)}) copy-start(bf16[2,316,64,64]{1,3,2,0:T(8,128)(2,1)} %param.19) | copy-start | bytes 15532036
  25.9 10.8 %copy-start.10 = (f32[64,64]{1,0:T(8,128)S(1)}, f32[64,64]{1,0:T(8,128)}, u32[]{:S(2)}) copy-start(f32[64,64]{1,0:T(8,128)} %transfer.1) | copy-start | bytes 49156
  25.9 38.3 %copy-start.1 = (bf16[64,6,128,128]{3,2,1,0:T(8,128)(2,1)S(1)}, bf16[64,6,128,128]{3,2,1,0:T(8,128)(2,1)}, u32[]{:S(2)}) copy-start(bf16[64,6,128,128]{3,2,1,0:T(8,128)(2,1)} %blocks.1) | copy-start | bytes 37748740
  25.9 38.3 %copy-start.8 = (s32[64,6]{0,1:T(8,128)S(1)}, s32[64,6]{0,1:T(8,128)}, u32[]{:S(2)}) copy-start(s32[64,6]{0,1:T(8,128)} %param.15) | copy-start | bytes 4612
  32.2 4.5 %copy-start = (bf16[2,384,64,64]{3,2,1,0:T(8,128)(2,1)}, bf16[2,384,64,64]{3,2,1,0:T(8,128)(2,1)S(1)}, u32[]{:S(2)}) copy-start(bf16[2,384,64,64]{3,2,1,0:T(8,128)(2,1)S(1)} %operator_table.1.table) | copy-start | bytes 18874372
  36.9 4.2 %collective-permute-start.3 = (f32[64,64]{1,0:T(8,128)S(1)}, f32[64,64]{1,0:T(8,128)S(1)}, u32[]{:S(2)}, u32[]{:S(2)}) collective-permute-start(f32[64,64]{1,0:T(8,128)S(1)} %fusion.6), channel_id=1, source_target_pairs={{0,2},{1,3},{2,0},{3,1},{4,6},{5,7},{6,4},{7,5},{8,10},{9,11},{10,... | collective-permute-start | bytes 49160 | tf_op jit(solution)/shard_map/ppermute | solution.py:292
  41.4 13.6 %collective-permute-start.4 = (f32[64,64]{1,0:T(8,128)S(1)}, f32[64,64]{1,0:T(8,128)S(1)}, u32[]{:S(2)}, u32[]{:S(2)}) collective-permute-start(f32[64,64]{1,0:T(8,128)S(1)} %fusion.4), channel_id=1, source_target_pairs={{0,4},{1,5},{2,6},{3,7},{4,0},{5,1},{6,2},{7,3},{8,12},{9,13},{10,... | collective-permute-start | bytes 49160 | tf_op jit(solution)/shard_map/ppermute | solution.py:292
  55.1 4.0 %collective-permute-start.5 = (f32[64,64]{1,0:T(8,128)S(1)}, f32[64,64]{1,0:T(8,128)S(1)}, u32[]{:S(2)}, u32[]{:S(2)}) collective-permute-start(f32[64,64]{1,0:T(8,128)S(1)} %fusion.2), channel_id=1, source_target_pairs={{0,8},{1,9},{2,10},{3,11},{4,12},{5,13},{6,14},{7,15},{8,0},{9,1},... | collective-permute-start | bytes 49160 | tf_op jit(solution)/shard_map/ppermute | solution.py:292
  59.3 4.9 %collective-permute-start.6 = (f32[64,64]{1,0:T(8,128)S(1)}, f32[64,64]{1,0:T(8,128)S(1)}, u32[]{:S(2)}, u32[]{:S(2)}) collective-permute-start(f32[64,64]{1,0:T(8,128)S(1)} %fusion), channel_id=1, source_target_pairs={{0,16},{1,17},{2,18},{3,19},{4,20},{5,21},{6,22},{7,23},{8,24},{9,... | collective-permute-start | bytes 49160 | tf_op jit(solution)/shard_map/ppermute | solution.py:292
  64.2 7.6 %copy-start.11 = (f32[5,64,64]{2,1,0:T(8,128)}, f32[5,64,64]{2,1,0:T(8,128)S(1)}, u32[]{:S(2)}) copy-start(f32[5,64,64]{2,1,0:T(8,128)S(1)} %bitcast_dynamic-update-slice_fusion.siblings) | copy-start | bytes 245764
  71.8 1.3 %copy-start.2 = (f32[64,64,128]{2,1,0:T(8,128)}, f32[64,64,128]{2,1,0:T(8,128)S(1)}, u32[]{:S(2)}) copy-start(f32[64,64,128]{2,1,0:T(8,128)S(1)} %near.1) | copy-start | bytes 6291460

commit v2 on v1

--- a/solution.py
+++ b/solution.py
@@ -29,18 +29,21 @@
     step = pl.program_id(0)
     leaf_pairs = 8 * pl.num_programs(0)
     rank = basis.shape[1]
-    parents = []
-    for p in range(2):
-        acc = None
-        for i in range(4):
-            c = 8 * p + 2 * i
-            pair = jnp.concatenate(
-                [mm(charges[c], basis[c], NT), mm(charges[c + 1], basis[c + 1], NT)], axis=1
-            ).astype(bf16)
-            send[step * 8 + p * 4 + i] = pair
-            term = mm(pair, child[c : c + 2].reshape(2 * rank, rank))
-            acc = term if acc is None else acc + term
-        parents.append(acc)
+    pairs = [
+        jnp.concatenate(
+            [mm(charges[c], basis[c], NT), mm(charges[c + 1], basis[c + 1], NT)], axis=1
+        ).astype(bf16)
+        for c in range(0, 16, 2)
+    ]
+    parents = [
+        mm(
+            jnp.concatenate(pairs[4 * p : 4 * p + 4], axis=1),
+            child[8 * p : 8 * p + 8].reshape(8 * rank, rank),
+        )
+        for p in range(2)
+    ]
+    for i, pair in enumerate(pairs):
+        send[step * 8 + i] = pair
     both = jnp.concatenate(parents, axis=1).astype(bf16)
     send[leaf_pairs + step] = both
     part = mm(both, parent[...].reshape(2 * rank, rank))
@@ -118,7 +121,7 @@
 NEAR_LEAVES = 8
 
 
-def near_kernel(base, near, left, own, right, blocks, out, sources, sems):
+def near_kernel(base, near, left, own, right, blocks, far, out, sources, sems):
     step = pl.program_id(0)
     leaves = own.shape[0]
 
@@ -134,20 +137,22 @@
             copy.wait()
 
     count = blocks.shape[1]
+    results = []
     for i in range(NEAR_LEAVES):
         row = step * NEAR_LEAVES + i
-        acc = None
+        acc = far[i]
         for n in range(0, count, 2):
             lhs = jnp.concatenate(
                 [sources[near[n, row] - base[0]], sources[near[n + 1, row] - base[0]]], axis=1
             )
             rhs = jnp.concatenate([blocks[i, n], blocks[i, n + 1]], axis=1)
-            term = mm(lhs, rhs, NT)
-            acc = term if acc is None else acc + term
+            acc = acc + mm(lhs, rhs, NT)
+        results.append(acc)
+    for i, acc in enumerate(results):
         out[i] = acc
 
 
-def near_call(base, near_rows, left, own, right, blocks):
+def near_call(base, near_rows, left, own, right, blocks, far):
     leaves, columns, points = own.shape
     count = blocks.shape[1]
     hbm = pl.BlockSpec(memory_space=pl.ANY)
@@ -161,6 +166,7 @@
                 hbm,
                 hbm,
                 pl.BlockSpec((NEAR_LEAVES, count, points, points), lambda i, *_: (i, 0, 0, 0)),
+                pl.BlockSpec((NEAR_LEAVES, columns, points), lambda i, *_: (i, 0, 0)),
             ],
             out_specs=pl.BlockSpec((NEAR_LEAVES, columns, points), lambda i, *_: (i, 0, 0)),
             scratch_shapes=[
@@ -171,7 +177,7 @@
         out_shape=jax.ShapeDtypeStruct((leaves, columns, points), f32),
         compiler_params=params(32),
         name="near",
-    )(base, near_rows, left, own, right, blocks)
+    )(base, near_rows, left, own, right, blocks, far)
 
 
 def doubled(pair, low):
@@ -180,48 +186,46 @@
     return jnp.where(low, pair, swapped), jnp.where(low, swapped, pair)
 
 
-def translated(acc, sources, table, level, lists, ops, base, row, low):
+def translated(acc, sources, table, lists, ops, base, row, low):
     count = lists.shape[0]
     for e in range(0, count, 4):
         picked = [sources[lists[e + i, row] - base] for i in range(4)]
         lhs = jnp.concatenate(
             [jnp.where(low, picked[0], picked[1]), jnp.where(low, picked[2], picked[3])], axis=1
         )
-        rhs = jnp.concatenate([table[level, ops[e + i, row]] for i in range(4)], axis=0)
+        rhs = jnp.concatenate([table[ops[e + i, row]] for i in range(4)], axis=0)
         acc = acc + mm(lhs, rhs)
     return acc
 
 
 def far_kernel(
     base, list0, op0, list1, op1,
-    left, own, right, table, siblings, transfer, couple, parent, child, basis, near,
-    out, leaf_sources, parent_sources, parent_locals,
+    left, own, right, table, siblings, transfer, couple, parent, child, basis,
+    out, leaf_sources, parent_sources, parent_locals, leaf_table, parent_table, sems,
 ):
     step = pl.program_id(0)
     parents = pl.num_programs(0)
-    leaves = 8 * parents
+    leaves = leaf_sources.shape[0] // 3
     columns = own.shape[1]
     rank = own.shape[2] // 2
     low = lax.broadcasted_iota(jnp.int32, (columns, 2 * rank), 1) < rank
 
     @pl.when(step == 0)
     def _():
+        ops = leaf_table.shape[0]
+        parent_copy = pltpu.make_async_copy(table.at[1, pl.ds(0, ops)], parent_table, sems.at[0])
+        leaf_copy = pltpu.make_async_copy(table.at[0, pl.ds(0, ops)], leaf_table, sems.at[1])
+        parent_copy.start()
+        leaf_copy.start()
         for i, ref in enumerate((left, own, right)):
-            def leaf_pair(n, _, i=i, ref=ref):
+            for n in range(leaves // 2):
                 a, b = doubled(ref[n], low)
                 leaf_sources[i * leaves + 2 * n] = a
                 leaf_sources[i * leaves + 2 * n + 1] = b
-                return 0
-
-            lax.fori_loop(0, leaves // 2, leaf_pair, 0)
-
-            def parent_pair(n, _, i=i, ref=ref):
+            for n in range(leaves // 16):
                 a, b = doubled(ref[leaves // 2 + n], low)
-                parent_sources[i * parents + 2 * n] = a
-                parent_sources[i * parents + 2 * n + 1] = b
-                return 0
-
-            lax.fori_loop(0, parents // 2, parent_pair, 0)
+                parent_sources[i * leaves // 8 + 2 * n] = a
+                parent_sources[i * leaves // 8 + 2 * n + 1] = b
         field = None
         for j in reversed(range(siblings.shape[0])):
             term = mm(siblings[j], couple[...], precision=highest)
@@ -229,52 +233,59 @@
                 term = term + mm(field, transfer[...], NT, precision=highest)
             field = term
         box_local = field.astype(bf16)
-
-        def one_parent(q, _):
-            acc = mm(box_local, parent[q], NT)
-            acc = translated(acc, parent_sources, table, 1, list1, op1, base[1], q, low)
+        parent_copy.wait()
+        accs = [
+            translated(mm(box_local, parent[q], NT), parent_sources, parent_table, list1, op1, base[1], q, low)
+            for q in range(leaves // 8)
+        ]
+        for q, acc in enumerate(accs):
             parent_locals[q] = acc.astype(bf16)
-            return 0
-
-        lax.fori_loop(0, parents, one_parent, 0)
+        leaf_copy.wait()
 
     parent_local = parent_locals[step]
-    for c in range(8):
-        row = step * 8 + c
-        acc = mm(parent_local, child[c], NT)
-        acc = translated(acc, leaf_sources, table, 0, list0, op0, base[0], row, low)
-        out[c] = near[c] + mm(acc.astype(bf16), basis[c])
-
-
-def far_call(base, list0, op0, list1, op1, left, own, right, table, siblings, transfer, couple, parent, child, basis, near):
+    accs = [
+        translated(mm(parent_local, child[c], NT), leaf_sources, leaf_table, list0, op0, base[0], step * 8 + c, low)
+        for c in range(8)
+    ]
+    results = [mm(acc.astype(bf16), basis[c]) for c, acc in enumerate(accs)]
+    for c, acc in enumerate(results):
+        out[c] = acc
+
+
+def far_call(base, list0, op0, list1, op1, left, own, right, table, count, siblings, transfer, couple, parent, child, basis):
     leaves, rank, points = basis.shape
     parents = parent.shape[0]
-    columns = near.shape[1]
+    columns = own.shape[1]
 
     def whole(x):
         return pl.BlockSpec(x.shape, lambda i, *_: (0,) * x.ndim)
 
-    def rows(x):
-        return pl.BlockSpec((8,) + x.shape[1:], lambda i, *_: (i,) + (0,) * (x.ndim - 1))
+    def rows(shape):
+        return pl.BlockSpec((8,) + shape[1:], lambda i, *_: (i,) + (0,) * (len(shape) - 1))
 
     return pl.pallas_call(
         far_kernel,
         grid_spec=pltpu.PrefetchScalarGridSpec(
             num_scalar_prefetch=5,
             grid=(parents,),
-            in_specs=[whole(x) for x in (left, own, right, table, siblings, transfer, couple, parent)]
-            + [rows(x) for x in (child, basis, near)],
-            out_specs=rows(near),
+            in_specs=[whole(x) for x in (left, own, right)]
+            + [pl.BlockSpec(memory_space=pl.ANY)]
+            + [whole(x) for x in (siblings, transfer, couple, parent)]
+            + [rows(x.shape) for x in (child, basis)],
+            out_specs=rows((leaves, columns, points)),
             scratch_shapes=[
                 pltpu.VMEM((3 * leaves, columns, 2 * rank), bf16),
                 pltpu.VMEM((3 * parents, columns, 2 * rank), bf16),
                 pltpu.VMEM((parents, columns, rank), bf16),
+                pltpu.VMEM((count, rank, rank), bf16),
+                pltpu.VMEM((count, rank, rank), bf16),
+                pltpu.SemaphoreType.DMA((2,)),
             ],
         ),
         out_shape=jax.ShapeDtypeStruct((leaves, columns, points), f32),
-        compiler_params=params(56),
+        compiler_params=params(40),
         name="far",
-    )(base, list0, op0, list1, op1, left, own, right, table, siblings, transfer, couple, parent, child, basis, near)
+    )(base, list0, op0, list1, op1, left, own, right, table, siblings, transfer, couple, parent, child, basis)
 
 
 def to_right(block):
@@ -314,12 +325,12 @@
         if level_bit + 1 < height:
             current = mm(current + partner, top_transfer, precision=highest)
     table = table_call(m2l_ops)
-    near = near_call(base, near_list.T, charges_left, charges, charges_right, near_blocks)
-    return far_call(
+    far = far_call(
         base, far_list0.T, far_op0.T, far_list1.T, far_op1.T,
-        moments_left, send, moments_right, table, jnp.stack(siblings),
-        top_transfer, top_couple, parent_transfer, child_transfer, leaf_basis, near,
+        moments_left, send, moments_right, table, m2l_ops.shape[1], jnp.stack(siblings),
+        top_transfer, top_couple, parent_transfer, child_transfer, leaf_basis,
     )
+    return near_call(base, near_list.T, charges_left, charges, charges_right, near_blocks, far)
 
 
 def solution(mesh):

time: 105 us -> 94 us (0.90)
  Pallas kernels: 50.6 us -> 34.7 us
  starting transfers between devices: 30.4 us -> 35 us
    pallas_call x1, Pallas kernels: 31.3 us -> 15.2 us  [far_call(): pl.pallas_call(far_kernel, grid_spec=pltpu.PrefetchScalarGridSpec(num_sca...]
    ppermute x5, starting transfers between devices: 20.2 us -> 24.8 us  [from_partner(): lax.ppermute(block, AXES, [(i, i ^ 1 << apart) for i in range(count)])]
    unnamed x30 -> x38, local copies, waits for them, and re-layouts: 14.7 us -> 15.4 us
  transfers between devices with their start and end apart: 9 -> 9, of which waited for: 4 -> 4; matrix products, arithmetic and copies ran while one was open for 3% -> 1% of each run, Pallas kernels for 13% -> 23%
where the time goes in v2:
time: 94 us; the launch traced here: 93.6 us
  starting transfers between devices  35 us (37%)
  Pallas kernels  34.7 us (37%)
  local copies, waits for them, and re-layouts  15.4 us (16%)
  waiting for transfers between devices  7.57 us (8%)
    ppermute x5, starting transfers between devices, from_partner(): lax.ppermute(block, AXES, [(i, i ^ 1 << apart) for i in range(count)])  24.8 us
    unnamed x38, local copies, waits for them, and re-layouts  15.4 us
    pallas_call x1, Pallas kernels, far_call(): pl.pallas_call(far_kernel, grid_spec=pltpu.PrefetchScalarGridSpec(num_sca...  15.2 us
    pallas_call x1, Pallas kernels, near_call(): pl.pallas_call(near_kernel, grid_spec=pltpu.PrefetchScalarGridSpec(num_sc...  8.43 us
    ppermute x2, starting transfers between devices, to_right(): return lax.ppermute(block, AXES, [(i, i + 1) for i in range(count - 1)])  7.6 us
    ppermute x5, waiting for transfers between devices, from_partner(): lax.ppermute(block, AXES, [(i, i ^ 1 << apart) for i in range(count)])  7.56 us
    pallas_call x1, Pallas kernels, table_call(): pl.pallas_call(table_kernel, grid=(levels, blocks), in_specs=[pl.BlockSpe...  6.3 us
    pallas_call x1, Pallas kernels, moments_call(): pl.pallas_call(moments_kernel, grid=(steps,), in_specs=[pl.BlockSpec((16,...  4.7 us
  transfers between devices with their start and end apart: 9, of which 4 were waited for; matrix products, arithmetic and copies ran while one was open for 1% of the time, Pallas kernels for 23%

profile of v2, /device:TPU:0, one launch (start us, length us, event | category | flops | bytes accessed | tf_op | source)
XLA Modules:
  0.0 93.6 jit_solution(10789852209272514921)
XLA Ops:
  0.0 1.2 %copy-done.3 = bf16[64,64,128]{2,1,0:T(8,128)(2,1)S(1)} copy-done((bf16[64,64,128]{2,1,0:T(8,128)(2,1)S(1)}, bf16[64,64,128]{2,1,0:T(8,128)(2,1)}, u32[]{:S(2)}) %copy-start.3) | copy-done | bytes 1048600
  1.2 1.2 %copy-done.5 = bf16[64,64,64]{2,1,0:T(8,128)(2,1)S(1)} copy-done((bf16[64,64,64]{2,1,0:T(8,128)(2,1)S(1)}, bf16[64,64,64]{2,1,0:T(8,128)(2,1)}, u32[]{:S(2)}) %copy-start.5) | copy-done | bytes 524312
  2.5 0.9 copy-done.8
  3.4 4.7 %moments.1 = (bf16[36,64,128]{2,1,0:T(8,128)(2,1)}, f32[64,64]{1,0:T(8,128)S(1)}) custom-call(bf16[64,64,128]{2,1,0:T(8,128)(2,1)} %own.1, bf16[64,64,128]{2,1,0:T(8,128)(2,1)S(1)} %copy-done.3, bf16[64,64,64]{2,1,0:T(8,128)(2,1)S(1)} %copy-done.5, bf16[8,64,64]{2,1,0:T(8,128)(2,1)S(1)} %copy-done.8), custom_call_target="tpu_custom_call" | custom-call | tf_op jit(solution)/shard_map/moments/pallas_call | solution.py:66
  8.1 3.2 %collective-permute-start.2 = (bf16[36,64,128]{2,1,0:T(8,128)(2,1)}, bf16[36,64,128]{2,1,0:T(8,128)(2,1)}, u32[]{:S(2)}, u32[]{:S(2)}) collective-permute-start(bf16[36,64,128]{2,1,0:T(8,128)(2,1)} %get-tuple-element.7.own), channel_id=1, source_target_pairs={{0,1},{1,2},{2,3},{3,4},{4,5},{5,6},{6,7},{7,8},{8,9},{9,10},{10,1... | collective-permute-start | bytes 1769480 | tf_op jit(solution)/shard_map/ppermute | solution.py:293
  11.2 1.3 %collective-permute-start.3 = (bf16[36,64,128]{2,1,0:T(8,128)(2,1)}, bf16[36,64,128]{2,1,0:T(8,128)(2,1)}, u32[]{:S(2)}, u32[]{:S(2)}) collective-permute-start(bf16[36,64,128]{2,1,0:T(8,128)(2,1)} %get-tuple-element.7.own), channel_id=1, source_target_pairs={{1,0},{2,1},{3,2},{4,3},{5,4},{6,5},{7,6},{8,7},{9,8},{10,9},{11,1... | collective-permute-start | bytes 1769480 | tf_op jit(solution)/shard_map/ppermute | solution.py:298
  12.5 4.4 %collective-permute-start = (bf16[64,64,128]{2,1,0:T(8,128)(2,1)}, bf16[64,64,128]{2,1,0:T(8,128)(2,1)S(1)}, u32[]{:S(2)}, u32[]{:S(2)}) collective-permute-start(bf16[64,64,128]{2,1,0:T(8,128)(2,1)} %own.1), channel_id=1, source_target_pairs={{0,1},{1,2},{2,3},{3,4},{4,5},{5,6},{6,7},{7,8},{8,9},{9,10},{10,1... | collective-permute-start | bytes 3145736 | tf_op jit(solution)/shard_map/ppermute | solution.py:293
  17.0 1.3 %collective-permute-start.1 = (bf16[64,64,128]{2,1,0:T(8,128)(2,1)}, bf16[64,64,128]{2,1,0:T(8,128)(2,1)}, u32[]{:S(2)}, u32[]{:S(2)}) collective-permute-start(bf16[64,64,128]{2,1,0:T(8,128)(2,1)} %own.1), channel_id=1, source_target_pairs={{1,0},{2,1},{3,2},{4,3},{5,4},{6,5},{7,6},{8,7},{9,8},{10,9},{11,1... | collective-permute-start | bytes 3145736 | tf_op jit(solution)/shard_map/ppermute | solution.py:298
  18.3 2.4 %collective-permute-start.4 = (f32[64,64]{1,0:T(8,128)S(1)}, f32[64,64]{1,0:T(8,128)S(1)}, u32[]{:S(2)}, u32[]{:S(2)}) collective-permute-start(f32[64,64]{1,0:T(8,128)S(1)} %get-tuple-element.8), channel_id=1, source_target_pairs={{0,1},{1,0},{2,3},{3,2},{4,5},{5,4},{6,7},{7,6},{8,9},{9,8},{10,11... | collective-permute-start | bytes 49160 | tf_op jit(solution)/shard_map/ppermute | solution.py:303
  20.7 2.8 %copy-done.2 = bf16[2,316,64,64]{1,3,2,0:T(8,128)(2,1)S(1)} copy-done((bf16[2,316,64,64]{1,3,2,0:T(8,128)(2,1)S(1)}, bf16[2,316,64,64]{1,3,2,0:T(8,128)(2,1)}, u32[]{:S(2)}) %copy-start.2) | copy-done | bytes 5177368
  23.6 6.3 %operator_table.1.table = bf16[2,384,64,64]{3,2,1,0:T(8,128)(2,1)S(1)} custom-call(bf16[2,64,64,316]{3,2,1,0:T(8,128)(2,1)S(1)} %bitcast.22), custom_call_target="tpu_custom_call" | custom-call | tf_op jit(solution)/shard_map/operator_table/pallas_call | solution.py:107
  29.9 4.5 %copy-done = bf16[2,384,64,64]{3,2,1,0:T(8,128)(2,1)} copy-done((bf16[2,384,64,64]{3,2,1,0:T(8,128)(2,1)}, bf16[2,384,64,64]{3,2,1,0:T(8,128)(2,1)S(1)}, u32[]{:S(2)}) %copy-start) | copy-done | bytes 6291480
  34.5 0.2 fusion.6
  34.7 2.4 %collective-permute-start.5 = (f32[64,64]{1,0:T(8,128)S(1)}, f32[64,64]{1,0:T(8,128)S(1)}, u32[]{:S(2)}, u32[]{:S(2)}) collective-permute-start(f32[64,64]{1,0:T(8,128)S(1)} %fusion.6), channel_id=1, source_target_pairs={{0,2},{1,3},{2,0},{3,1},{4,6},{5,7},{6,4},{7,5},{8,10},{9,11},{10,... | collective-permute-start | bytes 49160 | tf_op jit(solution)/shard_map/ppermute | solution.py:303
  37.1 1.9 %collective-permute-done.5 = f32[64,64]{1,0:T(8,128)S(1)} collective-permute-done((f32[64,64]{1,0:T(8,128)S(1)}, f32[64,64]{1,0:T(8,128)S(1)}, u32[]{:S(2)}, u32[]{:S(2)}) %collective-permute-start.5) | collective-permute-done | bytes 16416 | tf_op jit(solution)/shard_map/ppermute | solution.py:303
  39.2 13.9 %collective-permute-start.6 = (f32[64,64]{1,0:T(8,128)S(1)}, f32[64,64]{1,0:T(8,128)S(1)}, u32[]{:S(2)}, u32[]{:S(2)}) collective-permute-start(f32[64,64]{1,0:T(8,128)S(1)} %fusion.4), channel_id=1, source_target_pairs={{0,4},{1,5},{2,6},{3,7},{4,0},{5,1},{6,2},{7,3},{8,12},{9,13},{10,... | collective-permute-start | bytes 49160 | tf_op jit(solution)/shard_map/ppermute | solution.py:303
  53.0 1.9 %collective-permute-done.6 = f32[64,64]{1,0:T(8,128)S(1)} collective-permute-done((f32[64,64]{1,0:T(8,128)S(1)}, f32[64,64]{1,0:T(8,128)S(1)}, u32[]{:S(2)}, u32[]{:S(2)}) %collective-permute-start.6) | collective-permute-done | bytes 16416 | tf_op jit(solution)/shard_map/ppermute | solution.py:303
  55.1 3.1 %collective-permute-start.7 = (f32[64,64]{1,0:T(8,128)S(1)}, f32[64,64]{1,0:T(8,128)S(1)}, u32[]{:S(2)}, u32[]{:S(2)}) collective-permute-start(f32[64,64]{1,0:T(8,128)S(1)} %fusion.2), channel_id=1, source_target_pairs={{0,8},{1,9},{2,10},{3,11},{4,12},{5,13},{6,14},{7,15},{8,0},{9,1},... | collective-permute-start | bytes 49160 | tf_op jit(solution)/shard_map/ppermute | solution.py:303
  58.2 1.9 %collective-permute-done.7 = f32[64,64]{1,0:T(8,128)S(1)} collective-permute-done((f32[64,64]{1,0:T(8,128)S(1)}, f32[64,64]{1,0:T(8,128)S(1)}, u32[]{:S(2)}, u32[]{:S(2)}) %collective-permute-start.7) | collective-permute-done | bytes 16416 | tf_op jit(solution)/shard_map/ppermute | solution.py:303
  60.2 3.1 %collective-permute-start.8 = (f32[64,64]{1,0:T(8,128)S(1)}, f32[64,64]{1,0:T(8,128)S(1)}, u32[]{:S(2)}, u32[]{:S(2)}) collective-permute-start(f32[64,64]{1,0:T(8,128)S(1)} %fusion), channel_id=1, source_target_pairs={{0,16},{1,17},{2,18},{3,19},{4,20},{5,21},{6,22},{7,23},{8,24},{9,... | collective-permute-start | bytes 49160 | tf_op jit(solution)/shard_map/ppermute | solution.py:303
  63.3 1.9 %collective-permute-done.8 = f32[64,64]{1,0:T(8,128)S(1)} collective-permute-done((f32[64,64]{1,0:T(8,128)S(1)}, f32[64,64]{1,0:T(8,128)S(1)}, u32[]{:S(2)}, u32[]{:S(2)}) %collective-permute-start.8) | collective-permute-done | bytes 16416 | tf_op jit(solution)/shard_map/ppermute | solution.py:303
  65.3 15.2 %far.1 = f32[64,64,128]{2,1,0:T(8,128)S(1)} custom-call(s32[2]{0:T(128)S(1)} %pad_add_fusion.base, s32[24,64]{1,0:T(8,128)S(1)} %bitcast.25, s32[24,64]{1,0:T(8,128)S(1)} %bitcast.26, s32[24,8]{1,0:T(8,128)S(1)} %bitcast.23, s32[24,8]{1,0:T(8,128)S(1)} %bitcast.24, bf16[36,64,128]{2,1,0:T(8,128)(2,1)} %collective-permute-done.2.left, ...), custom_call_target="tpu_custom_call" | custom-call | tf_op jit(solution)/shard_map/far/pallas_call | solution.py:266
  80.6 4.6 %copy-done.1 = bf16[64,6,128,128]{3,2,1,0:T(8,128)(2,1)S(1)} copy-done((bf16[64,6,128,128]{3,2,1,0:T(8,128)(2,1)S(1)}, bf16[64,6,128,128]{3,2,1,0:T(8,128)(2,1)}, u32[]{:S(2)}) %copy-start.1) | copy-done | bytes 12582936
  85.2 8.4 %near.1 = f32[64,64,128]{2,1,0:T(8,128)} custom-call(s32[2]{0:T(128)S(1)} %pad_add_fusion.base, s32[6,64]{1,0:T(8,128)S(1)} %bitcast.27, bf16[64,64,128]{2,1,0:T(8,128)(2,1)S(1)} %collective-permute-done.left, bf16[64,64,128]{2,1,0:T(8,128)(2,1)} %own.1, bf16[64,64,128]{2,1,0:T(8,128)(2,1)} %collective-permute-done.1.right, ...), custom_call_target="tpu_custom_call" | custom-call | tf_op jit(solution)/shard_map/near/pallas_call | solution.py:159
  (42 shorter events, 0.8 us)
Async XLA Ops:
  0.0 1.2 %copy-start.3 = (bf16[64,64,128]{2,1,0:T(8,128)(2,1)S(1)}, bf16[64,64,128]{2,1,0:T(8,128)(2,1)}, u32[]{:S(2)}) copy-start(bf16[64,64,128]{2,1,0:T(8,128)(2,1)} %basis.3) | copy-start | bytes 3145732
  1.2 1.2 %copy-start.5 = (bf16[64,64,64]{2,1,0:T(8,128)(2,1)S(1)}, bf16[64,64,64]{2,1,0:T(8,128)(2,1)}, u32[]{:S(2)}) copy-start(bf16[64,64,64]{2,1,0:T(8,128)(2,1)} %child.3) | copy-start | bytes 1572868
  8.1 57.2 %collective-permute-start.2 = (bf16[36,64,128]{2,1,0:T(8,128)(2,1)}, bf16[36,64,128]{2,1,0:T(8,128)(2,1)}, u32[]{:S(2)}, u32[]{:S(2)}) collective-permute-start(bf16[36,64,128]{2,1,0:T(8,128)(2,1)} %get-tuple-element.7.own), channel_id=1, source_target_pairs={{0,1},{1,2},{2,3},{3,4},{4,5},{5,6},{6,7},{7,8},{8,9},{9,10},{10,1... | collective-permute-start | bytes 1769480 | tf_op jit(solution)/shard_map/ppermute | solution.py:293
  11.2 54.0 %collective-permute-start.3 = (bf16[36,64,128]{2,1,0:T(8,128)(2,1)}, bf16[36,64,128]{2,1,0:T(8,128)(2,1)}, u32[]{:S(2)}, u32[]{:S(2)}) collective-permute-start(bf16[36,64,128]{2,1,0:T(8,128)(2,1)} %get-tuple-element.7.own), channel_id=1, source_target_pairs={{1,0},{2,1},{3,2},{4,3},{5,4},{6,5},{7,6},{8,7},{9,8},{10,9},{11,1... | collective-permute-start | bytes 1769480 | tf_op jit(solution)/shard_map/ppermute | solution.py:298
  12.5 68.0 %collective-permute-start = (bf16[64,64,128]{2,1,0:T(8,128)(2,1)}, bf16[64,64,128]{2,1,0:T(8,128)(2,1)S(1)}, u32[]{:S(2)}, u32[]{:S(2)}) collective-permute-start(bf16[64,64,128]{2,1,0:T(8,128)(2,1)} %own.1), channel_id=1, source_target_pairs={{0,1},{1,2},{2,3},{3,4},{4,5},{5,6},{6,7},{7,8},{8,9},{9,10},{10,1... | collective-permute-start | bytes 3145736 | tf_op jit(solution)/shard_map/ppermute | solution.py:293
  17.0 63.6 %collective-permute-start.1 = (bf16[64,64,128]{2,1,0:T(8,128)(2,1)}, bf16[64,64,128]{2,1,0:T(8,128)(2,1)}, u32[]{:S(2)}, u32[]{:S(2)}) collective-permute-start(bf16[64,64,128]{2,1,0:T(8,128)(2,1)} %own.1), channel_id=1, source_target_pairs={{1,0},{2,1},{3,2},{4,3},{5,4},{6,5},{7,6},{8,7},{9,8},{10,9},{11,1... | collective-permute-start | bytes 3145736 | tf_op jit(solution)/shard_map/ppermute | solution.py:298
  18.3 16.3 %collective-permute-start.4 = (f32[64,64]{1,0:T(8,128)S(1)}, f32[64,64]{1,0:T(8,128)S(1)}, u32[]{:S(2)}, u32[]{:S(2)}) collective-permute-start(f32[64,64]{1,0:T(8,128)S(1)} %get-tuple-element.8), channel_id=1, source_target_pairs={{0,1},{1,0},{2,3},{3,2},{4,5},{5,4},{6,7},{7,6},{8,9},{9,8},{10,11... | collective-permute-start | bytes 49160 | tf_op jit(solution)/shard_map/ppermute | solution.py:303
  20.7 2.8 %copy-start.2 = (bf16[2,316,64,64]{1,3,2,0:T(8,128)(2,1)S(1)}, bf16[2,316,64,64]{1,3,2,0:T(8,128)(2,1)}, u32[]{:S(2)}) copy-start(bf16[2,316,64,64]{1,3,2,0:T(8,128)(2,1)} %param.19) | copy-start | bytes 15532036
  23.5 10.9 %copy-start.14 = (s32[8,24]{1,0:T(8,128)S(1)}, s32[8,24]{1,0:T(8,128)}, u32[]{:S(2)}) copy-start(s32[8,24]{1,0:T(8,128)} %param.22) | copy-start | bytes 2308
  23.5 11.0 %copy-start.15 = (s32[8,24]{1,0:T(8,128)S(1)}, s32[8,24]{1,0:T(8,128)}, u32[]{:S(2)}) copy-start(s32[8,24]{1,0:T(8,128)} %param.23) | copy-start | bytes 2308
  23.5 11.0 %copy-start.7 = (f32[64,64]{1,0:T(8,128)S(1)}, f32[64,64]{1,0:T(8,128)}, u32[]{:S(2)}) copy-start(f32[64,64]{1,0:T(8,128)} %transfer.1) | copy-start | bytes 49156
  23.5 41.7 %copy-start.4 = (bf16[64,64,128]{2,1,0:T(8,128)(2,1)S(1)}, bf16[64,64,128]{2,1,0:T(8,128)(2,1)}, u32[]{:S(2)}) copy-start(bf16[64,64,128]{2,1,0:T(8,128)(2,1)} %basis.3) | copy-start | bytes 3145732
  23.5 41.7 %copy-start.6 = (bf16[64,64,64]{2,1,0:T(8,128)(2,1)S(1)}, bf16[64,64,64]{2,1,0:T(8,128)(2,1)}, u32[]{:S(2)}) copy-start(bf16[64,64,64]{2,1,0:T(8,128)(2,1)} %child.3) | copy-start | bytes 1572868
  23.5 41.7 %copy-start.9 = (bf16[8,64,64]{2,1,0:T(8,128)(2,1)S(1)}, bf16[8,64,64]{2,1,0:T(8,128)(2,1)}, u32[]{:S(2)}) copy-start(bf16[8,64,64]{2,1,0:T(8,128)(2,1)} %parent.3) | copy-start | bytes 196612
  23.5 41.7 %copy-start.10 = (f32[64,64]{1,0:T(8,128)S(1)}, f32[64,64]{1,0:T(8,128)}, u32[]{:S(2)}) copy-start(f32[64,64]{1,0:T(8,128)} %couple.1) | copy-start | bytes 49156
  23.5 41.7 %copy-start.11 = (s32[64,24]{0,1:T(8,128)S(1)}, s32[64,24]{0,1:T(8,128)}, u32[]{:S(2)}) copy-start(s32[64,24]{0,1:T(8,128)} %param.20) | copy-start | bytes 18436
  23.5 41.7 %copy-start.12 = (s32[64,24]{0,1:T(8,128)S(1)}, s32[64,24]{0,1:T(8,128)}, u32[]{:S(2)}) copy-start(s32[64,24]{0,1:T(8,128)} %param.21) | copy-start | bytes 18436
  29.9 4.5 %copy-start = (bf16[2,384,64,64]{3,2,1,0:T(8,128)(2,1)}, bf16[2,384,64,64]{3,2,1,0:T(8,128)(2,1)S(1)}, u32[]{:S(2)}) copy-start(bf16[2,384,64,64]{3,2,1,0:T(8,128)(2,1)S(1)} %operator_table.1.table) | copy-start | bytes 18874372
  34.7 4.3 %collective-permute-start.5 = (f32[64,64]{1,0:T(8,128)S(1)}, f32[64,64]{1,0:T(8,128)S(1)}, u32[]{:S(2)}, u32[]{:S(2)}) collective-permute-start(f32[64,64]{1,0:T(8,128)S(1)} %fusion.6), channel_id=1, source_target_pairs={{0,2},{1,3},{2,0},{3,1},{4,6},{5,7},{6,4},{7,5},{8,10},{9,11},{10,... | collective-permute-start | bytes 49160 | tf_op jit(solution)/shard_map/ppermute | solution.py:303
  39.2 15.7 %collective-permute-start.6 = (f32[64,64]{1,0:T(8,128)S(1)}, f32[64,64]{1,0:T(8,128)S(1)}, u32[]{:S(2)}, u32[]{:S(2)}) collective-permute-start(f32[64,64]{1,0:T(8,128)S(1)} %fusion.4), channel_id=1, source_target_pairs={{0,4},{1,5},{2,6},{3,7},{4,0},{5,1},{6,2},{7,3},{8,12},{9,13},{10,... | collective-permute-start | bytes 49160 | tf_op jit(solution)/shard_map/ppermute | solution.py:303
  55.1 5.0 %collective-permute-start.7 = (f32[64,64]{1,0:T(8,128)S(1)}, f32[64,64]{1,0:T(8,128)S(1)}, u32[]{:S(2)}, u32[]{:S(2)}) collective-permute-start(f32[64,64]{1,0:T(8,128)S(1)} %fusion.2), channel_id=1, source_target_pairs={{0,8},{1,9},{2,10},{3,11},{4,12},{5,13},{6,14},{7,15},{8,0},{9,1},... | collective-permute-start | bytes 49160 | tf_op jit(solution)/shard_map/ppermute | solution.py:303
  60.2 5.0 %collective-permute-start.8 = (f32[64,64]{1,0:T(8,128)S(1)}, f32[64,64]{1,0:T(8,128)S(1)}, u32[]{:S(2)}, u32[]{:S(2)}) collective-permute-start(f32[64,64]{1,0:T(8,128)S(1)} %fusion), channel_id=1, source_target_pairs={{0,16},{1,17},{2,18},{3,19},{4,20},{5,21},{6,22},{7,23},{8,24},{9,... | collective-permute-start | bytes 49160 | tf_op jit(solution)/shard_map/ppermute | solution.py:303
  65.3 15.3 %copy-start.13 = (s32[64,6]{0,1:T(8,128)S(1)}, s32[64,6]{0,1:T(8,128)}, u32[]{:S(2)}) copy-start(s32[64,6]{0,1:T(8,128)} %param.15) | copy-start | bytes 4612
  80.6 4.6 %copy-start.1 = (bf16[64,6,128,128]{3,2,1,0:T(8,128)(2,1)S(1)}, bf16[64,6,128,128]{3,2,1,0:T(8,128)(2,1)}, u32[]{:S(2)}) copy-start(bf16[64,6,128,128]{3,2,1,0:T(8,128)(2,1)} %blocks.1) | copy-start | bytes 37748740
  (1 other events, 0.9 us)

commit v3 on v2

v3 whole, which is shorter than its diff:
```python
import functools

import jax
import jax.numpy as jnp
from jax import lax
from jax.experimental import pallas as pl
from jax.experimental.pallas import tpu as pltpu
from jax.sharding import PartitionSpec as P

highest = lax.Precision.HIGHEST
AXES = ("sx", "sy")
f32 = jnp.float32
bf16 = jnp.bfloat16
NN = (((1,), (0,)), ((), ()))
NT = (((1,), (1,)), ((), ()))


def mm(a, b, dims=NN, precision=None):
    return lax.dot_general(a, b, dims, precision=precision, preferred_element_type=f32)


def in_hbm(x):
    return pltpu.with_memory_space_constraint(x, pltpu.HBM)


VMEM = pl.BlockSpec(memory_space=pltpu.VMEM)


def params(mib):
    return pltpu.CompilerParams(
        dimension_semantics=("arbitrary",), vmem_limit_bytes=mib * 1024 * 1024
    )


def moments_kernel(charges, basis, child, parent, send, box):
    step = pl.program_id(0)
    leaf_pairs = 8 * pl.num_programs(0)
    rank = basis.shape[1]
    pairs = [
        jnp.concatenate(
            [mm(charges[c], basis[c], NT), mm(charges[c + 1], basis[c + 1], NT)], axis=1
        ).astype(bf16)
        for c in range(0, 16, 2)
    ]
    parents = [
        mm(
            jnp.concatenate(pairs[4 * p : 4 * p + 4], axis=1),
            child[8 * p : 8 * p + 8].reshape(8 * rank, rank),
        )
        for p in range(2)
    ]
    for i, pair in enumerate(pairs):
        send[step * 8 + i] = pair
    both = jnp.concatenate(parents, axis=1).astype(bf16)
    send[leaf_pairs + step] = both
    part = mm(both, parent[...].reshape(2 * rank, rank))

    @pl.when(step == 0)
    def _():
        box[...] = part

    @pl.when(step > 0)
    def _():
        box[...] += part


def moments_call(charges, basis, child, parent):
    leaves, columns, points = charges.shape
    rank = basis.shape[1]
    parents = parent.shape[0]
    steps = parents // 2
    pairs = leaves // 2 + parents // 2
    return pl.pallas_call(
        moments_kernel,
        grid=(steps,),
        in_specs=[
            pl.BlockSpec((16, columns, points), lambda i: (i, 0, 0)),
            pl.BlockSpec((16, rank, points), lambda i: (i, 0, 0)),
            pl.BlockSpec((16, rank, rank), lambda i: (i, 0, 0)),
            pl.BlockSpec((2, rank, rank), lambda i: (i, 0, 0)),
        ],
        out_specs=[
            pl.BlockSpec((pairs, columns, 2 * rank), lambda i: (0, 0, 0)),
            pl.BlockSpec((columns, rank), lambda i: (0, 0)),
        ],
        out_shape=[
            jax.ShapeDtypeStruct((pairs, columns, 2 * rank), bf16),
            jax.ShapeDtypeStruct((columns, rank), f32),
        ],
        compiler_params=params(16),
        name="moments",
    )(in_hbm(charges), in_hbm(basis), in_hbm(child), in_hbm(parent))


OPS_BLOCK = 128


def table_kernel(ops, table, turned):
    level = pl.program_id(0)
    first = pl.program_id(1) * OPS_BLOCK
    rank = ops.shape[1]
    half = rank // 2
    stride = turned.shape[0] // half
    for k in range(half):
        both = jnp.concatenate([ops[0, k], ops[0, k + half]], axis=0).astype(f32)
        turned[k * stride : k * stride + OPS_BLOCK, :] = both.T
    for o in range(OPS_BLOCK):
        rows = turned[pl.ds(o, half, stride=stride), :]
        table[level, first + o] = jnp.concatenate([rows[:, :rank], rows[:, rank:]], axis=0).astype(bf16)


def table_call(ops):
    levels, count, rank, _ = ops.shape
    blocks = pl.cdiv(count, OPS_BLOCK)
    turned_view = jnp.transpose(ops, (0, 2, 3, 1))
    return pl.pallas_call(
        table_kernel,
        grid=(levels, blocks),
        in_specs=[pl.BlockSpec((1, rank, rank, OPS_BLOCK), lambda t, i: (t, 0, 0, i))],
        out_specs=VMEM,
        out_shape=jax.ShapeDtypeStruct((levels, blocks * OPS_BLOCK, rank, rank), bf16),
        scratch_shapes=[pltpu.VMEM((rank // 2 * (OPS_BLOCK + 8), 2 * rank), f32)],
        compiler_params=pltpu.CompilerParams(
            dimension_semantics=("arbitrary", "arbitrary"), vmem_limit_bytes=16 * 1024 * 1024
        ),
        name="operator_table",
    )(in_hbm(turned_view))


NEAR_LEAVES = 8


def near_kernel(base, near, left, own, right, blocks, far, out, sources):
    step = pl.program_id(0)
    leaves = own.shape[0]

    @pl.when(step == 0)
    def _():
        for i, ref in enumerate((left, own, right)):
            for n in range(0, leaves, 8):
                sources[i * leaves + n : i * leaves + n + 8] = ref[n : n + 8]

    count = blocks.shape[1]
    results = []
    for i in range(NEAR_LEAVES):
        row = step * NEAR_LEAVES + i
        acc = far[i]
        for n in range(0, count, 2):
            lhs = jnp.concatenate(
                [sources[near[n, row] - base[0]], sources[near[n + 1, row] - base[0]]], axis=1
            )
            rhs = jnp.concatenate([blocks[i, n], blocks[i, n + 1]], axis=1)
            acc = acc + mm(lhs, rhs, NT)
        results.append(acc)
    for i, acc in enumerate(results):
        out[i] = acc


def near_call(base, near_rows, left, own, right, blocks, far):
    leaves, columns, points = own.shape
    count = blocks.shape[1]
    return pl.pallas_call(
        near_kernel,
        grid_spec=pltpu.PrefetchScalarGridSpec(
            num_scalar_prefetch=2,
            grid=(leaves // NEAR_LEAVES,),
            in_specs=[
                VMEM,
                VMEM,
                VMEM,
                pl.BlockSpec((NEAR_LEAVES, count, points, points), lambda i, *_: (i, 0, 0, 0)),
                pl.BlockSpec((NEAR_LEAVES, columns, points), lambda i, *_: (i, 0, 0)),
            ],
            out_specs=pl.BlockSpec((NEAR_LEAVES, columns, points), lambda i, *_: (i, 0, 0)),
            scratch_shapes=[
                pltpu.VMEM((3 * leaves, columns, points), bf16),
            ],
        ),
        out_shape=jax.ShapeDtypeStruct((leaves, columns, points), f32),
        compiler_params=params(16),
        name="near",
    )(base, near_rows, left, own, right, in_hbm(blocks), far)


def doubled(pair, low):
    rank = pair.shape[1] // 2
    swapped = jnp.concatenate([pair[:, rank:], pair[:, :rank]], axis=1)
    return jnp.where(low, pair, swapped), jnp.where(low, swapped, pair)


def translated(acc, sources, table, level, lists, ops, base, at, low):
    for e in range(0, len(at), 4):
        picked = [sources[lists[at[e + i]] - base] for i in range(4)]
        lhs = jnp.concatenate(
            [jnp.where(low, picked[0], picked[1]), jnp.where(low, picked[2], picked[3])], axis=1
        )
        rhs = jnp.concatenate([table[level, ops[at[e + i]]] for i in range(4)], axis=0)
        acc = acc + mm(lhs, rhs)
    return acc


def far_kernel(
    base, list0, op0, list1, op1,
    left, own, right, table, transfer, couple, parent, child, basis, *rest,
):
    siblings = rest[:-4]
    out, leaf_sources, parent_sources, parent_locals = rest[-4:]
    leaves = basis.shape[0]
    parents = parent.shape[0]
    columns = own.shape[1]
    rank = own.shape[2] // 2
    low = lax.broadcasted_iota(jnp.int32, (columns, 2 * rank), 1) < rank
    for i, ref in enumerate((left, own, right)):
        for n in range(leaves // 2):
            a, b = doubled(ref[n], low)
            leaf_sources[i * leaves + 2 * n] = a
            leaf_sources[i * leaves + 2 * n + 1] = b
        for n in range(parents // 2):
            a, b = doubled(ref[leaves // 2 + n], low)
            parent_sources[i * parents + 2 * n] = a
            parent_sources[i * parents + 2 * n + 1] = b
    field = None
    for sibling in reversed(siblings):
        term = mm(sibling[...], couple[...], precision=highest)
        if field is not None:
            term = term + mm(field, transfer[...], NT, precision=highest)
        field = term
    box_local = field.astype(bf16)
    accs = [
        translated(
            mm(box_local, parent[q], NT), parent_sources, table, 1, list1, op1, base[1],
            [(q, e) for e in range(list1.shape[1])], low,
        )
        for q in range(parents)
    ]
    for q, acc in enumerate(accs):
        parent_locals[q] = acc.astype(bf16)

    def one_parent(q, _):
        parent_local = parent_locals[q]
        accs = [
            translated(
                mm(parent_local, child[q * 8 + c], NT), leaf_sources, table, 0, list0, op0, base[0],
                [(e, q * 8 + c) for e in range(list0.shape[0])], low,
            )
            for c in range(8)
        ]
        results = [mm(acc.astype(bf16), basis[q * 8 + c]) for c, acc in enumerate(accs)]
        for c, acc in enumerate(results):
            out[q * 8 + c] = acc
        return 0

    lax.fori_loop(0, parents, one_parent, 0)


def far_call(base, list0, op0, list1, op1, left, own, right, table, siblings, transfer, couple, parent, child, basis):
    leaves, rank, points = basis.shape
    parents = parent.shape[0]
    columns = own.shape[1]
    smem = pl.BlockSpec(memory_space=pltpu.SMEM)
    return pl.pallas_call(
        far_kernel,
        in_specs=[smem] * 5 + [VMEM] * (9 + len(siblings)),
        out_specs=VMEM,
        scratch_shapes=[
            pltpu.VMEM((3 * leaves, columns, 2 * rank), bf16),
            pltpu.VMEM((3 * parents, columns, 2 * rank), bf16),
            pltpu.VMEM((parents, columns, rank), bf16),
        ],
        out_shape=jax.ShapeDtypeStruct((leaves, columns, points), f32),
        compiler_params=pltpu.CompilerParams(vmem_limit_bytes=16 * 1024 * 1024),
        name="far",
    )(base, list0, op0, list1, op1, left, own, right, table, transfer, couple, parent, child, basis, *siblings)


def to_right(block):
    count = lax.axis_size(AXES)
    return lax.ppermute(block, AXES, [(i, i + 1) for i in range(count - 1)])


def to_left(block):
    count = lax.axis_size(AXES)
    return lax.ppermute(block, AXES, [(i + 1, i) for i in range(count - 1)])


def from_partner(block, apart):
    count = lax.axis_size(AXES)
    return lax.ppermute(block, AXES, [(i, i ^ (1 << apart)) for i in range(count)])


def local(
    charges, near_blocks, near_list, leaf_basis, child_transfer, parent_transfer, m2l_ops,
    far_list0, far_op0, far_list1, far_op1, top_transfer, top_couple,
):
    leaves = charges.shape[0]
    parents = parent_transfer.shape[0]
    device = lax.axis_index(AXES)
    base = jnp.stack([(device - 1) * leaves, (device - 1) * parents]).astype(jnp.int32)
    send, box = moments_call(charges, leaf_basis, child_transfer, parent_transfer)
    height = lax.axis_size(AXES).bit_length() - 1
    siblings = []
    current = box
    for level_bit in range(height):
        if level_bit == 2:
            send, current = lax.optimization_barrier((send, current))
            moments_left = to_right(send)
            moments_right = to_left(send)
        partner = from_partner(current, level_bit)
        if level_bit == 2:
            charges_left = to_right(charges)
            charges_right = to_left(charges)
        siblings.append(partner)
        if level_bit + 1 < height:
            current = mm(current + partner, top_transfer, precision=highest)
    table = table_call(m2l_ops)
    far = far_call(
        base, far_list0.T, far_op0.T, far_list1, far_op1,
        moments_left, send, moments_right, table, siblings,
        top_transfer, top_couple, parent_transfer, child_transfer, leaf_basis,
    )
    return near_call(base, near_list.T, charges_left, charges, charges_right, near_blocks, far)


def solution(mesh):
    split = P(AXES)
    placed = (split,) * 6 + (P(),) + (split,) * 4 + (P(), P())
    return jax.shard_map(local, mesh=mesh, in_specs=placed, out_specs=split, check_vma=False)
```

time: 94 us -> 88.2 us (0.938)
  local copies, waits for them, and re-layouts: 15.4 us -> 0.06 us
  waiting for transfers between devices: 7.57 us -> 20.2 us
  starting transfers between devices: 35 us -> 30.3 us
  matrix products: 0.64 us -> 3.67 us
  Pallas kernels: 34.7 us -> 32.9 us
    unnamed x38 -> x22, local copies, waits for them, and re-layouts: 15.4 us -> 0.06 us
    ppermute x5, waiting for transfers between devices: 7.56 us -> 20.2 us  [from_partner(): lax.ppermute(block, AXES, [(i, i ^ 1 << apart) for i in range(count)])]
    pallas_call x1, Pallas kernels: 15.2 us -> 10.1 us  [far_call(): pl.pallas_call(far_kernel, in_specs=[smem] * 5 + [VMEM] * (9 + len(siblin...]
    ppermute x2, starting transfers between devices: 7.6 us -> 3.33 us  [to_right(): return lax.ppermute(block, AXES, [(i, i + 1) for i in range(count - 1)])]
    dot_general x4, matrix products: 0.64 us -> 3.67 us  [mm(): lax.dot_general(a, b, dims, precision=precision, preferred_element_type=f32)]
    pallas_call x1, Pallas kernels: 8.43 us -> 11.1 us  [near_call(): pl.pallas_call(near_kernel, grid_spec=pltpu.PrefetchScalarGridSpec(num_sc...]
    pallas_call x1, Pallas kernels: 6.3 us -> 7.44 us  [table_call(): pl.pallas_call(table_kernel, grid=(levels, blocks), in_specs=[pl.BlockSpe...]
  transfers between devices with their start and end apart: 9 -> 9, of which waited for: 4 -> 2; matrix products, arithmetic and copies ran while one was open for 1% -> 4% of each run, Pallas kernels for 23% -> 20%
where the time goes in v3:
time: 88.2 us; the launch traced here: 87.5 us
  Pallas kernels  32.9 us (37%)
  starting transfers between devices  30.3 us (34%)
  waiting for transfers between devices  20.2 us (23%)
  matrix products  3.67 us (4%)
    ppermute x5, starting transfers between devices, from_partner(): lax.ppermute(block, AXES, [(i, i ^ 1 << apart) for i in range(count)])  24.4 us
    ppermute x5, waiting for transfers between devices, from_partner(): lax.ppermute(block, AXES, [(i, i ^ 1 << apart) for i in range(count)])  20.2 us
    pallas_call x1, Pallas kernels, near_call(): pl.pallas_call(near_kernel, grid_spec=pltpu.PrefetchScalarGridSpec(num_sc...  11.1 us
    pallas_call x1, Pallas kernels, far_call(): pl.pallas_call(far_kernel, in_specs=[smem] * 5 + [VMEM] * (9 + len(siblin...  10.1 us
    pallas_call x1, Pallas kernels, table_call(): pl.pallas_call(table_kernel, grid=(levels, blocks), in_specs=[pl.BlockSpe...  7.44 us
    pallas_call x1, Pallas kernels, moments_call(): pl.pallas_call(moments_kernel, grid=(steps,), in_specs=[pl.BlockSpec((16,...  4.24 us
    dot_general x4, matrix products, mm(): lax.dot_general(a, b, dims, precision=precision, preferred_element_type=f32)  3.67 us
    ppermute x2, starting transfers between devices, to_right(): return lax.ppermute(block, AXES, [(i, i + 1) for i in range(count - 1)])  3.33 us
  transfers between devices with their start and end apart: 9, of which 2 were waited for; matrix products, arithmetic and copies ran while one was open for 4% of the time, Pallas kernels for 20%

profile of v3, /device:TPU:0, one launch (start us, length us, event | category | flops | bytes accessed | tf_op | source)
XLA Modules:
  0.0 87.5 jit_solution(11706534742537940555)
XLA Ops:
  0.0 4.2 %moments.1 = (bf16[36,64,128]{2,1,0:T(8,128)(2,1)S(1)}, f32[64,64]{1,0:T(8,128)S(1)}) custom-call(bf16[64,64,128]{2,1,0:T(8,128)(2,1)} %own.1, bf16[64,64,128]{2,1,0:T(8,128)(2,1)} %basis.3, bf16[64,64,64]{2,1,0:T(8,128)(2,1)} %child.3, bf16[8,64,64]{2,1,0:T(8,128)(2,1)} %parent.3), custom_call_target="tpu_custom_call" | custom-call | tf_op jit(solution)/shard_map/moments/pallas_call | solution.py:73
  4.2 0.5 collective-permute-start.2
  4.8 2.0 %collective-permute-start = (bf16[64,64,128]{2,1,0:T(8,128)(2,1)}, bf16[64,64,128]{2,1,0:T(8,128)(2,1)S(1)}, u32[]{:S(2)}, u32[]{:S(2)}) collective-permute-start(bf16[64,64,128]{2,1,0:T(8,128)(2,1)} %own.1), channel_id=1, source_target_pairs={{0,1},{1,2},{2,3},{3,4},{4,5},{5,6},{6,7},{7,8},{8,9},{9,10},{10,1... | collective-permute-start | bytes 3145736 | tf_op jit(solution)/shard_map/ppermute | solution.py:278
  6.8 1.3 %collective-permute-start.1 = (bf16[64,64,128]{2,1,0:T(8,128)(2,1)}, bf16[64,64,128]{2,1,0:T(8,128)(2,1)S(1)}, u32[]{:S(2)}, u32[]{:S(2)}) collective-permute-start(bf16[64,64,128]{2,1,0:T(8,128)(2,1)} %own.1), channel_id=1, source_target_pairs={{1,0},{2,1},{3,2},{4,3},{5,4},{6,5},{7,6},{8,7},{9,8},{10,9},{11,1... | collective-permute-start | bytes 3145736 | tf_op jit(solution)/shard_map/ppermute | solution.py:283
  8.1 0.9 %fusion.6 = f32[64,64]{1,0:T(8,128)S(1)} fusion(f32[64,64]{1,0:T(8,128)} %transfer.1, f32[64,64]{1,0:T(8,128)S(1)} %get-tuple-element.10, f32[64,64]{1,0:T(8,128)S(1)} %collective-permute-done.2.rest_0_), kind=kOutput, calls=%fused_computation.6 | convolution fusion | flops 3149824 | bytes 65536 | tf_op jit(solution)/shard_map/dot_general | solution.py:19
  9.0 4.8 %collective-permute-start.3 = (f32[64,64]{1,0:T(8,128)S(1)}, f32[64,64]{1,0:T(8,128)S(1)}, u32[]{:S(2)}, u32[]{:S(2)}) collective-permute-start(f32[64,64]{1,0:T(8,128)S(1)} %fusion.6), channel_id=1, source_target_pairs={{0,2},{1,3},{2,0},{3,1},{4,6},{5,7},{6,4},{7,5},{8,10},{9,11},{10,... | collective-permute-start | bytes 49160 | tf_op jit(solution)/shard_map/ppermute | solution.py:288
  13.9 12.7 %collective-permute-done.3.rest_1_ = f32[64,64]{1,0:T(8,128)S(1)} collective-permute-done((f32[64,64]{1,0:T(8,128)S(1)}, f32[64,64]{1,0:T(8,128)S(1)}, u32[]{:S(2)}, u32[]{:S(2)}) %collective-permute-start.3) | collective-permute-done | bytes 16416 | tf_op jit(solution)/shard_map/ppermute | solution.py:288
  26.5 0.9 %fusion.4 = f32[64,64]{1,0:T(8,128)S(1)} fusion(f32[64,64]{1,0:T(8,128)} %transfer.1, f32[64,64]{1,0:T(8,128)S(1)} %fusion.6, f32[64,64]{1,0:T(8,128)S(1)} %collective-permute-done.3.rest_1_), kind=kOutput, calls=%fused_computation.4 | convolution fusion | flops 3149824 | bytes 65536 | tf_op jit(solution)/shard_map/dot_general | solution.py:19
  27.5 10.0 %collective-permute-start.6 = (f32[64,64]{1,0:T(8,128)S(1)}, f32[64,64]{1,0:T(8,128)S(1)}, u32[]{:S(2)}, u32[]{:S(2)}) collective-permute-start(f32[64,64]{1,0:T(8,128)S(1)} %fusion.4), channel_id=1, source_target_pairs={{0,4},{1,5},{2,6},{3,7},{4,0},{5,1},{6,2},{7,3},{8,12},{9,13},{10,... | collective-permute-start | bytes 49160 | tf_op jit(solution)/shard_map/ppermute | solution.py:288
  37.4 1.3 %collective-permute-start.4 = (bf16[36,64,128]{2,1,0:T(8,128)(2,1)S(1)}, bf16[36,64,128]{2,1,0:T(8,128)(2,1)S(1)}, u32[]{:S(2)}, u32[]{:S(2)}) collective-permute-start(bf16[36,64,128]{2,1,0:T(8,128)(2,1)S(1)} %get-tuple-element.11.own), channel_id=1, source_target_pairs={{0,1},{1,2},{2,3},{3,4},{4,5},{5,6},{6,7},{7,8},{8,9},{9,10},{10,1... | collective-permute-start | bytes 1769480 | tf_op jit(solution)/shard_map/ppermute | solution.py:278
  38.7 1.3 %collective-permute-start.5 = (bf16[36,64,128]{2,1,0:T(8,128)(2,1)S(1)}, bf16[36,64,128]{2,1,0:T(8,128)(2,1)}, u32[]{:S(2)}, u32[]{:S(2)}) collective-permute-start(bf16[36,64,128]{2,1,0:T(8,128)(2,1)S(1)} %get-tuple-element.11.own), channel_id=1, source_target_pairs={{1,0},{2,1},{3,2},{4,3},{5,4},{6,5},{7,6},{8,7},{9,8},{10,9},{11,1... | collective-permute-start | bytes 1769480 | tf_op jit(solution)/shard_map/ppermute | solution.py:283
  40.1 0.9 %fusion.2 = f32[64,64]{1,0:T(8,128)S(1)} fusion(f32[64,64]{1,0:T(8,128)} %transfer.1, f32[64,64]{1,0:T(8,128)S(1)} %fusion.4, f32[64,64]{1,0:T(8,128)S(1)} %collective-permute-done.6.rest_2_), kind=kOutput, calls=%fused_computation.2 | convolution fusion | flops 3149824 | bytes 65536 | tf_op jit(solution)/shard_map/dot_general | solution.py:19
  41.0 6.4 %collective-permute-start.7 = (f32[64,64]{1,0:T(8,128)S(1)}, f32[64,64]{1,0:T(8,128)S(1)}, u32[]{:S(2)}, u32[]{:S(2)}) collective-permute-start(f32[64,64]{1,0:T(8,128)S(1)} %fusion.2), channel_id=1, source_target_pairs={{0,8},{1,9},{2,10},{3,11},{4,12},{5,13},{6,14},{7,15},{8,0},{9,1},... | collective-permute-start | bytes 49160 | tf_op jit(solution)/shard_map/ppermute | solution.py:288
  47.4 7.5 %collective-permute-done.7.rest_3_ = f32[64,64]{1,0:T(8,128)S(1)} collective-permute-done((f32[64,64]{1,0:T(8,128)S(1)}, f32[64,64]{1,0:T(8,128)S(1)}, u32[]{:S(2)}, u32[]{:S(2)}) %collective-permute-start.7) | collective-permute-done | bytes 16416 | tf_op jit(solution)/shard_map/ppermute | solution.py:288
  54.9 0.9 %fusion = f32[64,64]{1,0:T(8,128)S(1)} fusion(f32[64,64]{1,0:T(8,128)} %transfer.1, f32[64,64]{1,0:T(8,128)S(1)} %fusion.2, f32[64,64]{1,0:T(8,128)S(1)} %collective-permute-done.7.rest_3_), kind=kOutput, calls=%fused_computation | convolution fusion | flops 3149824 | bytes 65536 | tf_op jit(solution)/shard_map/dot_general | solution.py:19
  55.8 2.7 %collective-permute-start.8 = (f32[64,64]{1,0:T(8,128)S(1)}, f32[64,64]{1,0:T(8,128)S(1)}, u32[]{:S(2)}, u32[]{:S(2)}) collective-permute-start(f32[64,64]{1,0:T(8,128)S(1)} %fusion), channel_id=1, source_target_pairs={{0,16},{1,17},{2,18},{3,19},{4,20},{5,21},{6,22},{7,23},{8,24},{9,... | collective-permute-start | bytes 49160 | tf_op jit(solution)/shard_map/ppermute | solution.py:288
  58.5 0.1 pad_add_fusion.base
  58.6 0.0 copy-start.7
  58.6 0.0 copy-start.9
  58.6 7.4 %operator_table.1.table = bf16[2,384,64,64]{3,2,1,0:T(8,128)(2,1)S(1)} custom-call(bf16[2,64,64,316]{3,2,1,0:T(8,128)(2,1)} %bitcast.13), custom_call_target="tpu_custom_call" | custom-call | tf_op jit(solution)/shard_map/operator_table/pallas_call | solution.py:116
  66.2 0.0 copy-start.2
  66.2 0.0 copy-start.8
  66.2 10.1 %far.1 = f32[64,64,128]{2,1,0:T(8,128)S(1)} custom-call(s32[2]{0:T(128)S(1)} %pad_add_fusion.base, s32[24,64]{1,0:T(8,128)S(1)} %bitcast.10, s32[24,64]{1,0:T(8,128)S(1)} %bitcast.11, s32[8,24]{1,0:T(8,128)S(1)} %copy-done.9, s32[8,24]{1,0:T(8,128)S(1)} %copy-done.10, bf16[36,64,128]{2,1,0:T(8,128)(2,1)S(1)} %collective-permute-done.4.left, ...), custom_call_target="tpu_custom_call" | custom-call | tf_op jit(solution)/shard_map/far/pallas_call | solution.py:261
  76.3 11.1 %near.1 = f32[64,64,128]{2,1,0:T(8,128)} custom-call(s32[2]{0:T(128)S(1)} %pad_add_fusion.base, s32[6,64]{1,0:T(8,128)S(1)} %bitcast.12, bf16[64,64,128]{2,1,0:T(8,128)(2,1)S(1)} %collective-permute-done.left, bf16[64,64,128]{2,1,0:T(8,128)(2,1)S(1)} %copy-done.2, bf16[64,64,128]{2,1,0:T(8,128)(2,1)S(1)} %collective-permute-done.1.right, ...), custom_call_target="tpu_custom_call" | custom-call | tf_op jit(solution)/shard_map/near/pallas_call | solution.py:162
  (25 shorter events, 0.1 us)
Async XLA Ops:
  4.2 3.8 %collective-permute-start.2 = (f32[64,64]{1,0:T(8,128)S(1)}, f32[64,64]{1,0:T(8,128)S(1)}, u32[]{:S(2)}, u32[]{:S(2)}) collective-permute-start(f32[64,64]{1,0:T(8,128)S(1)} %get-tuple-element.10), channel_id=1, source_target_pairs={{0,1},{1,0},{2,3},{3,2},{4,5},{5,4},{6,7},{7,6},{8,9},{9,8},{10,11... | collective-permute-start | bytes 49160 | tf_op jit(solution)/shard_map/ppermute | solution.py:288
  4.8 71.5 %collective-permute-start = (bf16[64,64,128]{2,1,0:T(8,128)(2,1)}, bf16[64,64,128]{2,1,0:T(8,128)(2,1)S(1)}, u32[]{:S(2)}, u32[]{:S(2)}) collective-permute-start(bf16[64,64,128]{2,1,0:T(8,128)(2,1)} %own.1), channel_id=1, source_target_pairs={{0,1},{1,2},{2,3},{3,4},{4,5},{5,6},{6,7},{7,8},{8,9},{9,10},{10,1... | collective-permute-start | bytes 3145736 | tf_op jit(solution)/shard_map/ppermute | solution.py:278
  6.8 69.5 %collective-permute-start.1 = (bf16[64,64,128]{2,1,0:T(8,128)(2,1)}, bf16[64,64,128]{2,1,0:T(8,128)(2,1)S(1)}, u32[]{:S(2)}, u32[]{:S(2)}) collective-permute-start(bf16[64,64,128]{2,1,0:T(8,128)(2,1)} %own.1), channel_id=1, source_target_pairs={{1,0},{2,1},{3,2},{4,3},{5,4},{6,5},{7,6},{8,7},{9,8},{10,9},{11,1... | collective-permute-start | bytes 3145736 | tf_op jit(solution)/shard_map/ppermute | solution.py:283
  9.0 17.5 %collective-permute-start.3 = (f32[64,64]{1,0:T(8,128)S(1)}, f32[64,64]{1,0:T(8,128)S(1)}, u32[]{:S(2)}, u32[]{:S(2)}) collective-permute-start(f32[64,64]{1,0:T(8,128)S(1)} %fusion.6), channel_id=1, source_target_pairs={{0,2},{1,3},{2,0},{3,1},{4,6},{5,7},{6,4},{7,5},{8,10},{9,11},{10,... | collective-permute-start | bytes 49160 | tf_op jit(solution)/shard_map/ppermute | solution.py:288
  27.5 12.6 %collective-permute-start.6 = (f32[64,64]{1,0:T(8,128)S(1)}, f32[64,64]{1,0:T(8,128)S(1)}, u32[]{:S(2)}, u32[]{:S(2)}) collective-permute-start(f32[64,64]{1,0:T(8,128)S(1)} %fusion.4), channel_id=1, source_target_pairs={{0,4},{1,5},{2,6},{3,7},{4,0},{5,1},{6,2},{7,3},{8,12},{9,13},{10,... | collective-permute-start | bytes 49160 | tf_op jit(solution)/shard_map/ppermute | solution.py:288
  37.4 28.7 %collective-permute-start.4 = (bf16[36,64,128]{2,1,0:T(8,128)(2,1)S(1)}, bf16[36,64,128]{2,1,0:T(8,128)(2,1)S(1)}, u32[]{:S(2)}, u32[]{:S(2)}) collective-permute-start(bf16[36,64,128]{2,1,0:T(8,128)(2,1)S(1)} %get-tuple-element.11.own), channel_id=1, source_target_pairs={{0,1},{1,2},{2,3},{3,4},{4,5},{5,6},{6,7},{7,8},{8,9},{9,10},{10,1... | collective-permute-start | bytes 1769480 | tf_op jit(solution)/shard_map/ppermute | solution.py:278
  38.7 27.3 %collective-permute-start.5 = (bf16[36,64,128]{2,1,0:T(8,128)(2,1)S(1)}, bf16[36,64,128]{2,1,0:T(8,128)(2,1)}, u32[]{:S(2)}, u32[]{:S(2)}) collective-permute-start(bf16[36,64,128]{2,1,0:T(8,128)(2,1)S(1)} %get-tuple-element.11.own), channel_id=1, source_target_pairs={{1,0},{2,1},{3,2},{4,3},{5,4},{6,5},{7,6},{8,7},{9,8},{10,9},{11,1... | collective-permute-start | bytes 1769480 | tf_op jit(solution)/shard_map/ppermute | solution.py:283
  41.0 13.9 %collective-permute-start.7 = (f32[64,64]{1,0:T(8,128)S(1)}, f32[64,64]{1,0:T(8,128)S(1)}, u32[]{:S(2)}, u32[]{:S(2)}) collective-permute-start(f32[64,64]{1,0:T(8,128)S(1)} %fusion.2), channel_id=1, source_target_pairs={{0,8},{1,9},{2,10},{3,11},{4,12},{5,13},{6,14},{7,15},{8,0},{9,1},... | collective-permute-start | bytes 49160 | tf_op jit(solution)/shard_map/ppermute | solution.py:288
  55.8 10.2 %collective-permute-start.8 = (f32[64,64]{1,0:T(8,128)S(1)}, f32[64,64]{1,0:T(8,128)S(1)}, u32[]{:S(2)}, u32[]{:S(2)}) collective-permute-start(f32[64,64]{1,0:T(8,128)S(1)} %fusion), channel_id=1, source_target_pairs={{0,16},{1,17},{2,18},{3,19},{4,20},{5,21},{6,22},{7,23},{8,24},{9,... | collective-permute-start | bytes 49160 | tf_op jit(solution)/shard_map/ppermute | solution.py:288
  58.5 7.5 %copy-start = (bf16[64,64,128]{2,1,0:T(8,128)(2,1)S(1)}, bf16[64,64,128]{2,1,0:T(8,128)(2,1)}, u32[]{:S(2)}) copy-start(bf16[64,64,128]{2,1,0:T(8,128)(2,1)} %basis.3) | copy-start | bytes 3145732
  58.6 7.6 %copy-start.1 = (bf16[64,64,64]{2,1,0:T(8,128)(2,1)S(1)}, bf16[64,64,64]{2,1,0:T(8,128)(2,1)}, u32[]{:S(2)}) copy-start(bf16[64,64,64]{2,1,0:T(8,128)(2,1)} %child.3) | copy-start | bytes 1572868
  58.6 7.6 %copy-start.3 = (f32[64,64]{1,0:T(8,128)S(1)}, f32[64,64]{1,0:T(8,128)}, u32[]{:S(2)}) copy-start(f32[64,64]{1,0:T(8,128)} %transfer.1) | copy-start | bytes 49156
  58.6 7.6 %copy-start.4 = (bf16[8,64,64]{2,1,0:T(8,128)(2,1)S(1)}, bf16[8,64,64]{2,1,0:T(8,128)(2,1)}, u32[]{:S(2)}) copy-start(bf16[8,64,64]{2,1,0:T(8,128)(2,1)} %parent.3) | copy-start | bytes 196612
  58.6 7.6 %copy-start.5 = (f32[64,64]{1,0:T(8,128)S(1)}, f32[64,64]{1,0:T(8,128)}, u32[]{:S(2)}) copy-start(f32[64,64]{1,0:T(8,128)} %couple.1) | copy-start | bytes 49156
  58.6 7.6 %copy-start.6 = (s32[64,24]{0,1:T(8,128)S(1)}, s32[64,24]{0,1:T(8,128)}, u32[]{:S(2)}) copy-start(s32[64,24]{0,1:T(8,128)} %param.20) | copy-start | bytes 18436
  58.6 7.6 %copy-start.7 = (s32[64,24]{0,1:T(8,128)S(1)}, s32[64,24]{0,1:T(8,128)}, u32[]{:S(2)}) copy-start(s32[64,24]{0,1:T(8,128)} %param.21) | copy-start | bytes 18436
  58.6 7.6 %copy-start.9 = (s32[8,24]{1,0:T(8,128)S(1)}, s32[8,24]{1,0:T(8,128)}, u32[]{:S(2)}) copy-start(s32[8,24]{1,0:T(8,128)} %list1.1) | copy-start | bytes 2308
  58.6 7.6 %copy-start.10 = (s32[8,24]{1,0:T(8,128)S(1)}, s32[8,24]{1,0:T(8,128)}, u32[]{:S(2)}) copy-start(s32[8,24]{1,0:T(8,128)} %op1.1) | copy-start | bytes 2308
  66.2 10.1 %copy-start.2 = (bf16[64,64,128]{2,1,0:T(8,128)(2,1)S(1)}, bf16[64,64,128]{2,1,0:T(8,128)(2,1)}, u32[]{:S(2)}) copy-start(bf16[64,64,128]{2,1,0:T(8,128)(2,1)} %own.1) | copy-start | bytes 3145732
  66.2 10.1 %copy-start.8 = (s32[64,6]{0,1:T(8,128)S(1)}, s32[64,6]{0,1:T(8,128)}, u32[]{:S(2)}) copy-start(s32[64,6]{0,1:T(8,128)} %param.15) | copy-start | bytes 4612

commit v4 on v3

v4 whole, which is shorter than its diff:
```python
import functools

import jax
import jax.numpy as jnp
from jax import lax
from jax.experimental import pallas as pl
from jax.experimental.pallas import tpu as pltpu
from jax.sharding import PartitionSpec as P

highest = lax.Precision.HIGHEST
AXES = ("sx", "sy")
f32 = jnp.float32
bf16 = jnp.bfloat16
NN = (((1,), (0,)), ((), ()))
NT = (((1,), (1,)), ((), ()))


def mm(a, b, dims=NN, precision=None):
    return lax.dot_general(a, b, dims, precision=precision, preferred_element_type=f32)


def in_hbm(x):
    return pltpu.with_memory_space_constraint(x, pltpu.HBM)


VMEM = pl.BlockSpec(memory_space=pltpu.VMEM)
HBM = pl.BlockSpec(memory_space=pltpu.HBM)
SMEM = pl.BlockSpec(memory_space=pltpu.SMEM)


def params(mib):
    return pltpu.CompilerParams(
        dimension_semantics=("arbitrary",), vmem_limit_bytes=mib * 1024 * 1024
    )


def moments_kernel(charges, basis, child, parent, send, box):
    step = pl.program_id(0)
    leaf_pairs = 8 * pl.num_programs(0)
    rank = basis.shape[1]
    pairs = [
        jnp.concatenate(
            [mm(charges[c], basis[c], NT), mm(charges[c + 1], basis[c + 1], NT)], axis=1
        ).astype(bf16)
        for c in range(0, 16, 2)
    ]
    parents = [
        mm(
            jnp.concatenate(pairs[4 * p : 4 * p + 4], axis=1),
            child[8 * p : 8 * p + 8].reshape(8 * rank, rank),
        )
        for p in range(2)
    ]
    for i, pair in enumerate(pairs):
        send[step * 8 + i] = pair
    both = jnp.concatenate(parents, axis=1).astype(bf16)
    send[leaf_pairs + step] = both
    part = mm(both, parent[...].reshape(2 * rank, rank))

    @pl.when(step == 0)
    def _():
        box[...] = part

    @pl.when(step > 0)
    def _():
        box[...] += part


def moments_call(charges, basis, child, parent):
    leaves, columns, points = charges.shape
    rank = basis.shape[1]
    parents = parent.shape[0]
    steps = parents // 2
    pairs = leaves // 2 + parents // 2
    return pl.pallas_call(
        moments_kernel,
        grid=(steps,),
        in_specs=[
            pl.BlockSpec((16, columns, points), lambda i: (i, 0, 0)),
            pl.BlockSpec((16, rank, points), lambda i: (i, 0, 0)),
            pl.BlockSpec((16, rank, rank), lambda i: (i, 0, 0)),
            pl.BlockSpec((2, rank, rank), lambda i: (i, 0, 0)),
        ],
        out_specs=[
            pl.BlockSpec((pairs, columns, 2 * rank), lambda i: (0, 0, 0)),
            pl.BlockSpec((columns, rank), lambda i: (0, 0)),
        ],
        out_shape=[
            pltpu.HBM((pairs, columns, 2 * rank), bf16),
            jax.ShapeDtypeStruct((columns, rank), f32),
        ],
        compiler_params=params(16),
        name="moments",
    )(in_hbm(charges), in_hbm(basis), in_hbm(child), in_hbm(parent))


OPS_BLOCK = 128


def table_kernel(count, ops, transfer, couple, table, chain, turned):
    rank = ops.shape[1]
    half = rank // 2
    stride = turned.shape[0] // half
    level = pl.program_id(0)
    first = pl.program_id(1) * OPS_BLOCK

    @pl.when((level == 0) & (first == 0))
    def _():
        link = couple[...]
        chain[0] = link
        for j in range(1, chain.shape[0]):
            link = mm(mm(transfer[...], link, precision=highest), transfer[...], NT, precision=highest)
            chain[j] = link

    for k in range(half):
        both = jnp.concatenate([ops[0, k], ops[0, k + half]], axis=0).astype(f32)
        turned[k * stride : k * stride + OPS_BLOCK, :] = both.T

    def rows_of(start, stop):
        for o in range(start, stop):
            rows = turned[pl.ds(o, half, stride=stride), :]
            table[0, o] = jnp.concatenate([rows[:, :rank], rows[:, rank:]], axis=0).astype(bf16)

    rows_of(0, count % OPS_BLOCK)

    @pl.when(first + OPS_BLOCK <= count)
    def _():
        rows_of(count % OPS_BLOCK, OPS_BLOCK)


def table_call(ops, transfer, couple, links):
    levels, count, rank, _ = ops.shape
    return pl.pallas_call(
        functools.partial(table_kernel, count),
        grid=(levels, pl.cdiv(count, OPS_BLOCK)),
        in_specs=[pl.BlockSpec((1, rank, rank, OPS_BLOCK), lambda t, i: (t, 0, 0, i)), VMEM, VMEM],
        out_specs=[pl.BlockSpec((1, OPS_BLOCK, rank, rank), lambda t, i: (t, i, 0, 0)), VMEM],
        out_shape=[
            pltpu.HBM((levels, count, rank, rank), bf16),
            jax.ShapeDtypeStruct((links, rank, rank), f32),
        ],
        scratch_shapes=[pltpu.VMEM((rank // 2 * (OPS_BLOCK + 8), 2 * rank), f32)],
        compiler_params=pltpu.CompilerParams(
            dimension_semantics=("arbitrary", "arbitrary"), vmem_limit_bytes=16 * 1024 * 1024
        ),
        name="operator_table",
    )(in_hbm(jnp.transpose(ops, (0, 2, 3, 1))), transfer, couple)


NEAR_LEAVES = 8


def near_kernel(base, near, left, own, right, blocks, far, out, sources, block_buf, out_buf, halo_sems, in_sems, out_sems):
    leaves = own.shape[0]
    count = blocks.shape[1]
    chunks = leaves // NEAR_LEAVES

    def fetch(c):
        rows = pl.ds(c * NEAR_LEAVES, NEAR_LEAVES)
        return pltpu.make_async_copy(blocks.at[rows], block_buf.at[rows], in_sems.at[c])

    def store(c):
        rows = pl.ds(c * NEAR_LEAVES, NEAR_LEAVES)
        return pltpu.make_async_copy(out_buf.at[rows], out.at[rows], out_sems.at[c])

    halo = [
        pltpu.make_async_copy(ref, sources.at[pl.ds(i * leaves, leaves)], halo_sems.at[i])
        for i, ref in enumerate((left, own, right))
    ]
    for copy in halo:
        copy.start()
    for c in range(chunks):
        fetch(c).start()
    for copy in halo:
        copy.wait()

    def one_chunk(c, _):
        fetch(c).wait()
        results = []
        for i in range(NEAR_LEAVES):
            row = c * NEAR_LEAVES + i
            acc = far[row]
            for n in range(0, count, 2):
                lhs = jnp.concatenate(
                    [sources[near[n, row] - base[0]], sources[near[n + 1, row] - base[0]]], axis=1
                )
                rhs = jnp.concatenate([block_buf[row, n], block_buf[row, n + 1]], axis=1)
                acc = acc + mm(lhs, rhs, NT)
            results.append(acc)
        for i, acc in enumerate(results):
            out_buf[c * NEAR_LEAVES + i] = acc
        store(c).start()
        return 0

    lax.fori_loop(0, chunks, one_chunk, 0)
    for c in range(chunks):
        store(c).wait()


def near_call(base, near_rows, left, own, right, blocks, far):
    leaves, columns, points = own.shape
    chunks = leaves // NEAR_LEAVES
    return pl.pallas_call(
        near_kernel,
        in_specs=[SMEM, SMEM, HBM, HBM, HBM, HBM, VMEM],
        out_specs=HBM,
        scratch_shapes=[
            pltpu.VMEM((3 * leaves, columns, points), bf16),
            pltpu.VMEM(blocks.shape, bf16),
            pltpu.VMEM((leaves, columns, points), f32),
            pltpu.SemaphoreType.DMA((3,)),
            pltpu.SemaphoreType.DMA((chunks,)),
            pltpu.SemaphoreType.DMA((chunks,)),
        ],
        out_shape=jax.ShapeDtypeStruct((leaves, columns, points), f32),
        compiler_params=pltpu.CompilerParams(vmem_limit_bytes=24 * 1024 * 1024),
        name="near",
    )(base, near_rows, in_hbm(left), in_hbm(own), in_hbm(right), in_hbm(blocks), far)


def doubled(pair, low):
    rank = pair.shape[1] // 2
    swapped = jnp.concatenate([pair[:, rank:], pair[:, :rank]], axis=1)
    return jnp.where(low, pair, swapped), jnp.where(low, swapped, pair)


def translated(acc, sources, table, lists, ops, base, at, low):
    for e in range(0, len(at), 4):
        picked = [sources[lists[at[e + i]] - base] for i in range(4)]
        lhs = jnp.concatenate(
            [jnp.where(low, picked[0], picked[1]), jnp.where(low, picked[2], picked[3])], axis=1
        )
        rhs = jnp.concatenate([table[ops[at[e + i]]] for i in range(4)], axis=0)
        acc = acc + mm(lhs, rhs)
    return acc


def far_kernel(
    base, list0, op0, list1, op1,
    left, own, right, table, chain, parent, child, basis, *rest,
):
    siblings = rest[:-8]
    out, halo, leaf_sources, parent_sources, parent_locals, leaf_table, parent_table, sems = rest[-8:]
    leaves = basis.shape[0]
    parents = parent.shape[0]
    columns = own.shape[1]
    rank = own.shape[2] // 2
    low = lax.broadcasted_iota(jnp.int32, (columns, 2 * rank), 1) < rank
    copies = [
        pltpu.make_async_copy(source, target, sems.at[i])
        for i, (source, target) in enumerate(
            [
                (own, halo.at[1]),
                (left, halo.at[0]),
                (right, halo.at[2]),
                (table.at[1], parent_table),
                (table.at[0], leaf_table),
            ]
        )
    ]
    for copy in copies:
        copy.start()
    field = mm(siblings[0][...], chain[0], precision=highest)
    for j in range(1, len(siblings)):
        field = field + mm(siblings[j][...], chain[j], precision=highest)
    box_local = field.astype(bf16)
    for copy, i in zip(copies, (1, 0, 2)):
        copy.wait()
        for n in range(leaves // 2):
            a, b = doubled(halo[i, n], low)
            leaf_sources[i * leaves + 2 * n] = a
            leaf_sources[i * leaves + 2 * n + 1] = b
        for n in range(parents // 2):
            a, b = doubled(halo[i, leaves // 2 + n], low)
            parent_sources[i * parents + 2 * n] = a
            parent_sources[i * parents + 2 * n + 1] = b
    copies[3].wait()
    accs = [
        translated(
            mm(box_local, parent[q], NT), parent_sources, parent_table, list1, op1, base[1],
            [(q, e) for e in range(list1.shape[1])], low,
        )
        for q in range(parents)
    ]
    for q, acc in enumerate(accs):
        parent_locals[q] = acc.astype(bf16)
    copies[4].wait()

    def one_parent(q, _):
        parent_local = parent_locals[q]
        accs = [
            translated(
                mm(parent_local, child[q * 8 + c], NT), leaf_sources, leaf_table, list0, op0, base[0],
                [(e, q * 8 + c) for e in range(list0.shape[0])], low,
            )
            for c in range(8)
        ]
        results = [mm(acc.astype(bf16), basis[q * 8 + c]) for c, acc in enumerate(accs)]
        for c, acc in enumerate(results):
            out[q * 8 + c] = acc
        return 0

    lax.fori_loop(0, parents, one_parent, 0)


def far_call(base, list0, op0, list1, op1, left, own, right, table, siblings, chain, parent, child, basis):
    leaves, rank, points = basis.shape
    parents = parent.shape[0]
    columns = own.shape[1]
    return pl.pallas_call(
        far_kernel,
        in_specs=[SMEM] * 5 + [HBM] * 4 + [VMEM] * (4 + len(siblings)),
        out_specs=VMEM,
        scratch_shapes=[
            pltpu.VMEM((3,) + own.shape, bf16),
            pltpu.VMEM((3 * leaves, columns, 2 * rank), bf16),
            pltpu.VMEM((3 * parents, columns, 2 * rank), bf16),
            pltpu.VMEM((parents, columns, rank), bf16),
            pltpu.VMEM(table.shape[1:], bf16),
            pltpu.VMEM(table.shape[1:], bf16),
            pltpu.SemaphoreType.DMA((5,)),
        ],
        out_shape=jax.ShapeDtypeStruct((leaves, columns, points), f32),
        compiler_params=pltpu.CompilerParams(vmem_limit_bytes=32 * 1024 * 1024),
        name="far",
    )(base, list0, op0, list1, op1, in_hbm(left), in_hbm(own), in_hbm(right), in_hbm(table), chain, parent, child, basis, *siblings)


def to_right(block):
    count = lax.axis_size(AXES)
    return lax.ppermute(block, AXES, [(i, i + 1) for i in range(count - 1)])


def to_left(block):
    count = lax.axis_size(AXES)
    return lax.ppermute(block, AXES, [(i + 1, i) for i in range(count - 1)])


def from_partner(block, apart):
    count = lax.axis_size(AXES)
    return lax.ppermute(block, AXES, [(i, i ^ (1 << apart)) for i in range(count)])


def after(x, *arrived):
    for y in arrived:
        x = x + jnp.minimum(jnp.abs(y[0, 0, 0].astype(f32)), 0.0)
    return x


def local(
    charges, near_blocks, near_list, leaf_basis, child_transfer, parent_transfer, m2l_ops,
    far_list0, far_op0, far_list1, far_op1, top_transfer, top_couple,
):
    leaves = charges.shape[0]
    parents = parent_transfer.shape[0]
    device = lax.axis_index(AXES)
    base = jnp.stack([(device - 1) * leaves, (device - 1) * parents]).astype(jnp.int32)
    height = lax.axis_size(AXES).bit_length() - 1
    tie = lax.optimization_barrier
    charges_left = to_right(charges)
    send, total = moments_call(charges, leaf_basis, child_transfer, parent_transfer)
    siblings = []
    for level in range(height):
        if level == 1:
            total, ops = tie((total, m2l_ops))
            table, chain = table_call(ops, top_transfer, top_couple, height)
        if level == 2:
            total, send = tie((after(total, charges_left), send))
            moments_left = to_right(send)
            moments_right = to_left(send)
        if level == height - 1:
            total, charges = tie((after(total, moments_left, moments_right), charges))
            charges_right = to_left(charges)
        partner = from_partner(total, level)
        if level == 1:
            partner, chain = tie((partner, chain))
        siblings.append(partner)
        total = total + partner
    far = far_call(
        base, far_list0.T, far_op0.T, far_list1, far_op1,
        moments_left, send, moments_right, table, siblings,
        chain, parent_transfer, child_transfer, leaf_basis,
    )
    return near_call(base, near_list.T, charges_left, charges, charges_right, near_blocks, far)


def solution(mesh):
    split = P(AXES)
    placed = (split,) * 6 + (P(),) + (split,) * 4 + (P(), P())
    return jax.shard_map(local, mesh=mesh, in_specs=placed, out_specs=split, check_vma=False)
```

time: 88.2 us -> 89.2 us (1.011)
  starting transfers between devices: 30.3 us -> 21.5 us
  Pallas kernels: 32.9 us -> 40.6 us
  matrix products: 3.67 us -> 0 us
  local copies, waits for them, and re-layouts: 0.06 us -> 3.26 us
  between operations: 0.28 us -> 2.15 us
    ppermute x5, starting transfers between devices: 24.4 us -> 13.3 us  [from_partner(): lax.ppermute(block, AXES, [(i, i ^ 1 << apart) for i in range(count)])]
    pallas_call x3, Pallas kernels: 28.7 us -> 35.5 us  [the longest x1 12.5 us: far_call(): pl.pallas_call(far_kernel, in_specs=[SMEM] * 5 + [HBM] * 4 + [VMEM] * (4...]
    dot_general x4 -> x0, matrix products: 3.67 us -> none  [mm(): lax.dot_general(a, b, dims, precision=precision, preferred_element_type=f32)]
    ppermute x2, starting transfers between devices: 3.33 us -> 5.64 us  [to_right(): return lax.ppermute(block, AXES, [(i, i + 1) for i in range(count - 1)])]
    slice x0 -> x3, local copies, waits for them, and re-layouts: none -> 1.7 us  [after(): x = x + jnp.minimum(jnp.abs(y[0, 0, 0].astype(f32)), 0.0)]
    unnamed x22 -> x28, local copies, waits for them, and re-layouts: 0.06 us -> 1.56 us
  transfers between devices with their start and end apart: 9 -> 9, of which waited for: 2 -> 3; matrix products, arithmetic and copies ran while one was open for 4% -> 1% of each run, Pallas kernels for 20% -> 33%
where the time goes in v4:
time: 89.2 us; the launch traced here: 88.6 us
  Pallas kernels  40.6 us (46%)
  starting transfers between devices  21.5 us (24%)
  waiting for transfers between devices  21 us (24%)
  local copies, waits for them, and re-layouts  3.26 us (4%)
  between operations  2.15 us (2%)
    ppermute x5, waiting for transfers between devices, from_partner(): lax.ppermute(block, AXES, [(i, i ^ 1 << apart) for i in range(count)])  21 us
    ppermute x5, starting transfers between devices, from_partner(): lax.ppermute(block, AXES, [(i, i ^ 1 << apart) for i in range(count)])  13.3 us
    pallas_call x1, Pallas kernels, far_call(): pl.pallas_call(far_kernel, in_specs=[SMEM] * 5 + [HBM] * 4 + [VMEM] * (4...  12.5 us
    pallas_call x1, Pallas kernels, near_call(): pl.pallas_call(near_kernel, in_specs=[SMEM, SMEM, HBM, HBM, HBM, HBM, VME...  11.8 us
    pallas_call x1, Pallas kernels, table_call(): pl.pallas_call(functools.partial(table_kernel, count), grid=(levels, pl.c...  11.2 us
    ppermute x2, starting transfers between devices, to_right(): return lax.ppermute(block, AXES, [(i, i + 1) for i in range(count - 1)])  5.64 us
    pallas_call x1, Pallas kernels, moments_call(): pl.pallas_call(moments_kernel, grid=(steps,), in_specs=[pl.BlockSpec((16,...  5.08 us
    ppermute x2, starting transfers between devices, to_left(): return lax.ppermute(block, AXES, [(i + 1, i) for i in range(count - 1)])  2.58 us
  transfers between devices with their start and end apart: 9, of which 3 were waited for; matrix products, arithmetic and copies ran while one was open for 1% of the time, Pallas kernels for 33%

profile of v4, /device:TPU:0, one launch (start us, length us, event | category | flops | bytes accessed | tf_op | source)
XLA Modules:
  0.0 88.6 jit_solution(3530101847403953279)
XLA Ops:
  0.0 2.6 %collective-permute-start = (bf16[64,64,128]{2,1,0:T(8,128)(2,1)}, bf16[64,64,128]{2,1,0:T(8,128)(2,1)S(1)}, u32[]{:S(2)}, u32[]{:S(2)}) collective-permute-start(bf16[64,64,128]{2,1,0:T(8,128)(2,1)} %own), channel_id=1, source_target_pairs={{0,1},{1,2},{2,3},{3,4},{4,5},{5,6},{6,7},{7,8},{8,9},{9,10},{10,1... | collective-permute-start | bytes 3145736 | tf_op jit(solution)/shard_map/ppermute | solution.py:331
  2.6 5.1 %moments.1 = (bf16[36,64,128]{2,1,0:T(8,128)(2,1)}, f32[64,64]{1,0:T(8,128)S(1)}) custom-call(bf16[64,64,128]{2,1,0:T(8,128)(2,1)} %own, bf16[64,64,128]{2,1,0:T(8,128)(2,1)} %basis.3, bf16[64,64,64]{2,1,0:T(8,128)(2,1)} %child.3, bf16[8,64,64]{2,1,0:T(8,128)(2,1)} %parent.3), custom_call_target="tpu_custom_call" | custom-call | tf_op jit(solution)/shard_map/moments/pallas_call | solution.py:75
  7.7 2.6 %collective-permute-start.1 = (f32[64,64]{1,0:T(8,128)S(1)}, f32[64,64]{1,0:T(8,128)S(1)}, u32[]{:S(2)}, u32[]{:S(2)}) collective-permute-start(f32[64,64]{1,0:T(8,128)S(1)} %get-tuple-element.17), channel_id=1, source_target_pairs={{0,1},{1,0},{2,3},{3,2},{4,5},{5,4},{6,7},{7,6},{8,9},{9,8},{10,11... | collective-permute-start | bytes 49160 | tf_op jit(solution)/shard_map/ppermute | solution.py:341
  10.3 0.9 collective-permute-done.1.rest_0_
  11.1 1.4 %collective-permute-start.2 = (f32[64,64]{1,0:T(8,128)S(1)}, f32[64,64]{1,0:T(8,128)S(1)}, u32[]{:S(2)}, u32[]{:S(2)}) collective-permute-start(f32[64,64]{1,0:T(8,128)S(1)} %add.35), channel_id=1, source_target_pairs={{0,2},{1,3},{2,0},{3,1},{4,6},{5,7},{6,4},{7,5},{8,10},{9,11},{10,... | collective-permute-start | bytes 49160 | tf_op jit(solution)/shard_map/ppermute | solution.py:341
  12.6 0.8 copy-done.3
  13.3 0.8 copy-done.4
  14.1 11.2 %operator_table.1 = (bf16[2,316,64,64]{3,2,1,0:T(8,128)(2,1)}, f32[5,64,64]{2,1,0:T(8,128)S(1)}) custom-call(bf16[2,64,64,316]{3,2,1,0:T(8,128)(2,1)} %bitcast.12, f32[64,64]{1,0:T(8,128)S(1)} %copy-done.3, f32[64,64]{1,0:T(8,128)S(1)} %copy-done.4), custom_call_target="tpu_custom_call" | custom-call | tf_op jit(solution)/shard_map/operator_table/pallas_call | solution.py:133
  25.3 0.0 collective-permute-done.left
  25.3 0.6 slice.12
  26.6 1.3 %collective-permute-start.6 = (bf16[36,64,128]{2,1,0:T(8,128)(2,1)S(1)}, bf16[36,64,128]{2,1,0:T(8,128)(2,1)S(1)}, u32[]{:S(2)}, u32[]{:S(2)}) collective-permute-start(bf16[36,64,128]{2,1,0:T(8,128)(2,1)S(1)} %copy-done.11), channel_id=1, source_target_pairs={{1,0},{2,1},{3,2},{4,3},{5,4},{6,5},{7,6},{8,7},{9,8},{10,9},{11,1... | collective-permute-start | bytes 1769480 | tf_op jit(solution)/shard_map/ppermute | solution.py:336
  27.9 3.1 %collective-permute-start.5 = (bf16[36,64,128]{2,1,0:T(8,128)(2,1)S(1)}, bf16[36,64,128]{2,1,0:T(8,128)(2,1)S(1)}, u32[]{:S(2)}, u32[]{:S(2)}) collective-permute-start(bf16[36,64,128]{2,1,0:T(8,128)(2,1)S(1)} %copy-done.11), channel_id=1, source_target_pairs={{0,1},{1,2},{2,3},{3,4},{4,5},{5,6},{6,7},{7,8},{8,9},{9,10},{10,1... | collective-permute-start | bytes 1769480 | tf_op jit(solution)/shard_map/ppermute | solution.py:331
  30.9 1.6 %collective-permute-start.3 = (f32[64,64]{1,0:T(8,128)S(1)}, f32[64,64]{1,0:T(8,128)S(1)}, u32[]{:S(2)}, u32[]{:S(2)}) collective-permute-start(f32[64,64]{1,0:T(8,128)S(1)} %add_add_fusion.1), channel_id=1, source_target_pairs={{0,4},{1,5},{2,6},{3,7},{4,0},{5,1},{6,2},{7,3},{8,12},{9,13},{10,... | collective-permute-start | bytes 49160 | tf_op jit(solution)/shard_map/ppermute | solution.py:341
  32.5 6.2 %collective-permute-done.3.rest_2_ = f32[64,64]{1,0:T(8,128)S(1)} collective-permute-done((f32[64,64]{1,0:T(8,128)S(1)}, f32[64,64]{1,0:T(8,128)S(1)}, u32[]{:S(2)}, u32[]{:S(2)}) %collective-permute-start.3) | collective-permute-done | bytes 16416 | tf_op jit(solution)/shard_map/ppermute | solution.py:341
  38.7 1.6 %collective-permute-start.4 = (f32[64,64]{1,0:T(8,128)S(1)}, f32[64,64]{1,0:T(8,128)S(1)}, u32[]{:S(2)}, u32[]{:S(2)}) collective-permute-start(f32[64,64]{1,0:T(8,128)S(1)} %add.39), channel_id=1, source_target_pairs={{0,8},{1,9},{2,10},{3,11},{4,12},{5,13},{6,14},{7,15},{8,0},{9,1},... | collective-permute-start | bytes 49160 | tf_op jit(solution)/shard_map/ppermute | solution.py:341
  40.3 0.5 slice.14
  41.5 0.6 slice.13
  42.8 1.3 %collective-permute-start.7 = (bf16[64,64,128]{2,1,0:T(8,128)(2,1)}, bf16[64,64,128]{2,1,0:T(8,128)(2,1)}, u32[]{:S(2)}, u32[]{:S(2)}) collective-permute-start(bf16[64,64,128]{2,1,0:T(8,128)(2,1)} %own), channel_id=1, source_target_pairs={{1,0},{2,1},{3,2},{4,3},{5,4},{6,5},{7,6},{8,7},{9,8},{10,9},{11,1... | collective-permute-start | bytes 3145736 | tf_op jit(solution)/shard_map/ppermute | solution.py:336
  44.1 6.1 %collective-permute-start.8 = (f32[64,64]{1,0:T(8,128)S(1)}, f32[64,64]{1,0:T(8,128)S(1)}, u32[]{:S(2)}, u32[]{:S(2)}) collective-permute-start(f32[64,64]{1,0:T(8,128)S(1)} %add_add_fusion), channel_id=1, source_target_pairs={{0,16},{1,17},{2,18},{3,19},{4,20},{5,21},{6,22},{7,23},{8,24},{9,... | collective-permute-start | bytes 49160 | tf_op jit(solution)/shard_map/ppermute | solution.py:341
  50.3 0.1 pad_add_fusion.base
  50.4 13.9 %collective-permute-done.8.rest_4_ = f32[64,64]{1,0:T(8,128)S(1)} collective-permute-done((f32[64,64]{1,0:T(8,128)S(1)}, f32[64,64]{1,0:T(8,128)S(1)}, u32[]{:S(2)}, u32[]{:S(2)}) %collective-permute-start.8) | collective-permute-done | bytes 16416 | tf_op jit(solution)/shard_map/ppermute | solution.py:341
  64.3 0.0 copy-start.9
  64.3 12.5 %far.1 = f32[64,64,128]{2,1,0:T(8,128)S(1)} custom-call(s32[2]{0:T(128)S(1)} %pad_add_fusion.base, s32[24,64]{1,0:T(8,128)S(1)} %bitcast.9, s32[24,64]{1,0:T(8,128)S(1)} %bitcast.10, s32[8,24]{1,0:T(8,128)S(1)} %copy-done.7, s32[8,24]{1,0:T(8,128)S(1)} %copy-done.8, bf16[36,64,128]{2,1,0:T(8,128)(2,1)} %copy-done.13, ...), custom_call_target="tpu_custom_call" | custom-call | tf_op jit(solution)/shard_map/far/pallas_call | solution.py:310
  76.8 11.8 %near.1 = f32[64,64,128]{2,1,0:T(8,128)} custom-call(s32[2]{0:T(128)S(1)} %pad_add_fusion.base, s32[6,64]{1,0:T(8,128)S(1)} %bitcast.11, bf16[64,64,128]{2,1,0:T(8,128)(2,1)} %copy-done.10, bf16[64,64,128]{2,1,0:T(8,128)(2,1)} %own, bf16[64,64,128]{2,1,0:T(8,128)(2,1)} %collective-permute-done.7.right, bf16[64,6,128,128]{3,2,1,0:T(8,128)(2,1)} %blocks.1, ...), custom_call_target="tpu_custom_call" | custom-call | tf_op jit(solution)/shard_map/near/pallas_call | solution.py:203
  (34 shorter events, 0.1 us)
Async XLA Ops:
  0.0 64.2 %copy-start.2 = (bf16[8,64,64]{2,1,0:T(8,128)(2,1)S(1)}, bf16[8,64,64]{2,1,0:T(8,128)(2,1)}, u32[]{:S(2)}) copy-start(bf16[8,64,64]{2,1,0:T(8,128)(2,1)} %parent.3) | copy-start | bytes 196612
  0.0 64.2 %copy-start.1 = (bf16[64,64,64]{2,1,0:T(8,128)(2,1)S(1)}, bf16[64,64,64]{2,1,0:T(8,128)(2,1)}, u32[]{:S(2)}) copy-start(bf16[64,64,64]{2,1,0:T(8,128)(2,1)} %child.3) | copy-start | bytes 1572868
  0.0 64.2 %copy-start = (bf16[64,64,128]{2,1,0:T(8,128)(2,1)S(1)}, bf16[64,64,128]{2,1,0:T(8,128)(2,1)}, u32[]{:S(2)}) copy-start(bf16[64,64,128]{2,1,0:T(8,128)(2,1)} %basis.3) | copy-start | bytes 3145732
  0.0 64.2 %copy-start.8 = (s32[8,24]{1,0:T(8,128)S(1)}, s32[8,24]{1,0:T(8,128)}, u32[]{:S(2)}) copy-start(s32[8,24]{1,0:T(8,128)} %op1.1) | copy-start | bytes 2308
  0.0 64.2 %copy-start.7 = (s32[8,24]{1,0:T(8,128)S(1)}, s32[8,24]{1,0:T(8,128)}, u32[]{:S(2)}) copy-start(s32[8,24]{1,0:T(8,128)} %list1.1) | copy-start | bytes 2308
  0.0 64.2 %copy-start.6 = (s32[64,24]{0,1:T(8,128)S(1)}, s32[64,24]{0,1:T(8,128)}, u32[]{:S(2)}) copy-start(s32[64,24]{0,1:T(8,128)} %param.21) | copy-start | bytes 18436
  0.0 64.2 %copy-start.5 = (s32[64,24]{0,1:T(8,128)S(1)}, s32[64,24]{0,1:T(8,128)}, u32[]{:S(2)}) copy-start(s32[64,24]{0,1:T(8,128)} %param.20) | copy-start | bytes 18436
  0.0 25.3 %collective-permute-start = (bf16[64,64,128]{2,1,0:T(8,128)(2,1)}, bf16[64,64,128]{2,1,0:T(8,128)(2,1)S(1)}, u32[]{:S(2)}, u32[]{:S(2)}) collective-permute-start(bf16[64,64,128]{2,1,0:T(8,128)(2,1)} %own), channel_id=1, source_target_pairs={{0,1},{1,2},{2,3},{3,4},{4,5},{5,6},{6,7},{7,8},{8,9},{9,10},{10,1... | collective-permute-start | bytes 3145736 | tf_op jit(solution)/shard_map/ppermute | solution.py:331
  7.7 3.4 %collective-permute-start.1 = (f32[64,64]{1,0:T(8,128)S(1)}, f32[64,64]{1,0:T(8,128)S(1)}, u32[]{:S(2)}, u32[]{:S(2)}) collective-permute-start(f32[64,64]{1,0:T(8,128)S(1)} %get-tuple-element.17), channel_id=1, source_target_pairs={{0,1},{1,0},{2,3},{3,2},{4,5},{5,4},{6,7},{7,6},{8,9},{9,8},{10,11... | collective-permute-start | bytes 49160 | tf_op jit(solution)/shard_map/ppermute | solution.py:341
  11.1 14.2 %collective-permute-start.2 = (f32[64,64]{1,0:T(8,128)S(1)}, f32[64,64]{1,0:T(8,128)S(1)}, u32[]{:S(2)}, u32[]{:S(2)}) collective-permute-start(f32[64,64]{1,0:T(8,128)S(1)} %add.35), channel_id=1, source_target_pairs={{0,2},{1,3},{2,0},{3,1},{4,6},{5,7},{6,4},{7,5},{8,10},{9,11},{10,... | collective-permute-start | bytes 49160 | tf_op jit(solution)/shard_map/ppermute | solution.py:341
  12.6 0.8 copy-start.3
  13.3 0.8 copy-start.4
  14.1 12.5 %copy-start.11 = (bf16[36,64,128]{2,1,0:T(8,128)(2,1)S(1)}, bf16[36,64,128]{2,1,0:T(8,128)(2,1)}, u32[]{:S(2)}) copy-start(bf16[36,64,128]{2,1,0:T(8,128)(2,1)} %get-tuple-element.24.own) | copy-start | bytes 1769476
  25.3 17.5 %copy-start.10 = (bf16[64,64,128]{2,1,0:T(8,128)(2,1)}, bf16[64,64,128]{2,1,0:T(8,128)(2,1)S(1)}, u32[]{:S(2)}) copy-start(bf16[64,64,128]{2,1,0:T(8,128)(2,1)S(1)} %collective-permute-done.left) | copy-start | bytes 3145732
  26.6 13.8 %collective-permute-start.6 = (bf16[36,64,128]{2,1,0:T(8,128)(2,1)S(1)}, bf16[36,64,128]{2,1,0:T(8,128)(2,1)S(1)}, u32[]{:S(2)}, u32[]{:S(2)}) collective-permute-start(bf16[36,64,128]{2,1,0:T(8,128)(2,1)S(1)} %copy-done.11), channel_id=1, source_target_pairs={{1,0},{2,1},{3,2},{4,3},{5,4},{6,5},{7,6},{8,7},{9,8},{10,9},{11,1... | collective-permute-start | bytes 1769480 | tf_op jit(solution)/shard_map/ppermute | solution.py:336
  27.9 13.7 %collective-permute-start.5 = (bf16[36,64,128]{2,1,0:T(8,128)(2,1)S(1)}, bf16[36,64,128]{2,1,0:T(8,128)(2,1)S(1)}, u32[]{:S(2)}, u32[]{:S(2)}) collective-permute-start(bf16[36,64,128]{2,1,0:T(8,128)(2,1)S(1)} %copy-done.11), channel_id=1, source_target_pairs={{0,1},{1,2},{2,3},{3,4},{4,5},{5,6},{6,7},{7,8},{8,9},{9,10},{10,1... | collective-permute-start | bytes 1769480 | tf_op jit(solution)/shard_map/ppermute | solution.py:331
  30.9 7.8 %collective-permute-start.3 = (f32[64,64]{1,0:T(8,128)S(1)}, f32[64,64]{1,0:T(8,128)S(1)}, u32[]{:S(2)}, u32[]{:S(2)}) collective-permute-start(f32[64,64]{1,0:T(8,128)S(1)} %add_add_fusion.1), channel_id=1, source_target_pairs={{0,4},{1,5},{2,6},{3,7},{4,0},{5,1},{6,2},{7,3},{8,12},{9,13},{10,... | collective-permute-start | bytes 49160 | tf_op jit(solution)/shard_map/ppermute | solution.py:341
  38.7 4.0 %collective-permute-start.4 = (f32[64,64]{1,0:T(8,128)S(1)}, f32[64,64]{1,0:T(8,128)S(1)}, u32[]{:S(2)}, u32[]{:S(2)}) collective-permute-start(f32[64,64]{1,0:T(8,128)S(1)} %add.39), channel_id=1, source_target_pairs={{0,8},{1,9},{2,10},{3,11},{4,12},{5,13},{6,14},{7,15},{8,0},{9,1},... | collective-permute-start | bytes 49160 | tf_op jit(solution)/shard_map/ppermute | solution.py:341
  40.3 2.5 %copy-start.12 = (bf16[36,64,128]{2,1,0:T(8,128)(2,1)}, bf16[36,64,128]{2,1,0:T(8,128)(2,1)S(1)}, u32[]{:S(2)}) copy-start(bf16[36,64,128]{2,1,0:T(8,128)(2,1)S(1)} %collective-permute-done.6.right) | copy-start | bytes 1769476
  41.5 1.3 %copy-start.13 = (bf16[36,64,128]{2,1,0:T(8,128)(2,1)}, bf16[36,64,128]{2,1,0:T(8,128)(2,1)S(1)}, u32[]{:S(2)}) copy-start(bf16[36,64,128]{2,1,0:T(8,128)(2,1)S(1)} %collective-permute-done.5.left) | copy-start | bytes 1769476
  42.8 34.0 %collective-permute-start.7 = (bf16[64,64,128]{2,1,0:T(8,128)(2,1)}, bf16[64,64,128]{2,1,0:T(8,128)(2,1)}, u32[]{:S(2)}, u32[]{:S(2)}) collective-permute-start(bf16[64,64,128]{2,1,0:T(8,128)(2,1)} %own), channel_id=1, source_target_pairs={{1,0},{2,1},{3,2},{4,3},{5,4},{6,5},{7,6},{8,7},{9,8},{10,9},{11,1... | collective-permute-start | bytes 3145736 | tf_op jit(solution)/shard_map/ppermute | solution.py:336
  44.1 20.1 %collective-permute-start.8 = (f32[64,64]{1,0:T(8,128)S(1)}, f32[64,64]{1,0:T(8,128)S(1)}, u32[]{:S(2)}, u32[]{:S(2)}) collective-permute-start(f32[64,64]{1,0:T(8,128)S(1)} %add_add_fusion), channel_id=1, source_target_pairs={{0,16},{1,17},{2,18},{3,19},{4,20},{5,21},{6,22},{7,23},{8,24},{9,... | collective-permute-start | bytes 49160 | tf_op jit(solution)/shard_map/ppermute | solution.py:341
  64.3 12.5 %copy-start.9 = (s32[64,6]{0,1:T(8,128)S(1)}, s32[64,6]{0,1:T(8,128)}, u32[]{:S(2)}) copy-start(s32[64,6]{0,1:T(8,128)} %param.15) | copy-start | bytes 4612

commit v5 on v4

--- a/solution.py
+++ b/solution.py
@@ -97,15 +97,19 @@
 OPS_BLOCK = 128
 
 
-def table_kernel(count, ops, transfer, couple, table, chain, turned):
+def table_kernel(count, ops, *refs):
+    *top, table, chain, turned = refs
     rank = ops.shape[1]
     half = rank // 2
     stride = turned.shape[0] // half
-    level = pl.program_id(0)
-    first = pl.program_id(1) * OPS_BLOCK
-
-    @pl.when((level == 0) & (first == 0))
+    first = pl.program_id(0) * OPS_BLOCK
+
+    @pl.when(first == 0)
     def _():
+        if not top:
+            chain[...] = jnp.zeros_like(chain)
+            return
+        transfer, couple = top
         link = couple[...]
         chain[0] = link
         for j in range(1, chain.shape[0]):
@@ -119,7 +123,7 @@
     def rows_of(start, stop):
         for o in range(start, stop):
             rows = turned[pl.ds(o, half, stride=stride), :]
-            table[0, o] = jnp.concatenate([rows[:, :rank], rows[:, rank:]], axis=0).astype(bf16)
+            table[o] = jnp.concatenate([rows[:, :rank], rows[:, rank:]], axis=0).astype(bf16)
 
     rows_of(0, count % OPS_BLOCK)
 
@@ -128,37 +132,32 @@
         rows_of(count % OPS_BLOCK, OPS_BLOCK)
 
 
-def table_call(ops, transfer, couple, links):
-    levels, count, rank, _ = ops.shape
+def table_call(ops, level, top, links):
+    _, count, rank, _ = ops.shape
     return pl.pallas_call(
         functools.partial(table_kernel, count),
-        grid=(levels, pl.cdiv(count, OPS_BLOCK)),
-        in_specs=[pl.BlockSpec((1, rank, rank, OPS_BLOCK), lambda t, i: (t, 0, 0, i)), VMEM, VMEM],
-        out_specs=[pl.BlockSpec((1, OPS_BLOCK, rank, rank), lambda t, i: (t, i, 0, 0)), VMEM],
+        grid=(pl.cdiv(count, OPS_BLOCK),),
+        in_specs=[pl.BlockSpec((1, rank, rank, OPS_BLOCK), lambda i: (level, 0, 0, i))]
+        + [VMEM for _ in top],
+        out_specs=[pl.BlockSpec((OPS_BLOCK, rank, rank), lambda i: (i, 0, 0)), VMEM],
         out_shape=[
-            pltpu.HBM((levels, count, rank, rank), bf16),
+            pltpu.HBM((count, rank, rank), bf16),
             jax.ShapeDtypeStruct((links, rank, rank), f32),
         ],
         scratch_shapes=[pltpu.VMEM((rank // 2 * (OPS_BLOCK + 8), 2 * rank), f32)],
-        compiler_params=pltpu.CompilerParams(
-            dimension_semantics=("arbitrary", "arbitrary"), vmem_limit_bytes=16 * 1024 * 1024
-        ),
+        compiler_params=params(16),
         name="operator_table",
-    )(in_hbm(jnp.transpose(ops, (0, 2, 3, 1))), transfer, couple)
+    )(in_hbm(jnp.transpose(ops, (0, 2, 3, 1))), *top)
 
 
 NEAR_LEAVES = 8
 
 
-def near_kernel(base, near, left, own, right, blocks, far, out, sources, block_buf, out_buf, halo_sems, in_sems, out_sems):
+def near_kernel(base, near, left, own, right, blocks, far, out, sources, out_buf, halo_sems, out_sems):
     leaves = own.shape[0]
     count = blocks.shape[1]
     chunks = leaves // NEAR_LEAVES
 
-    def fetch(c):
-        rows = pl.ds(c * NEAR_LEAVES, NEAR_LEAVES)
-        return pltpu.make_async_copy(blocks.at[rows], block_buf.at[rows], in_sems.at[c])
-
     def store(c):
         rows = pl.ds(c * NEAR_LEAVES, NEAR_LEAVES)
         return pltpu.make_async_copy(out_buf.at[rows], out.at[rows], out_sems.at[c])
@@ -169,13 +168,10 @@
     ]
     for copy in halo:
         copy.start()
-    for c in range(chunks):
-        fetch(c).start()
     for copy in halo:
         copy.wait()
 
     def one_chunk(c, _):
-        fetch(c).wait()
         results = []
         for i in range(NEAR_LEAVES):
             row = c * NEAR_LEAVES + i
@@ -184,7 +180,7 @@
                 lhs = jnp.concatenate(
                     [sources[near[n, row] - base[0]], sources[near[n + 1, row] - base[0]]], axis=1
                 )
-                rhs = jnp.concatenate([block_buf[row, n], block_buf[row, n + 1]], axis=1)
+                rhs = jnp.concatenate([blocks[row, n], blocks[row, n + 1]], axis=1)
                 acc = acc + mm(lhs, rhs, NT)
             results.append(acc)
         for i, acc in enumerate(results):
@@ -202,20 +198,18 @@
     chunks = leaves // NEAR_LEAVES
     return pl.pallas_call(
         near_kernel,
-        in_specs=[SMEM, SMEM, HBM, HBM, HBM, HBM, VMEM],
+        in_specs=[SMEM, SMEM, HBM, HBM, HBM, VMEM, VMEM],
         out_specs=HBM,
         scratch_shapes=[
             pltpu.VMEM((3 * leaves, columns, points), bf16),
-            pltpu.VMEM(blocks.shape, bf16),
             pltpu.VMEM((leaves, columns, points), f32),
             pltpu.SemaphoreType.DMA((3,)),
             pltpu.SemaphoreType.DMA((chunks,)),
-            pltpu.SemaphoreType.DMA((chunks,)),
         ],
         out_shape=jax.ShapeDtypeStruct((leaves, columns, points), f32),
         compiler_params=pltpu.CompilerParams(vmem_limit_bytes=24 * 1024 * 1024),
         name="near",
-    )(base, near_rows, in_hbm(left), in_hbm(own), in_hbm(right), in_hbm(blocks), far)
+    )(base, near_rows, in_hbm(left), in_hbm(own), in_hbm(right), blocks, far)
 
 
 def doubled(pair, low):
@@ -237,10 +231,10 @@
 
 def far_kernel(
     base, list0, op0, list1, op1,
-    left, own, right, table, chain, parent, child, basis, *rest,
+    left, own, right, leaf_ops, parent_ops, blocks, chain, parent, child, basis, *rest,
 ):
-    siblings = rest[:-8]
-    out, halo, leaf_sources, parent_sources, parent_locals, leaf_table, parent_table, sems = rest[-8:]
+    siblings = rest[:-9]
+    out, fetched, halo, leaf_sources, parent_sources, parent_locals, leaf_table, parent_table, sems = rest[-9:]
     leaves = basis.shape[0]
     parents = parent.shape[0]
     columns = own.shape[1]
@@ -253,8 +247,9 @@
                 (own, halo.at[1]),
                 (left, halo.at[0]),
                 (right, halo.at[2]),
-                (table.at[1], parent_table),
-                (table.at[0], leaf_table),
+                (parent_ops, parent_table),
+                (leaf_ops, leaf_table),
+                (blocks, fetched),
             ]
         )
     ]
@@ -301,29 +296,34 @@
         return 0
 
     lax.fori_loop(0, parents, one_parent, 0)
-
-
-def far_call(base, list0, op0, list1, op1, left, own, right, table, siblings, chain, parent, child, basis):
+    copies[5].wait()
+
+
+def far_call(base, list0, op0, list1, op1, left, own, right, leaf_ops, parent_ops, blocks, siblings, chain, parent, child, basis):
     leaves, rank, points = basis.shape
     parents = parent.shape[0]
     columns = own.shape[1]
     return pl.pallas_call(
         far_kernel,
-        in_specs=[SMEM] * 5 + [HBM] * 4 + [VMEM] * (4 + len(siblings)),
-        out_specs=VMEM,
+        in_specs=[SMEM] * 5 + [HBM] * 6 + [VMEM] * (4 + len(siblings)),
+        out_specs=[VMEM, VMEM],
         scratch_shapes=[
             pltpu.VMEM((3,) + own.shape, bf16),
             pltpu.VMEM((3 * leaves, columns, 2 * rank), bf16),
             pltpu.VMEM((3 * parents, columns, 2 * rank), bf16),
             pltpu.VMEM((parents, columns, rank), bf16),
-            pltpu.VMEM(table.shape[1:], bf16),
-            pltpu.VMEM(table.shape[1:], bf16),
-            pltpu.SemaphoreType.DMA((5,)),
-        ],
-        out_shape=jax.ShapeDtypeStruct((leaves, columns, points), f32),
-        compiler_params=pltpu.CompilerParams(vmem_limit_bytes=32 * 1024 * 1024),
+            pltpu.VMEM(leaf_ops.shape, bf16),
+            pltpu.VMEM(parent_ops.shape, bf16),
+            pltpu.SemaphoreType.DMA((6,)),
+        ],
+        out_shape=[jax.ShapeDtypeStruct((leaves, columns, points), f32), pltpu.VMEM(blocks.shape, bf16)],
+        compiler_params=pltpu.CompilerParams(vmem_limit_bytes=24 * 1024 * 1024),
         name="far",
-    )(base, list0, op0, list1, op1, in_hbm(left), in_hbm(own), in_hbm(right), in_hbm(table), chain, parent, child, basis, *siblings)
+    )(
+        base, list0, op0, list1, op1,
+        *[in_hbm(x) for x in (left, own, right, leaf_ops, parent_ops, blocks)],
+        chain, parent, child, basis, *siblings,
+    )
 
 
 def to_right(block):
@@ -363,25 +363,32 @@
     for level in range(height):
         if level == 1:
             total, ops = tie((total, m2l_ops))
-            table, chain = table_call(ops, top_transfer, top_couple, height)
+            leaf_ops, token = table_call(ops, 0, (), 1)
         if level == 2:
             total, send = tie((after(total, charges_left), send))
             moments_left = to_right(send)
             moments_right = to_left(send)
+        if level == 3:
+            total, ops = tie((total, m2l_ops))
+            parent_ops, chain = table_call(ops, 1, (top_transfer, top_couple), height)
         if level == height - 1:
-            total, charges = tie((after(total, moments_left, moments_right), charges))
-            charges_right = to_left(charges)
+            total = after(total, moments_left, moments_right)
         partner = from_partner(total, level)
         if level == 1:
+            partner = after(partner, token)
+        if level == 3:
             partner, chain = tie((partner, chain))
+        if level == height - 1:
+            partner, charges = tie((partner, charges))
+            charges_right = to_left(charges)
         siblings.append(partner)
         total = total + partner
-    far = far_call(
+    far, blocks = far_call(
         base, far_list0.T, far_op0.T, far_list1, far_op1,
-        moments_left, send, moments_right, table, siblings,
+        moments_left, send, moments_right, leaf_ops, parent_ops, near_blocks, siblings,
         chain, parent_transfer, child_transfer, leaf_basis,
     )
-    return near_call(base, near_list.T, charges_left, charges, charges_right, near_blocks, far)
+    return near_call(base, near_list.T, charges_left, charges, charges_right, blocks, far)
 
 
 def solution(mesh):

time: 89.2 us -> 77.1 us (0.86)
  waiting for transfers between devices: 21 us -> 12.4 us
  starting transfers between devices: 21.5 us -> 19.3 us
  Pallas kernels: 40.6 us -> 39.1 us
  local copies, waits for them, and re-layouts: 3.26 us -> 2.33 us
    ppermute x5, waiting for transfers between devices: 21 us -> 12.4 us  [from_partner(): lax.ppermute(block, AXES, [(i, i ^ 1 << apart) for i in range(count)])]
    unnamed x28, local copies, waits for them, and re-layouts: 1.56 us -> 0.06 us
    pallas_call x3 -> x4, Pallas kernels: 35.5 us -> 34.1 us  [the longest x2 12.9 us: table_call(): pl.pallas_call(functools.partial(table_kernel, count), grid=(pl.cdiv(coun...]
    ppermute x5, starting transfers between devices: 13.3 us -> 12.1 us  [from_partner(): lax.ppermute(block, AXES, [(i, i ^ 1 << apart) for i in range(count)])]
    ppermute x2, starting transfers between devices: 5.64 us -> 4.55 us  [to_right(): return lax.ppermute(block, AXES, [(i, i + 1) for i in range(count - 1)])]
    slice x3 -> x4, local copies, waits for them, and re-layouts: 1.7 us -> 2.27 us  [after(): x = x + jnp.minimum(jnp.abs(y[0, 0, 0].astype(f32)), 0.0)]
  transfers between devices with their start and end apart: 9 -> 9, of which waited for: 3 -> 3; matrix products, arithmetic and copies ran while one was open for 1% -> 2% of each run, Pallas kernels for 33% -> 40%
where the time goes in v5:
time: 77.1 us; the launch traced here: 75.9 us
  Pallas kernels  39.1 us (51%)
  starting transfers between devices  19.3 us (25%)
  waiting for transfers between devices  12.4 us (16%)
  between operations  2.7 us (4%)
  local copies, waits for them, and re-layouts  2.33 us (3%)
    pallas_call x2, Pallas kernels, table_call(): pl.pallas_call(functools.partial(table_kernel, count), grid=(pl.cdiv(coun...  12.9 us
    pallas_call x1, Pallas kernels, far_call(): pl.pallas_call(far_kernel, in_specs=[SMEM] * 5 + [HBM] * 6 + [VMEM] * (4...  12.5 us
    ppermute x5, waiting for transfers between devices, from_partner(): lax.ppermute(block, AXES, [(i, i ^ 1 << apart) for i in range(count)])  12.4 us
    ppermute x5, starting transfers between devices, from_partner(): lax.ppermute(block, AXES, [(i, i ^ 1 << apart) for i in range(count)])  12.1 us
    pallas_call x1, Pallas kernels, near_call(): pl.pallas_call(near_kernel, in_specs=[SMEM, SMEM, HBM, HBM, HBM, VMEM, VM...  8.58 us
    pallas_call x1, Pallas kernels, moments_call(): pl.pallas_call(moments_kernel, grid=(steps,), in_specs=[pl.BlockSpec((16,...  5.08 us
    ppermute x2, starting transfers between devices, to_right(): return lax.ppermute(block, AXES, [(i, i + 1) for i in range(count - 1)])  4.55 us
    ppermute x2, starting transfers between devices, to_left(): return lax.ppermute(block, AXES, [(i + 1, i) for i in range(count - 1)])  2.57 us
  transfers between devices with their start and end apart: 9, of which 3 were waited for; matrix products, arithmetic and copies ran while one was open for 2% of the time, Pallas kernels for 40%

profile of v5, /device:TPU:0, one launch (start us, length us, event | category | flops | bytes accessed | tf_op | source)
XLA Modules:
  0.0 75.9 jit_solution(9032653845066578334)
XLA Ops:
  0.0 2.5 %collective-permute-start = (bf16[64,64,128]{2,1,0:T(8,128)(2,1)}, bf16[64,64,128]{2,1,0:T(8,128)(2,1)S(1)}, u32[]{:S(2)}, u32[]{:S(2)}) collective-permute-start(bf16[64,64,128]{2,1,0:T(8,128)(2,1)} %own), channel_id=1, source_target_pairs={{0,1},{1,2},{2,3},{3,4},{4,5},{5,6},{6,7},{7,8},{8,9},{9,10},{10,1... | collective-permute-start | bytes 3145736 | tf_op jit(solution)/shard_map/ppermute | solution.py:331
  2.6 5.1 %moments.1 = (bf16[36,64,128]{2,1,0:T(8,128)(2,1)}, f32[64,64]{1,0:T(8,128)S(1)}) custom-call(bf16[64,64,128]{2,1,0:T(8,128)(2,1)} %own, bf16[64,64,128]{2,1,0:T(8,128)(2,1)} %basis.3, bf16[64,64,64]{2,1,0:T(8,128)(2,1)} %child.3, bf16[8,64,64]{2,1,0:T(8,128)(2,1)} %parent.3), custom_call_target="tpu_custom_call" | custom-call | tf_op jit(solution)/shard_map/moments/pallas_call | solution.py:75
  7.6 2.6 %collective-permute-start.1 = (f32[64,64]{1,0:T(8,128)S(1)}, f32[64,64]{1,0:T(8,128)S(1)}, u32[]{:S(2)}, u32[]{:S(2)}) collective-permute-start(f32[64,64]{1,0:T(8,128)S(1)} %get-tuple-element.23), channel_id=1, source_target_pairs={{0,1},{1,0},{2,3},{3,2},{4,5},{5,4},{6,7},{7,6},{8,9},{9,8},{10,11... | collective-permute-start | bytes 49160 | tf_op jit(solution)/shard_map/ppermute | solution.py:341
  10.2 0.9 %collective-permute-done.1.rest_0_ = f32[64,64]{1,0:T(8,128)S(1)} collective-permute-done((f32[64,64]{1,0:T(8,128)S(1)}, f32[64,64]{1,0:T(8,128)S(1)}, u32[]{:S(2)}, u32[]{:S(2)}) %collective-permute-start.1) | collective-permute-done | bytes 16416 | tf_op jit(solution)/shard_map/ppermute | solution.py:341
  11.1 1.4 %collective-permute-start.2 = (f32[64,64]{1,0:T(8,128)S(1)}, f32[64,64]{1,0:T(8,128)S(1)}, u32[]{:S(2)}, u32[]{:S(2)}) collective-permute-start(f32[64,64]{1,0:T(8,128)S(1)} %add.41), channel_id=1, source_target_pairs={{0,2},{1,3},{2,0},{3,1},{4,6},{5,7},{6,4},{7,5},{8,10},{9,11},{10,... | collective-permute-start | bytes 49160 | tf_op jit(solution)/shard_map/ppermute | solution.py:341
  12.5 0.0 copy-start.6
  12.5 0.0 copy-start.8
  12.6 5.8 %operator_table.2 = (bf16[316,64,64]{2,1,0:T(8,128)(2,1)}, f32[1,64,64]{2,1,0:T(8,128)S(1)}) custom-call(bf16[2,64,64,316]{3,2,1,0:T(8,128)(2,1)} %bitcast.14), custom_call_target="tpu_custom_call" | custom-call | tf_op jit(solution)/shard_map/operator_table/pallas_call | solution.py:137
  18.4 0.6 slice.12
  19.7 0.6 slice.16
  20.9 2.0 %collective-permute-start.5 = (bf16[36,64,128]{2,1,0:T(8,128)(2,1)S(1)}, bf16[36,64,128]{2,1,0:T(8,128)(2,1)S(1)}, u32[]{:S(2)}, u32[]{:S(2)}) collective-permute-start(bf16[36,64,128]{2,1,0:T(8,128)(2,1)S(1)} %copy-done.11), channel_id=1, source_target_pairs={{0,1},{1,2},{2,3},{3,4},{4,5},{5,6},{6,7},{7,8},{8,9},{9,10},{10,1... | collective-permute-start | bytes 1769480 | tf_op jit(solution)/shard_map/ppermute | solution.py:331
  22.9 1.3 %collective-permute-start.6 = (bf16[36,64,128]{2,1,0:T(8,128)(2,1)S(1)}, bf16[36,64,128]{2,1,0:T(8,128)(2,1)S(1)}, u32[]{:S(2)}, u32[]{:S(2)}) collective-permute-start(bf16[36,64,128]{2,1,0:T(8,128)(2,1)S(1)} %copy-done.11), channel_id=1, source_target_pairs={{1,0},{2,1},{3,2},{4,3},{5,4},{6,5},{7,6},{8,7},{9,8},{10,9},{11,1... | collective-permute-start | bytes 1769480 | tf_op jit(solution)/shard_map/ppermute | solution.py:336
  24.2 4.8 %collective-permute-start.3 = (f32[64,64]{1,0:T(8,128)S(1)}, f32[64,64]{1,0:T(8,128)S(1)}, u32[]{:S(2)}, u32[]{:S(2)}) collective-permute-start(f32[64,64]{1,0:T(8,128)S(1)} %get-tuple-element.28), channel_id=1, source_target_pairs={{0,4},{1,5},{2,6},{3,7},{4,0},{5,1},{6,2},{7,3},{8,12},{9,13},{10,... | collective-permute-start | bytes 49160 | tf_op jit(solution)/shard_map/ppermute | solution.py:341
  29.0 8.2 %collective-permute-done.3.rest_2_ = f32[64,64]{1,0:T(8,128)S(1)} collective-permute-done((f32[64,64]{1,0:T(8,128)S(1)}, f32[64,64]{1,0:T(8,128)S(1)}, u32[]{:S(2)}, u32[]{:S(2)}) %collective-permute-start.3) | collective-permute-done | bytes 16416 | tf_op jit(solution)/shard_map/ppermute | solution.py:341
  37.1 1.6 %collective-permute-start.4 = (f32[64,64]{1,0:T(8,128)S(1)}, f32[64,64]{1,0:T(8,128)S(1)}, u32[]{:S(2)}, u32[]{:S(2)}) collective-permute-start(f32[64,64]{1,0:T(8,128)S(1)} %add.47), channel_id=1, source_target_pairs={{0,8},{1,9},{2,10},{3,11},{4,12},{5,13},{6,14},{7,15},{8,0},{9,1},... | collective-permute-start | bytes 49160 | tf_op jit(solution)/shard_map/ppermute | solution.py:341
  38.7 7.1 %operator_table.3 = (bf16[316,64,64]{2,1,0:T(8,128)(2,1)}, f32[5,64,64]{2,1,0:T(8,128)S(1)}) custom-call(bf16[2,64,64,316]{3,2,1,0:T(8,128)(2,1)} %bitcast.15, f32[64,64]{1,0:T(8,128)S(1)} %copy-done.3, f32[64,64]{1,0:T(8,128)S(1)} %copy-done.4), custom_call_target="tpu_custom_call" | custom-call | tf_op jit(solution)/shard_map/operator_table/pallas_call | solution.py:137
  45.8 0.6 slice.17
  47.1 0.5 slice.18
  48.2 1.8 %collective-permute-start.7 = (f32[64,64]{1,0:T(8,128)S(1)}, f32[64,64]{1,0:T(8,128)S(1)}, u32[]{:S(2)}, u32[]{:S(2)}) collective-permute-start(f32[64,64]{1,0:T(8,128)S(1)} %add_add_fusion), channel_id=1, source_target_pairs={{0,16},{1,17},{2,18},{3,19},{4,20},{5,21},{6,22},{7,23},{8,24},{9,... | collective-permute-start | bytes 49160 | tf_op jit(solution)/shard_map/ppermute | solution.py:341
  50.0 3.3 %collective-permute-done.7.rest_4_ = f32[64,64]{1,0:T(8,128)S(1)} collective-permute-done((f32[64,64]{1,0:T(8,128)S(1)}, f32[64,64]{1,0:T(8,128)S(1)}, u32[]{:S(2)}, u32[]{:S(2)}) %collective-permute-start.7) | collective-permute-done | bytes 16416 | tf_op jit(solution)/shard_map/ppermute | solution.py:341
  53.3 1.3 %collective-permute-start.8 = (bf16[64,64,128]{2,1,0:T(8,128)(2,1)}, bf16[64,64,128]{2,1,0:T(8,128)(2,1)}, u32[]{:S(2)}, u32[]{:S(2)}) collective-permute-start(bf16[64,64,128]{2,1,0:T(8,128)(2,1)} %own), channel_id=1, source_target_pairs={{1,0},{2,1},{3,2},{4,3},{5,4},{6,5},{7,6},{8,7},{9,8},{10,9},{11,1... | collective-permute-start | bytes 3145736 | tf_op jit(solution)/shard_map/ppermute | solution.py:336
  54.6 0.1 pad_add_fusion.base
  54.8 12.5 %far.1 = (f32[64,64,128]{2,1,0:T(8,128)S(1)}, bf16[64,6,128,128]{3,2,1,0:T(8,128)(2,1)S(1)}) custom-call(s32[2]{0:T(128)S(1)} %pad_add_fusion.base, s32[24,64]{1,0:T(8,128)S(1)} %bitcast.11, s32[24,64]{1,0:T(8,128)S(1)} %bitcast.12, s32[8,24]{1,0:T(8,128)S(1)} %copy-done.7, s32[8,24]{1,0:T(8,128)S(1)} %copy-done.8, bf16[36,64,128]{2,1,0:T(8,128)(2,1)} %copy-done.12, ...), custom_call_target="tpu_custom_call" | custom-call | tf_op jit(solution)/shard_map/far/pallas_call | solution.py:306
  67.3 8.6 %near.1 = f32[64,64,128]{2,1,0:T(8,128)} custom-call(s32[2]{0:T(128)S(1)} %pad_add_fusion.base, s32[6,64]{1,0:T(8,128)S(1)} %bitcast.13, bf16[64,64,128]{2,1,0:T(8,128)(2,1)} %copy-done.10, bf16[64,64,128]{2,1,0:T(8,128)(2,1)} %own, bf16[64,64,128]{2,1,0:T(8,128)(2,1)} %collective-permute-done.8.right, ...), custom_call_target="tpu_custom_call" | custom-call | tf_op jit(solution)/shard_map/near/pallas_call | solution.py:199
  (36 shorter events, 0.1 us)
Async XLA Ops:
  0.0 38.7 %copy-start.3 = (f32[64,64]{1,0:T(8,128)S(1)}, f32[64,64]{1,0:T(8,128)}, u32[]{:S(2)}) copy-start(f32[64,64]{1,0:T(8,128)} %refs_0_.1) | copy-start | bytes 49156
  0.0 38.7 %copy-start.4 = (f32[64,64]{1,0:T(8,128)S(1)}, f32[64,64]{1,0:T(8,128)}, u32[]{:S(2)}) copy-start(f32[64,64]{1,0:T(8,128)} %refs_1_.1) | copy-start | bytes 49156
  0.0 19.7 %collective-permute-start = (bf16[64,64,128]{2,1,0:T(8,128)(2,1)}, bf16[64,64,128]{2,1,0:T(8,128)(2,1)S(1)}, u32[]{:S(2)}, u32[]{:S(2)}) collective-permute-start(bf16[64,64,128]{2,1,0:T(8,128)(2,1)} %own), channel_id=1, source_target_pairs={{0,1},{1,2},{2,3},{3,4},{4,5},{5,6},{6,7},{7,8},{8,9},{9,10},{10,1... | collective-permute-start | bytes 3145736 | tf_op jit(solution)/shard_map/ppermute | solution.py:331
  7.6 13.2 %copy-start.11 = (bf16[36,64,128]{2,1,0:T(8,128)(2,1)S(1)}, bf16[36,64,128]{2,1,0:T(8,128)(2,1)}, u32[]{:S(2)}) copy-start(bf16[36,64,128]{2,1,0:T(8,128)(2,1)} %get-tuple-element.33.own) | copy-start | bytes 1769476
  7.6 3.4 %collective-permute-start.1 = (f32[64,64]{1,0:T(8,128)S(1)}, f32[64,64]{1,0:T(8,128)S(1)}, u32[]{:S(2)}, u32[]{:S(2)}) collective-permute-start(f32[64,64]{1,0:T(8,128)S(1)} %get-tuple-element.23), channel_id=1, source_target_pairs={{0,1},{1,0},{2,3},{3,2},{4,5},{5,4},{6,7},{7,6},{8,9},{9,8},{10,11... | collective-permute-start | bytes 49160 | tf_op jit(solution)/shard_map/ppermute | solution.py:341
  11.1 9.7 %collective-permute-start.2 = (f32[64,64]{1,0:T(8,128)S(1)}, f32[64,64]{1,0:T(8,128)S(1)}, u32[]{:S(2)}, u32[]{:S(2)}) collective-permute-start(f32[64,64]{1,0:T(8,128)S(1)} %add.41), channel_id=1, source_target_pairs={{0,2},{1,3},{2,0},{3,1},{4,6},{5,7},{6,4},{7,5},{8,10},{9,11},{10,... | collective-permute-start | bytes 49160 | tf_op jit(solution)/shard_map/ppermute | solution.py:341
  12.5 42.2 %copy-start = (bf16[64,64,128]{2,1,0:T(8,128)(2,1)S(1)}, bf16[64,64,128]{2,1,0:T(8,128)(2,1)}, u32[]{:S(2)}) copy-start(bf16[64,64,128]{2,1,0:T(8,128)(2,1)} %basis.3) | copy-start | bytes 3145732
  12.5 42.2 %copy-start.1 = (bf16[64,64,64]{2,1,0:T(8,128)(2,1)S(1)}, bf16[64,64,64]{2,1,0:T(8,128)(2,1)}, u32[]{:S(2)}) copy-start(bf16[64,64,64]{2,1,0:T(8,128)(2,1)} %child.3) | copy-start | bytes 1572868
  12.5 42.2 %copy-start.2 = (bf16[8,64,64]{2,1,0:T(8,128)(2,1)S(1)}, bf16[8,64,64]{2,1,0:T(8,128)(2,1)}, u32[]{:S(2)}) copy-start(bf16[8,64,64]{2,1,0:T(8,128)(2,1)} %parent.3) | copy-start | bytes 196612
  12.5 42.2 %copy-start.5 = (s32[64,24]{0,1:T(8,128)S(1)}, s32[64,24]{0,1:T(8,128)}, u32[]{:S(2)}) copy-start(s32[64,24]{0,1:T(8,128)} %param.20) | copy-start | bytes 18436
  12.5 42.2 %copy-start.6 = (s32[64,24]{0,1:T(8,128)S(1)}, s32[64,24]{0,1:T(8,128)}, u32[]{:S(2)}) copy-start(s32[64,24]{0,1:T(8,128)} %param.21) | copy-start | bytes 18436
  12.5 42.2 %copy-start.7 = (s32[8,24]{1,0:T(8,128)S(1)}, s32[8,24]{1,0:T(8,128)}, u32[]{:S(2)}) copy-start(s32[8,24]{1,0:T(8,128)} %list1.1) | copy-start | bytes 2308
  12.5 42.2 %copy-start.8 = (s32[8,24]{1,0:T(8,128)S(1)}, s32[8,24]{1,0:T(8,128)}, u32[]{:S(2)}) copy-start(s32[8,24]{1,0:T(8,128)} %op1.1) | copy-start | bytes 2308
  19.7 33.6 %copy-start.10 = (bf16[64,64,128]{2,1,0:T(8,128)(2,1)}, bf16[64,64,128]{2,1,0:T(8,128)(2,1)S(1)}, u32[]{:S(2)}) copy-start(bf16[64,64,128]{2,1,0:T(8,128)(2,1)S(1)} %collective-permute-done.left) | copy-start | bytes 3145732
  20.9 25.0 %collective-permute-start.5 = (bf16[36,64,128]{2,1,0:T(8,128)(2,1)S(1)}, bf16[36,64,128]{2,1,0:T(8,128)(2,1)S(1)}, u32[]{:S(2)}, u32[]{:S(2)}) collective-permute-start(bf16[36,64,128]{2,1,0:T(8,128)(2,1)S(1)} %copy-done.11), channel_id=1, source_target_pairs={{0,1},{1,2},{2,3},{3,4},{4,5},{5,6},{6,7},{7,8},{8,9},{9,10},{10,1... | collective-permute-start | bytes 1769480 | tf_op jit(solution)/shard_map/ppermute | solution.py:331
  22.9 24.2 %collective-permute-start.6 = (bf16[36,64,128]{2,1,0:T(8,128)(2,1)S(1)}, bf16[36,64,128]{2,1,0:T(8,128)(2,1)S(1)}, u32[]{:S(2)}, u32[]{:S(2)}) collective-permute-start(bf16[36,64,128]{2,1,0:T(8,128)(2,1)S(1)} %copy-done.11), channel_id=1, source_target_pairs={{1,0},{2,1},{3,2},{4,3},{5,4},{6,5},{7,6},{8,7},{9,8},{10,9},{11,1... | collective-permute-start | bytes 1769480 | tf_op jit(solution)/shard_map/ppermute | solution.py:336
  24.2 12.9 %collective-permute-start.3 = (f32[64,64]{1,0:T(8,128)S(1)}, f32[64,64]{1,0:T(8,128)S(1)}, u32[]{:S(2)}, u32[]{:S(2)}) collective-permute-start(f32[64,64]{1,0:T(8,128)S(1)} %get-tuple-element.28), channel_id=1, source_target_pairs={{0,4},{1,5},{2,6},{3,7},{4,0},{5,1},{6,2},{7,3},{8,12},{9,13},{10,... | collective-permute-start | bytes 49160 | tf_op jit(solution)/shard_map/ppermute | solution.py:341
  37.1 8.7 %collective-permute-start.4 = (f32[64,64]{1,0:T(8,128)S(1)}, f32[64,64]{1,0:T(8,128)S(1)}, u32[]{:S(2)}, u32[]{:S(2)}) collective-permute-start(f32[64,64]{1,0:T(8,128)S(1)} %add.47), channel_id=1, source_target_pairs={{0,8},{1,9},{2,10},{3,11},{4,12},{5,13},{6,14},{7,15},{8,0},{9,1},... | collective-permute-start | bytes 49160 | tf_op jit(solution)/shard_map/ppermute | solution.py:341
  45.8 8.8 %copy-start.12 = (bf16[36,64,128]{2,1,0:T(8,128)(2,1)}, bf16[36,64,128]{2,1,0:T(8,128)(2,1)S(1)}, u32[]{:S(2)}) copy-start(bf16[36,64,128]{2,1,0:T(8,128)(2,1)S(1)} %collective-permute-done.5.left) | copy-start | bytes 1769476
  47.0 7.6 %copy-start.13 = (bf16[36,64,128]{2,1,0:T(8,128)(2,1)}, bf16[36,64,128]{2,1,0:T(8,128)(2,1)S(1)}, u32[]{:S(2)}) copy-start(bf16[36,64,128]{2,1,0:T(8,128)(2,1)S(1)} %collective-permute-done.6.right) | copy-start | bytes 1769476
  48.2 5.1 %collective-permute-start.7 = (f32[64,64]{1,0:T(8,128)S(1)}, f32[64,64]{1,0:T(8,128)S(1)}, u32[]{:S(2)}, u32[]{:S(2)}) collective-permute-start(f32[64,64]{1,0:T(8,128)S(1)} %add_add_fusion), channel_id=1, source_target_pairs={{0,16},{1,17},{2,18},{3,19},{4,20},{5,21},{6,22},{7,23},{8,24},{9,... | collective-permute-start | bytes 49160 | tf_op jit(solution)/shard_map/ppermute | solution.py:341
  53.3 14.0 %collective-permute-start.8 = (bf16[64,64,128]{2,1,0:T(8,128)(2,1)}, bf16[64,64,128]{2,1,0:T(8,128)(2,1)}, u32[]{:S(2)}, u32[]{:S(2)}) collective-permute-start(bf16[64,64,128]{2,1,0:T(8,128)(2,1)} %own), channel_id=1, source_target_pairs={{1,0},{2,1},{3,2},{4,3},{5,4},{6,5},{7,6},{8,7},{9,8},{10,9},{11,1... | collective-permute-start | bytes 3145736 | tf_op jit(solution)/shard_map/ppermute | solution.py:336
  54.8 12.6 %copy-start.9 = (s32[64,6]{0,1:T(8,128)S(1)}, s32[64,6]{0,1:T(8,128)}, u32[]{:S(2)}) copy-start(s32[64,6]{0,1:T(8,128)} %param.15) | copy-start | bytes 4612

commit v6 on v5

--- a/solution.py
+++ b/solution.py
@@ -97,55 +97,69 @@
 OPS_BLOCK = 128
 
 
-def table_kernel(count, ops, *refs):
-    *top, table, chain, turned = refs
-    rank = ops.shape[1]
+def table_kernel(level, ops, *refs):
+    *top, table, chain, fetched, turned, turned_back, in_sems, out_sems = refs
+    rank, _, count = fetched.shape
     half = rank // 2
+    quarter = rank // 4
     stride = turned.shape[0] // half
-    first = pl.program_id(0) * OPS_BLOCK
-
-    @pl.when(first == 0)
-    def _():
-        if not top:
-            chain[...] = jnp.zeros_like(chain)
-            return
+
+    def fetch(i):
+        rows = pl.ds(i * quarter, quarter)
+        return pltpu.make_async_copy(ops.at[level, rows], fetched.at[rows], in_sems.at[i])
+
+    for i in (0, 2, 1, 3):
+        fetch(i).start()
+    if top:
         transfer, couple = top
         link = couple[...]
         chain[0] = link
         for j in range(1, chain.shape[0]):
             link = mm(mm(transfer[...], link, precision=highest), transfer[...], NT, precision=highest)
             chain[j] = link
-
-    for k in range(half):
-        both = jnp.concatenate([ops[0, k], ops[0, k + half]], axis=0).astype(f32)
-        turned[k * stride : k * stride + OPS_BLOCK, :] = both.T
-
-    def rows_of(start, stop):
-        for o in range(start, stop):
+    else:
+        chain[...] = jnp.zeros_like(chain)
+    for part in range(2):
+        fetch(part).wait()
+        fetch(part + 2).wait()
+        for k in range(part * quarter, (part + 1) * quarter):
+            both = jnp.concatenate([fetched[k], fetched[k + half]], axis=0).astype(f32)
+            turned[k * stride : k * stride + count, :] = both.T
+    copies = []
+    for first in range(0, count, OPS_BLOCK):
+        size = min(OPS_BLOCK, count - first)
+        for o in range(first, first + size):
             rows = turned[pl.ds(o, half, stride=stride), :]
-            table[o] = jnp.concatenate([rows[:, :rank], rows[:, rank:]], axis=0).astype(bf16)
-
-    rows_of(0, count % OPS_BLOCK)
-
-    @pl.when(first + OPS_BLOCK <= count)
-    def _():
-        rows_of(count % OPS_BLOCK, OPS_BLOCK)
+            turned_back[o] = jnp.concatenate([rows[:, :rank], rows[:, rank:]], axis=0).astype(bf16)
+        block = pl.ds(first, size)
+        copies.append(
+            pltpu.make_async_copy(turned_back.at[block], table.at[block], out_sems.at[first // OPS_BLOCK])
+        )
+        copies[-1].start()
+    for copy in copies:
+        copy.wait()
 
 
 def table_call(ops, level, top, links):
     _, count, rank, _ = ops.shape
+    stride = pl.cdiv(count, 8) * 8
+    stride += 8 * (stride // 8 % 2 == 0)
     return pl.pallas_call(
-        functools.partial(table_kernel, count),
-        grid=(pl.cdiv(count, OPS_BLOCK),),
-        in_specs=[pl.BlockSpec((1, rank, rank, OPS_BLOCK), lambda i: (level, 0, 0, i))]
-        + [VMEM for _ in top],
-        out_specs=[pl.BlockSpec((OPS_BLOCK, rank, rank), lambda i: (i, 0, 0)), VMEM],
+        functools.partial(table_kernel, level),
+        in_specs=[HBM] + [VMEM for _ in top],
+        out_specs=[HBM, VMEM],
         out_shape=[
             pltpu.HBM((count, rank, rank), bf16),
             jax.ShapeDtypeStruct((links, rank, rank), f32),
         ],
-        scratch_shapes=[pltpu.VMEM((rank // 2 * (OPS_BLOCK + 8), 2 * rank), f32)],
-        compiler_params=params(16),
+        scratch_shapes=[
+            pltpu.VMEM((rank, rank, count), bf16),
+            pltpu.VMEM((rank // 2 * stride, 2 * rank), f32),
+            pltpu.VMEM((count, rank, rank), bf16),
+            pltpu.SemaphoreType.DMA((4,)),
+            pltpu.SemaphoreType.DMA((pl.cdiv(count, OPS_BLOCK),)),
+        ],
+        compiler_params=pltpu.CompilerParams(vmem_limit_bytes=24 * 1024 * 1024),
         name="operator_table",
     )(in_hbm(jnp.transpose(ops, (0, 2, 3, 1))), *top)
 
@@ -253,7 +267,7 @@
             ]
         )
     ]
-    for copy in copies:
+    for copy in copies[:5]:
         copy.start()
     field = mm(siblings[0][...], chain[0], precision=highest)
     for j in range(1, len(siblings)):
@@ -280,6 +294,7 @@
     for q, acc in enumerate(accs):
         parent_locals[q] = acc.astype(bf16)
     copies[4].wait()
+    copies[5].start()
 
     def one_parent(q, _):
         parent_local = parent_locals[q]
@@ -343,7 +358,7 @@
 
 def after(x, *arrived):
     for y in arrived:
-        x = x + jnp.minimum(jnp.abs(y[0, 0, 0].astype(f32)), 0.0)
+        x = x + jnp.minimum(jnp.abs(y[0, : x.shape[0], : x.shape[1]].astype(f32)), 0.0)
     return x
 
 
@@ -365,11 +380,11 @@
             total, ops = tie((total, m2l_ops))
             leaf_ops, token = table_call(ops, 0, (), 1)
         if level == 2:
-            total, send = tie((after(total, charges_left), send))
+            total = after(total, charges_left)
+        if level == 3:
+            total, send, ops = tie((total, send, m2l_ops))
             moments_left = to_right(send)
             moments_right = to_left(send)
-        if level == 3:
-            total, ops = tie((total, m2l_ops))
             parent_ops, chain = table_call(ops, 1, (top_transfer, top_couple), height)
         if level == height - 1:
             total = after(total, moments_left, moments_right)

time: 77.1 us -> 72.1 us (0.935)
  the two profiles are of different devices: /device:TPU:0 before, /device:TPU:1 now
where the time goes in v6:
time: 72.1 us; the launch traced here: 71.8 us
  Pallas kernels  37.6 us (52%)
  starting transfers between devices  25.4 us (35%)
  waiting for transfers between devices  8.46 us (12%)
    ppermute x5, starting transfers between devices, from_partner(): lax.ppermute(block, AXES, [(i, i ^ 1 << apart) for i in range(count)])  13.2 us
    pallas_call x1, Pallas kernels, far_call(): pl.pallas_call(far_kernel, in_specs=[SMEM] * 5 + [HBM] * 6 + [VMEM] * (4...  12.5 us
    pallas_call x2, Pallas kernels, table_call(): pl.pallas_call(functools.partial(table_kernel, level), in_specs=[HBM] + [...  11.4 us
    pallas_call x1, Pallas kernels, near_call(): pl.pallas_call(near_kernel, in_specs=[SMEM, SMEM, HBM, HBM, HBM, VMEM, VM...  8.58 us
    ppermute x2, starting transfers between devices, to_right(): return lax.ppermute(block, AXES, [(i, i + 1) for i in range(count - 1)])  8.29 us
    pallas_call x1, Pallas kernels, moments_call(): pl.pallas_call(moments_kernel, grid=(steps,), in_specs=[pl.BlockSpec((16,...  5.08 us
    ppermute x2, starting transfers between devices, to_left(): return lax.ppermute(block, AXES, [(i + 1, i) for i in range(count - 1)])  3.83 us
    ppermute x5, waiting for transfers between devices, from_partner(): lax.ppermute(block, AXES, [(i, i ^ 1 << apart) for i in range(count)])  3.82 us
  transfers between devices with their start and end apart: 9, of which 5 were waited for; matrix products, arithmetic and copies ran while one was open for 0% of the time, Pallas kernels for 40%

profile of v6, /device:TPU:1, one launch (start us, length us, event | category | flops | bytes accessed | tf_op | source)
XLA Modules:
  0.0 71.8 jit_solution(9540150969859926932)
XLA Ops:
  0.0 4.7 %collective-permute-start = (bf16[64,64,128]{2,1,0:T(8,128)(2,1)}, bf16[64,64,128]{2,1,0:T(8,128)(2,1)S(1)}, u32[]{:S(2)}, u32[]{:S(2)}) collective-permute-start(bf16[64,64,128]{2,1,0:T(8,128)(2,1)} %own), channel_id=1, source_target_pairs={{0,1},{1,2},{2,3},{3,4},{4,5},{5,6},{6,7},{7,8},{8,9},{9,10},{10,1... | collective-permute-start | bytes 3145736 | tf_op jit(solution)/shard_map/ppermute | solution.py:346
  4.7 5.1 %moments.1 = (bf16[36,64,128]{2,1,0:T(8,128)(2,1)}, f32[64,64]{1,0:T(8,128)S(1)}) custom-call(bf16[64,64,128]{2,1,0:T(8,128)(2,1)} %own, bf16[64,64,128]{2,1,0:T(8,128)(2,1)} %basis.3, bf16[64,64,64]{2,1,0:T(8,128)(2,1)} %child.3, bf16[8,64,64]{2,1,0:T(8,128)(2,1)} %parent.3), custom_call_target="tpu_custom_call" | custom-call | tf_op jit(solution)/shard_map/moments/pallas_call | solution.py:75
  9.8 0.0 collective-permute-start.1
  9.8 1.2 %collective-permute-done.1.rest_0_ = f32[64,64]{1,0:T(8,128)S(1)} collective-permute-done((f32[64,64]{1,0:T(8,128)S(1)}, f32[64,64]{1,0:T(8,128)S(1)}, u32[]{:S(2)}, u32[]{:S(2)}) %collective-permute-start.1) | collective-permute-done | bytes 16416 | tf_op jit(solution)/shard_map/ppermute | solution.py:356
  11.0 1.2 %collective-permute-start.2 = (f32[64,64]{1,0:T(8,128)S(1)}, f32[64,64]{1,0:T(8,128)S(1)}, u32[]{:S(2)}, u32[]{:S(2)}) collective-permute-start(f32[64,64]{1,0:T(8,128)S(1)} %add.29), channel_id=1, source_target_pairs={{0,2},{1,3},{2,0},{3,1},{4,6},{5,7},{6,4},{7,5},{8,10},{9,11},{10,... | collective-permute-start | bytes 49160 | tf_op jit(solution)/shard_map/ppermute | solution.py:356
  12.1 0.0 copy-start.6
  12.1 0.0 copy-start.7
  12.2 0.0 copy-start.8
  12.2 5.5 %operator_table.2 = (bf16[316,64,64]{2,1,0:T(8,128)(2,1)}, f32[1,64,64]{2,1,0:T(8,128)S(1)}) custom-call(bf16[2,64,64,316]{3,2,1,0:T(8,128)(2,1)} %bitcast.21), custom_call_target="tpu_custom_call" | custom-call | tf_op jit(solution)/shard_map/operator_table/pallas_call | solution.py:147
  17.7 2.7 %collective-permute-start.3 = (f32[64,64]{1,0:T(8,128)S(1)}, f32[64,64]{1,0:T(8,128)S(1)}, u32[]{:S(2)}, u32[]{:S(2)}) collective-permute-start(f32[64,64]{1,0:T(8,128)S(1)} %get-tuple-element.39), channel_id=1, source_target_pairs={{0,4},{1,5},{2,6},{3,7},{4,0},{5,1},{6,2},{7,3},{8,12},{9,13},{10,... | collective-permute-start | bytes 49160 | tf_op jit(solution)/shard_map/ppermute | solution.py:356
  20.4 1.3 %collective-permute-done.3.rest_2_ = f32[64,64]{1,0:T(8,128)S(1)} collective-permute-done((f32[64,64]{1,0:T(8,128)S(1)}, f32[64,64]{1,0:T(8,128)S(1)}, u32[]{:S(2)}, u32[]{:S(2)}) %collective-permute-start.3) | collective-permute-done | bytes 16416 | tf_op jit(solution)/shard_map/ppermute | solution.py:356
  21.7 3.6 %collective-permute-start.5 = (bf16[36,64,128]{2,1,0:T(8,128)(2,1)S(1)}, bf16[36,64,128]{2,1,0:T(8,128)(2,1)S(1)}, u32[]{:S(2)}, u32[]{:S(2)}) collective-permute-start(bf16[36,64,128]{2,1,0:T(8,128)(2,1)S(1)} %copy-done.13), channel_id=1, source_target_pairs={{0,1},{1,2},{2,3},{3,4},{4,5},{5,6},{6,7},{7,8},{8,9},{9,10},{10,1... | collective-permute-start | bytes 1769480 | tf_op jit(solution)/shard_map/ppermute | solution.py:346
  25.4 1.9 %collective-permute-start.6 = (bf16[36,64,128]{2,1,0:T(8,128)(2,1)S(1)}, bf16[36,64,128]{2,1,0:T(8,128)(2,1)S(1)}, u32[]{:S(2)}, u32[]{:S(2)}) collective-permute-start(bf16[36,64,128]{2,1,0:T(8,128)(2,1)S(1)} %copy-done.13), channel_id=1, source_target_pairs={{1,0},{2,1},{3,2},{4,3},{5,4},{6,5},{7,6},{8,7},{9,8},{10,9},{11,1... | collective-permute-start | bytes 1769480 | tf_op jit(solution)/shard_map/ppermute | solution.py:351
  27.3 2.4 %collective-permute-start.4 = (f32[64,64]{1,0:T(8,128)S(1)}, f32[64,64]{1,0:T(8,128)S(1)}, u32[]{:S(2)}, u32[]{:S(2)}) collective-permute-start(f32[64,64]{1,0:T(8,128)S(1)} %add.33), channel_id=1, source_target_pairs={{0,8},{1,9},{2,10},{3,11},{4,12},{5,13},{6,14},{7,15},{8,0},{9,1},... | collective-permute-start | bytes 49160 | tf_op jit(solution)/shard_map/ppermute | solution.py:356
  29.7 5.9 %operator_table.3 = (bf16[316,64,64]{2,1,0:T(8,128)(2,1)}, f32[5,64,64]{2,1,0:T(8,128)S(1)}) custom-call(bf16[2,64,64,316]{3,2,1,0:T(8,128)(2,1)} %bitcast.22, f32[64,64]{1,0:T(8,128)S(1)} %copy-done.3, f32[64,64]{1,0:T(8,128)S(1)} %copy-done.4), custom_call_target="tpu_custom_call" | custom-call | tf_op jit(solution)/shard_map/operator_table/pallas_call | solution.py:147
  35.6 2.8 %collective-permute-done.5.left = bf16[36,64,128]{2,1,0:T(8,128)(2,1)S(1)} collective-permute-done((bf16[36,64,128]{2,1,0:T(8,128)(2,1)S(1)}, bf16[36,64,128]{2,1,0:T(8,128)(2,1)S(1)}, u32[]{:S(2)}, u32[]{:S(2)}) %collective-permute-start.5) | collective-permute-done | bytes 589856 | tf_op jit(solution)/shard_map/ppermute | solution.py:346
  38.5 7.0 %collective-permute-start.7 = (f32[64,64]{1,0:T(8,128)S(1)}, f32[64,64]{1,0:T(8,128)S(1)}, u32[]{:S(2)}, u32[]{:S(2)}) collective-permute-start(f32[64,64]{1,0:T(8,128)S(1)} %bitcast_add_fusion), channel_id=1, source_target_pairs={{0,16},{1,17},{2,18},{3,19},{4,20},{5,21},{6,22},{7,23},{8,24},{9,... | collective-permute-start | bytes 49160 | tf_op jit(solution)/shard_map/ppermute | solution.py:356
  45.5 1.3 %collective-permute-done.7.rest_4_ = f32[64,64]{1,0:T(8,128)S(1)} collective-permute-done((f32[64,64]{1,0:T(8,128)S(1)}, f32[64,64]{1,0:T(8,128)S(1)}, u32[]{:S(2)}, u32[]{:S(2)}) %collective-permute-start.7) | collective-permute-done | bytes 16416 | tf_op jit(solution)/shard_map/ppermute | solution.py:356
  46.8 1.9 %collective-permute-start.8 = (bf16[64,64,128]{2,1,0:T(8,128)(2,1)}, bf16[64,64,128]{2,1,0:T(8,128)(2,1)}, u32[]{:S(2)}, u32[]{:S(2)}) collective-permute-start(bf16[64,64,128]{2,1,0:T(8,128)(2,1)} %own), channel_id=1, source_target_pairs={{1,0},{2,1},{3,2},{4,3},{5,4},{6,5},{7,6},{8,7},{9,8},{10,9},{11,1... | collective-permute-start | bytes 3145736 | tf_op jit(solution)/shard_map/ppermute | solution.py:351
  48.7 0.1 pad_add_fusion.base
  48.9 0.0 copy-start.9
  48.9 12.5 %far.1 = (f32[64,64,128]{2,1,0:T(8,128)S(1)}, bf16[64,6,128,128]{3,2,1,0:T(8,128)(2,1)S(1)}) custom-call(s32[2]{0:T(128)S(1)} %pad_add_fusion.base, s32[24,64]{1,0:T(8,128)S(1)} %bitcast.18, s32[24,64]{1,0:T(8,128)S(1)} %bitcast.19, s32[8,24]{1,0:T(8,128)S(1)} %copy-done.7, s32[8,24]{1,0:T(8,128)S(1)} %copy-done.8, bf16[36,64,128]{2,1,0:T(8,128)(2,1)} %copy-done.11, ...), custom_call_target="tpu_custom_call" | custom-call | tf_op jit(solution)/shard_map/far/pallas_call | solution.py:321
  61.4 1.8 %collective-permute-done.8.right = bf16[64,64,128]{2,1,0:T(8,128)(2,1)} collective-permute-done((bf16[64,64,128]{2,1,0:T(8,128)(2,1)}, bf16[64,64,128]{2,1,0:T(8,128)(2,1)}, u32[]{:S(2)}, u32[]{:S(2)}) %collective-permute-start.8) | collective-permute-done | bytes 1048608 | tf_op jit(solution)/shard_map/ppermute | solution.py:351
  63.2 8.6 %near.1 = f32[64,64,128]{2,1,0:T(8,128)} custom-call(s32[2]{0:T(128)S(1)} %pad_add_fusion.base, s32[6,64]{1,0:T(8,128)S(1)} %bitcast.20, bf16[64,64,128]{2,1,0:T(8,128)(2,1)} %copy-done.10, bf16[64,64,128]{2,1,0:T(8,128)(2,1)} %own, bf16[64,64,128]{2,1,0:T(8,128)(2,1)} %collective-permute-done.8.right, ...), custom_call_target="tpu_custom_call" | custom-call | tf_op jit(solution)/shard_map/near/pallas_call | solution.py:213
  (32 shorter events, 0.1 us)
Async XLA Ops:
  0.0 29.7 %copy-start.3 = (f32[64,64]{1,0:T(8,128)S(1)}, f32[64,64]{1,0:T(8,128)}, u32[]{:S(2)}) copy-start(f32[64,64]{1,0:T(8,128)} %refs_0_.1) | copy-start | bytes 49156
  0.0 29.7 %copy-start.4 = (f32[64,64]{1,0:T(8,128)S(1)}, f32[64,64]{1,0:T(8,128)}, u32[]{:S(2)}) copy-start(f32[64,64]{1,0:T(8,128)} %refs_1_.1) | copy-start | bytes 49156
  0.0 17.7 %collective-permute-start = (bf16[64,64,128]{2,1,0:T(8,128)(2,1)}, bf16[64,64,128]{2,1,0:T(8,128)(2,1)S(1)}, u32[]{:S(2)}, u32[]{:S(2)}) collective-permute-start(bf16[64,64,128]{2,1,0:T(8,128)(2,1)} %own), channel_id=1, source_target_pairs={{0,1},{1,2},{2,3},{3,4},{4,5},{5,6},{6,7},{7,8},{8,9},{9,10},{10,1... | collective-permute-start | bytes 3145736 | tf_op jit(solution)/shard_map/ppermute | solution.py:346
  9.8 12.0 %copy-start.13 = (bf16[36,64,128]{2,1,0:T(8,128)(2,1)S(1)}, bf16[36,64,128]{2,1,0:T(8,128)(2,1)}, u32[]{:S(2)}) copy-start(bf16[36,64,128]{2,1,0:T(8,128)(2,1)} %get-tuple-element.31.own) | copy-start | bytes 1769476
  9.8 1.2 %collective-permute-start.1 = (f32[64,64]{1,0:T(8,128)S(1)}, f32[64,64]{1,0:T(8,128)S(1)}, u32[]{:S(2)}, u32[]{:S(2)}) collective-permute-start(f32[64,64]{1,0:T(8,128)S(1)} %get-tuple-element.22), channel_id=1, source_target_pairs={{0,1},{1,0},{2,3},{3,2},{4,5},{5,4},{6,7},{7,6},{8,9},{9,8},{10,11... | collective-permute-start | bytes 49160 | tf_op jit(solution)/shard_map/ppermute | solution.py:356
  11.0 6.7 %collective-permute-start.2 = (f32[64,64]{1,0:T(8,128)S(1)}, f32[64,64]{1,0:T(8,128)S(1)}, u32[]{:S(2)}, u32[]{:S(2)}) collective-permute-start(f32[64,64]{1,0:T(8,128)S(1)} %add.29), channel_id=1, source_target_pairs={{0,2},{1,3},{2,0},{3,1},{4,6},{5,7},{6,4},{7,5},{8,10},{9,11},{10,... | collective-permute-start | bytes 49160 | tf_op jit(solution)/shard_map/ppermute | solution.py:356
  12.1 36.7 %copy-start = (bf16[64,64,128]{2,1,0:T(8,128)(2,1)S(1)}, bf16[64,64,128]{2,1,0:T(8,128)(2,1)}, u32[]{:S(2)}) copy-start(bf16[64,64,128]{2,1,0:T(8,128)(2,1)} %basis.3) | copy-start | bytes 3145732
  12.1 36.7 %copy-start.1 = (bf16[64,64,64]{2,1,0:T(8,128)(2,1)S(1)}, bf16[64,64,64]{2,1,0:T(8,128)(2,1)}, u32[]{:S(2)}) copy-start(bf16[64,64,64]{2,1,0:T(8,128)(2,1)} %child.3) | copy-start | bytes 1572868
  12.1 36.7 %copy-start.2 = (bf16[8,64,64]{2,1,0:T(8,128)(2,1)S(1)}, bf16[8,64,64]{2,1,0:T(8,128)(2,1)}, u32[]{:S(2)}) copy-start(bf16[8,64,64]{2,1,0:T(8,128)(2,1)} %parent.3) | copy-start | bytes 196612
  12.1 36.7 %copy-start.5 = (s32[64,24]{0,1:T(8,128)S(1)}, s32[64,24]{0,1:T(8,128)}, u32[]{:S(2)}) copy-start(s32[64,24]{0,1:T(8,128)} %param.20) | copy-start | bytes 18436
  12.1 36.7 %copy-start.6 = (s32[64,24]{0,1:T(8,128)S(1)}, s32[64,24]{0,1:T(8,128)}, u32[]{:S(2)}) copy-start(s32[64,24]{0,1:T(8,128)} %param.21) | copy-start | bytes 18436
  12.1 36.7 %copy-start.7 = (s32[8,24]{1,0:T(8,128)S(1)}, s32[8,24]{1,0:T(8,128)}, u32[]{:S(2)}) copy-start(s32[8,24]{1,0:T(8,128)} %list1.1) | copy-start | bytes 2308
  12.2 36.7 %copy-start.8 = (s32[8,24]{1,0:T(8,128)S(1)}, s32[8,24]{1,0:T(8,128)}, u32[]{:S(2)}) copy-start(s32[8,24]{1,0:T(8,128)} %op1.1) | copy-start | bytes 2308
  17.7 29.1 %copy-start.10 = (bf16[64,64,128]{2,1,0:T(8,128)(2,1)}, bf16[64,64,128]{2,1,0:T(8,128)(2,1)S(1)}, u32[]{:S(2)}) copy-start(bf16[64,64,128]{2,1,0:T(8,128)(2,1)S(1)} %collective-permute-done.left) | copy-start | bytes 3145732
  17.7 4.0 %collective-permute-start.3 = (f32[64,64]{1,0:T(8,128)S(1)}, f32[64,64]{1,0:T(8,128)S(1)}, u32[]{:S(2)}, u32[]{:S(2)}) collective-permute-start(f32[64,64]{1,0:T(8,128)S(1)} %get-tuple-element.39), channel_id=1, source_target_pairs={{0,4},{1,5},{2,6},{3,7},{4,0},{5,1},{6,2},{7,3},{8,12},{9,13},{10,... | collective-permute-start | bytes 49160 | tf_op jit(solution)/shard_map/ppermute | solution.py:356
  21.7 16.8 %collective-permute-start.5 = (bf16[36,64,128]{2,1,0:T(8,128)(2,1)S(1)}, bf16[36,64,128]{2,1,0:T(8,128)(2,1)S(1)}, u32[]{:S(2)}, u32[]{:S(2)}) collective-permute-start(bf16[36,64,128]{2,1,0:T(8,128)(2,1)S(1)} %copy-done.13), channel_id=1, source_target_pairs={{0,1},{1,2},{2,3},{3,4},{4,5},{5,6},{6,7},{7,8},{8,9},{9,10},{10,1... | collective-permute-start | bytes 1769480 | tf_op jit(solution)/shard_map/ppermute | solution.py:346
  25.4 13.1 %collective-permute-start.6 = (bf16[36,64,128]{2,1,0:T(8,128)(2,1)S(1)}, bf16[36,64,128]{2,1,0:T(8,128)(2,1)S(1)}, u32[]{:S(2)}, u32[]{:S(2)}) collective-permute-start(bf16[36,64,128]{2,1,0:T(8,128)(2,1)S(1)} %copy-done.13), channel_id=1, source_target_pairs={{1,0},{2,1},{3,2},{4,3},{5,4},{6,5},{7,6},{8,7},{9,8},{10,9},{11,1... | collective-permute-start | bytes 1769480 | tf_op jit(solution)/shard_map/ppermute | solution.py:351
  27.3 8.3 %collective-permute-start.4 = (f32[64,64]{1,0:T(8,128)S(1)}, f32[64,64]{1,0:T(8,128)S(1)}, u32[]{:S(2)}, u32[]{:S(2)}) collective-permute-start(f32[64,64]{1,0:T(8,128)S(1)} %add.33), channel_id=1, source_target_pairs={{0,8},{1,9},{2,10},{3,11},{4,12},{5,13},{6,14},{7,15},{8,0},{9,1},... | collective-permute-start | bytes 49160 | tf_op jit(solution)/shard_map/ppermute | solution.py:356
  38.5 10.3 %copy-start.11 = (bf16[36,64,128]{2,1,0:T(8,128)(2,1)}, bf16[36,64,128]{2,1,0:T(8,128)(2,1)S(1)}, u32[]{:S(2)}) copy-start(bf16[36,64,128]{2,1,0:T(8,128)(2,1)S(1)} %collective-permute-done.5.left) | copy-start | bytes 1769476
  38.5 10.2 %copy-start.12 = (bf16[36,64,128]{2,1,0:T(8,128)(2,1)}, bf16[36,64,128]{2,1,0:T(8,128)(2,1)S(1)}, u32[]{:S(2)}) copy-start(bf16[36,64,128]{2,1,0:T(8,128)(2,1)S(1)} %collective-permute-done.6.right) | copy-start | bytes 1769476
  38.5 8.3 %collective-permute-start.7 = (f32[64,64]{1,0:T(8,128)S(1)}, f32[64,64]{1,0:T(8,128)S(1)}, u32[]{:S(2)}, u32[]{:S(2)}) collective-permute-start(f32[64,64]{1,0:T(8,128)S(1)} %bitcast_add_fusion), channel_id=1, source_target_pairs={{0,16},{1,17},{2,18},{3,19},{4,20},{5,21},{6,22},{7,23},{8,24},{9,... | collective-permute-start | bytes 49160 | tf_op jit(solution)/shard_map/ppermute | solution.py:356
  46.8 16.4 %collective-permute-start.8 = (bf16[64,64,128]{2,1,0:T(8,128)(2,1)}, bf16[64,64,128]{2,1,0:T(8,128)(2,1)}, u32[]{:S(2)}, u32[]{:S(2)}) collective-permute-start(bf16[64,64,128]{2,1,0:T(8,128)(2,1)} %own), channel_id=1, source_target_pairs={{1,0},{2,1},{3,2},{4,3},{5,4},{6,5},{7,6},{8,7},{9,8},{10,9},{11,1... | collective-permute-start | bytes 3145736 | tf_op jit(solution)/shard_map/ppermute | solution.py:351
  48.9 14.4 %copy-start.9 = (s32[64,6]{0,1:T(8,128)S(1)}, s32[64,6]{0,1:T(8,128)}, u32[]{:S(2)}) copy-start(s32[64,6]{0,1:T(8,128)} %param.15) | copy-start | bytes 4612

commit v7 on v6

--- a/solution.py
+++ b/solution.py
@@ -164,7 +164,7 @@
     )(in_hbm(jnp.transpose(ops, (0, 2, 3, 1))), *top)
 
 
-NEAR_LEAVES = 8
+NEAR_LEAVES = 16
 
 
 def near_kernel(base, near, left, own, right, blocks, far, out, sources, out_buf, halo_sems, out_sems):
@@ -189,14 +189,15 @@
         results = []
         for i in range(NEAR_LEAVES):
             row = c * NEAR_LEAVES + i
-            acc = far[row]
+            acc = None
             for n in range(0, count, 2):
-                lhs = jnp.concatenate(
+                lhs = jnp.concatenate([blocks[row, n], blocks[row, n + 1]], axis=1)
+                rhs = jnp.concatenate(
                     [sources[near[n, row] - base[0]], sources[near[n + 1, row] - base[0]]], axis=1
                 )
-                rhs = jnp.concatenate([blocks[row, n], blocks[row, n + 1]], axis=1)
-                acc = acc + mm(lhs, rhs, NT)
-            results.append(acc)
+                term = mm(lhs, rhs, NT)
+                acc = term if acc is None else acc + term
+            results.append(far[row] + acc.T)
         for i, acc in enumerate(results):
             out_buf[c * NEAR_LEAVES + i] = acc
         store(c).start()
@@ -386,15 +387,15 @@
             moments_left = to_right(send)
             moments_right = to_left(send)
             parent_ops, chain = table_call(ops, 1, (top_transfer, top_couple), height)
-        if level == height - 1:
-            total = after(total, moments_left, moments_right)
         partner = from_partner(total, level)
         if level == 1:
             partner = after(partner, token)
         if level == 3:
             partner, chain = tie((partner, chain))
         if level == height - 1:
-            partner, charges = tie((partner, charges))
+            partner, charges, moments_left, moments_right = tie(
+                (partner, charges, moments_left, moments_right)
+            )
             charges_right = to_left(charges)
         siblings.append(partner)
         total = total + partner

time: 72.1 us -> 70.4 us (0.976)
  the two profiles are of different devices: /device:TPU:1 before, /device:TPU:0 now
where the time goes in v7:
time: 70.4 us; the launch traced here: 69 us
  Pallas kernels  36.4 us (52%)
  starting transfers between devices  23.8 us (34%)
  waiting for transfers between devices  7.51 us (11%)
  local copies, waits for them, and re-layouts  0.93 us (1%)
    ppermute x5, starting transfers between devices, from_partner(): lax.ppermute(block, AXES, [(i, i ^ 1 << apart) for i in range(count)])  17.4 us
    pallas_call x1, Pallas kernels, far_call(): pl.pallas_call(far_kernel, in_specs=[SMEM] * 5 + [HBM] * 6 + [VMEM] * (4...  12.6 us
    pallas_call x2, Pallas kernels, table_call(): pl.pallas_call(functools.partial(table_kernel, level), in_specs=[HBM] + [...  11.4 us
    ppermute x5, waiting for transfers between devices, from_partner(): lax.ppermute(block, AXES, [(i, i ^ 1 << apart) for i in range(count)])  7.5 us
    pallas_call x1, Pallas kernels, near_call(): pl.pallas_call(near_kernel, in_specs=[SMEM, SMEM, HBM, HBM, HBM, VMEM, VM...  7.41 us
    pallas_call x1, Pallas kernels, moments_call(): pl.pallas_call(moments_kernel, grid=(steps,), in_specs=[pl.BlockSpec((16,...  5.08 us
    ppermute x2, starting transfers between devices, to_right(): return lax.ppermute(block, AXES, [(i, i + 1) for i in range(count - 1)])  3.87 us
    ppermute x2, starting transfers between devices, to_left(): return lax.ppermute(block, AXES, [(i + 1, i) for i in range(count - 1)])  2.57 us
  transfers between devices with their start and end apart: 9, of which 4 were waited for; matrix products, arithmetic and copies ran while one was open for 0% of the time, Pallas kernels for 42%

profile of v7, /device:TPU:0, one launch (start us, length us, event | category | flops | bytes accessed | tf_op | source)
XLA Modules:
  0.0 69.0 jit_solution(1055273678600491502)
XLA Ops:
  0.0 2.5 %collective-permute-start = (bf16[64,64,128]{2,1,0:T(8,128)(2,1)}, bf16[64,64,128]{2,1,0:T(8,128)(2,1)S(1)}, u32[]{:S(2)}, u32[]{:S(2)}) collective-permute-start(bf16[64,64,128]{2,1,0:T(8,128)(2,1)} %own), channel_id=1, source_target_pairs={{0,1},{1,2},{2,3},{3,4},{4,5},{5,6},{6,7},{7,8},{8,9},{9,10},{10,1... | collective-permute-start | bytes 3145736 | tf_op jit(solution)/shard_map/ppermute | solution.py:347
  2.6 5.1 %moments.1 = (bf16[36,64,128]{2,1,0:T(8,128)(2,1)}, f32[64,64]{1,0:T(8,128)S(1)}) custom-call(bf16[64,64,128]{2,1,0:T(8,128)(2,1)} %own, bf16[64,64,128]{2,1,0:T(8,128)(2,1)} %basis.3, bf16[64,64,64]{2,1,0:T(8,128)(2,1)} %child.3, bf16[8,64,64]{2,1,0:T(8,128)(2,1)} %parent.3), custom_call_target="tpu_custom_call" | custom-call | tf_op jit(solution)/shard_map/moments/pallas_call | solution.py:75
  7.6 2.6 %collective-permute-start.1 = (f32[64,64]{1,0:T(8,128)S(1)}, f32[64,64]{1,0:T(8,128)S(1)}, u32[]{:S(2)}, u32[]{:S(2)}) collective-permute-start(f32[64,64]{1,0:T(8,128)S(1)} %get-tuple-element.24), channel_id=1, source_target_pairs={{0,1},{1,0},{2,3},{3,2},{4,5},{5,4},{6,7},{7,6},{8,9},{9,8},{10,11... | collective-permute-start | bytes 49160 | tf_op jit(solution)/shard_map/ppermute | solution.py:357
  10.2 0.9 %collective-permute-done.1.rest_0_ = f32[64,64]{1,0:T(8,128)S(1)} collective-permute-done((f32[64,64]{1,0:T(8,128)S(1)}, f32[64,64]{1,0:T(8,128)S(1)}, u32[]{:S(2)}, u32[]{:S(2)}) %collective-permute-start.1) | collective-permute-done | bytes 16416 | tf_op jit(solution)/shard_map/ppermute | solution.py:357
  11.1 1.4 %collective-permute-start.2 = (f32[64,64]{1,0:T(8,128)S(1)}, f32[64,64]{1,0:T(8,128)S(1)}, u32[]{:S(2)}, u32[]{:S(2)}) collective-permute-start(f32[64,64]{1,0:T(8,128)S(1)} %add.23), channel_id=1, source_target_pairs={{0,2},{1,3},{2,0},{3,1},{4,6},{5,7},{6,4},{7,5},{8,10},{9,11},{10,... | collective-permute-start | bytes 49160 | tf_op jit(solution)/shard_map/ppermute | solution.py:357
  12.5 0.0 copy-start.6
  12.5 0.0 copy-start.7
  12.5 0.0 copy-start.8
  12.6 5.5 %operator_table.2 = (bf16[316,64,64]{2,1,0:T(8,128)(2,1)}, f32[1,64,64]{2,1,0:T(8,128)S(1)}) custom-call(bf16[2,64,64,316]{3,2,1,0:T(8,128)(2,1)} %bitcast.15), custom_call_target="tpu_custom_call" | custom-call | tf_op jit(solution)/shard_map/operator_table/pallas_call | solution.py:147
  18.1 3.0 %collective-permute-start.3 = (f32[64,64]{1,0:T(8,128)S(1)}, f32[64,64]{1,0:T(8,128)S(1)}, u32[]{:S(2)}, u32[]{:S(2)}) collective-permute-start(f32[64,64]{1,0:T(8,128)S(1)} %get-tuple-element.43), channel_id=1, source_target_pairs={{0,4},{1,5},{2,6},{3,7},{4,0},{5,1},{6,2},{7,3},{8,12},{9,13},{10,... | collective-permute-start | bytes 49160 | tf_op jit(solution)/shard_map/ppermute | solution.py:357
  21.1 1.9 %collective-permute-done.3.rest_2_ = f32[64,64]{1,0:T(8,128)S(1)} collective-permute-done((f32[64,64]{1,0:T(8,128)S(1)}, f32[64,64]{1,0:T(8,128)S(1)}, u32[]{:S(2)}, u32[]{:S(2)}) %collective-permute-start.3) | collective-permute-done | bytes 16416 | tf_op jit(solution)/shard_map/ppermute | solution.py:357
  23.0 1.3 %collective-permute-start.6 = (bf16[36,64,128]{2,1,0:T(8,128)(2,1)S(1)}, bf16[36,64,128]{2,1,0:T(8,128)(2,1)S(1)}, u32[]{:S(2)}, u32[]{:S(2)}) collective-permute-start(bf16[36,64,128]{2,1,0:T(8,128)(2,1)S(1)} %copy-done.11), channel_id=1, source_target_pairs={{0,1},{1,2},{2,3},{3,4},{4,5},{5,6},{6,7},{7,8},{8,9},{9,10},{10,1... | collective-permute-start | bytes 1769480 | tf_op jit(solution)/shard_map/ppermute | solution.py:347
  24.3 1.3 %collective-permute-start.7 = (bf16[36,64,128]{2,1,0:T(8,128)(2,1)S(1)}, bf16[36,64,128]{2,1,0:T(8,128)(2,1)S(1)}, u32[]{:S(2)}, u32[]{:S(2)}) collective-permute-start(bf16[36,64,128]{2,1,0:T(8,128)(2,1)S(1)} %copy-done.11), channel_id=1, source_target_pairs={{1,0},{2,1},{3,2},{4,3},{5,4},{6,5},{7,6},{8,7},{9,8},{10,9},{11,1... | collective-permute-start | bytes 1769480 | tf_op jit(solution)/shard_map/ppermute | solution.py:352
  25.6 7.8 %collective-permute-start.4 = (f32[64,64]{1,0:T(8,128)S(1)}, f32[64,64]{1,0:T(8,128)S(1)}, u32[]{:S(2)}, u32[]{:S(2)}) collective-permute-start(f32[64,64]{1,0:T(8,128)S(1)} %add.27), channel_id=1, source_target_pairs={{0,8},{1,9},{2,10},{3,11},{4,12},{5,13},{6,14},{7,15},{8,0},{9,1},... | collective-permute-start | bytes 49160 | tf_op jit(solution)/shard_map/ppermute | solution.py:357
  33.4 5.9 %operator_table.3 = (bf16[316,64,64]{2,1,0:T(8,128)(2,1)}, f32[5,64,64]{2,1,0:T(8,128)S(1)}) custom-call(bf16[2,64,64,316]{3,2,1,0:T(8,128)(2,1)} %bitcast.16, f32[64,64]{1,0:T(8,128)S(1)} %copy-done.3, f32[64,64]{1,0:T(8,128)S(1)} %copy-done.4), custom_call_target="tpu_custom_call" | custom-call | tf_op jit(solution)/shard_map/operator_table/pallas_call | solution.py:147
  39.4 2.5 %collective-permute-done.4.rest_3_ = f32[64,64]{1,0:T(8,128)S(1)} collective-permute-done((f32[64,64]{1,0:T(8,128)S(1)}, f32[64,64]{1,0:T(8,128)S(1)}, u32[]{:S(2)}, u32[]{:S(2)}) %collective-permute-start.4) | collective-permute-done | bytes 16416 | tf_op jit(solution)/shard_map/ppermute | solution.py:357
  41.9 2.6 %collective-permute-start.5 = (f32[64,64]{1,0:T(8,128)S(1)}, f32[64,64]{1,0:T(8,128)S(1)}, u32[]{:S(2)}, u32[]{:S(2)}) collective-permute-start(f32[64,64]{1,0:T(8,128)S(1)} %add.28), channel_id=1, source_target_pairs={{0,16},{1,17},{2,18},{3,19},{4,20},{5,21},{6,22},{7,23},{8,24},{9,... | collective-permute-start | bytes 49160 | tf_op jit(solution)/shard_map/ppermute | solution.py:357
  44.5 2.2 %collective-permute-done.5.rest_4_ = f32[64,64]{1,0:T(8,128)S(1)} collective-permute-done((f32[64,64]{1,0:T(8,128)S(1)}, f32[64,64]{1,0:T(8,128)S(1)}, u32[]{:S(2)}, u32[]{:S(2)}) %collective-permute-start.5) | collective-permute-done | bytes 16416 | tf_op jit(solution)/shard_map/ppermute | solution.py:357
  46.7 0.9 %copy-done.12 = bf16[36,64,128]{2,1,0:T(8,128)(2,1)} copy-done((bf16[36,64,128]{2,1,0:T(8,128)(2,1)}, bf16[36,64,128]{2,1,0:T(8,128)(2,1)S(1)}, u32[]{:S(2)}) %copy-start.12) | copy-done | bytes 589848
  47.6 1.3 %collective-permute-start.8 = (bf16[64,64,128]{2,1,0:T(8,128)(2,1)}, bf16[64,64,128]{2,1,0:T(8,128)(2,1)}, u32[]{:S(2)}, u32[]{:S(2)}) collective-permute-start(bf16[64,64,128]{2,1,0:T(8,128)(2,1)} %own), channel_id=1, source_target_pairs={{1,0},{2,1},{3,2},{4,3},{5,4},{6,5},{7,6},{8,7},{9,8},{10,9},{11,1... | collective-permute-start | bytes 3145736 | tf_op jit(solution)/shard_map/ppermute | solution.py:352
  48.9 0.1 pad_add_fusion.base
  49.0 0.0 copy-start.9
  49.1 12.6 %far.1 = (f32[64,64,128]{2,1,0:T(8,128)S(1)}, bf16[64,6,128,128]{3,2,1,0:T(8,128)(2,1)S(1)}) custom-call(s32[2]{0:T(128)S(1)} %pad_add_fusion.base, s32[24,64]{1,0:T(8,128)S(1)} %bitcast.12, s32[24,64]{1,0:T(8,128)S(1)} %bitcast.13, s32[8,24]{1,0:T(8,128)S(1)} %copy-done.7, s32[8,24]{1,0:T(8,128)S(1)} %copy-done.8, bf16[36,64,128]{2,1,0:T(8,128)(2,1)} %copy-done.12, ...), custom_call_target="tpu_custom_call" | custom-call | tf_op jit(solution)/shard_map/far/pallas_call | solution.py:322
  61.6 7.4 %near.1 = f32[64,64,128]{2,1,0:T(8,128)} custom-call(s32[2]{0:T(128)S(1)} %pad_add_fusion.base, s32[6,64]{1,0:T(8,128)S(1)} %bitcast.14, bf16[64,64,128]{2,1,0:T(8,128)(2,1)} %copy-done.10, bf16[64,64,128]{2,1,0:T(8,128)(2,1)} %own, bf16[64,64,128]{2,1,0:T(8,128)(2,1)} %collective-permute-done.8.right, ...), custom_call_target="tpu_custom_call" | custom-call | tf_op jit(solution)/shard_map/near/pallas_call | solution.py:214
  (32 shorter events, 0.1 us)
Async XLA Ops:
  0.0 33.4 %copy-start.3 = (f32[64,64]{1,0:T(8,128)S(1)}, f32[64,64]{1,0:T(8,128)}, u32[]{:S(2)}) copy-start(f32[64,64]{1,0:T(8,128)} %refs_0_.1) | copy-start | bytes 49156
  0.0 33.4 %copy-start.4 = (f32[64,64]{1,0:T(8,128)S(1)}, f32[64,64]{1,0:T(8,128)}, u32[]{:S(2)}) copy-start(f32[64,64]{1,0:T(8,128)} %refs_1_.1) | copy-start | bytes 49156
  0.0 18.0 %collective-permute-start = (bf16[64,64,128]{2,1,0:T(8,128)(2,1)}, bf16[64,64,128]{2,1,0:T(8,128)(2,1)S(1)}, u32[]{:S(2)}, u32[]{:S(2)}) collective-permute-start(bf16[64,64,128]{2,1,0:T(8,128)(2,1)} %own), channel_id=1, source_target_pairs={{0,1},{1,2},{2,3},{3,4},{4,5},{5,6},{6,7},{7,8},{8,9},{9,10},{10,1... | collective-permute-start | bytes 3145736 | tf_op jit(solution)/shard_map/ppermute | solution.py:347
  7.6 15.3 %copy-start.11 = (bf16[36,64,128]{2,1,0:T(8,128)(2,1)S(1)}, bf16[36,64,128]{2,1,0:T(8,128)(2,1)}, u32[]{:S(2)}) copy-start(bf16[36,64,128]{2,1,0:T(8,128)(2,1)} %get-tuple-element.33.own) | copy-start | bytes 1769476
  7.6 3.4 %collective-permute-start.1 = (f32[64,64]{1,0:T(8,128)S(1)}, f32[64,64]{1,0:T(8,128)S(1)}, u32[]{:S(2)}, u32[]{:S(2)}) collective-permute-start(f32[64,64]{1,0:T(8,128)S(1)} %get-tuple-element.24), channel_id=1, source_target_pairs={{0,1},{1,0},{2,3},{3,2},{4,5},{5,4},{6,7},{7,6},{8,9},{9,8},{10,11... | collective-permute-start | bytes 49160 | tf_op jit(solution)/shard_map/ppermute | solution.py:357
  11.1 7.0 %collective-permute-start.2 = (f32[64,64]{1,0:T(8,128)S(1)}, f32[64,64]{1,0:T(8,128)S(1)}, u32[]{:S(2)}, u32[]{:S(2)}) collective-permute-start(f32[64,64]{1,0:T(8,128)S(1)} %add.23), channel_id=1, source_target_pairs={{0,2},{1,3},{2,0},{3,1},{4,6},{5,7},{6,4},{7,5},{8,10},{9,11},{10,... | collective-permute-start | bytes 49160 | tf_op jit(solution)/shard_map/ppermute | solution.py:357
  12.5 36.5 %copy-start = (bf16[64,64,128]{2,1,0:T(8,128)(2,1)S(1)}, bf16[64,64,128]{2,1,0:T(8,128)(2,1)}, u32[]{:S(2)}) copy-start(bf16[64,64,128]{2,1,0:T(8,128)(2,1)} %basis.3) | copy-start | bytes 3145732
  12.5 36.5 %copy-start.1 = (bf16[64,64,64]{2,1,0:T(8,128)(2,1)S(1)}, bf16[64,64,64]{2,1,0:T(8,128)(2,1)}, u32[]{:S(2)}) copy-start(bf16[64,64,64]{2,1,0:T(8,128)(2,1)} %child.3) | copy-start | bytes 1572868
  12.5 36.5 %copy-start.2 = (bf16[8,64,64]{2,1,0:T(8,128)(2,1)S(1)}, bf16[8,64,64]{2,1,0:T(8,128)(2,1)}, u32[]{:S(2)}) copy-start(bf16[8,64,64]{2,1,0:T(8,128)(2,1)} %parent.3) | copy-start | bytes 196612
  12.5 36.5 %copy-start.5 = (s32[64,24]{0,1:T(8,128)S(1)}, s32[64,24]{0,1:T(8,128)}, u32[]{:S(2)}) copy-start(s32[64,24]{0,1:T(8,128)} %param.20) | copy-start | bytes 18436
  12.5 36.5 %copy-start.6 = (s32[64,24]{0,1:T(8,128)S(1)}, s32[64,24]{0,1:T(8,128)}, u32[]{:S(2)}) copy-start(s32[64,24]{0,1:T(8,128)} %param.21) | copy-start | bytes 18436
  12.5 36.5 %copy-start.7 = (s32[8,24]{1,0:T(8,128)S(1)}, s32[8,24]{1,0:T(8,128)}, u32[]{:S(2)}) copy-start(s32[8,24]{1,0:T(8,128)} %list1.1) | copy-start | bytes 2308
  12.5 36.5 %copy-start.8 = (s32[8,24]{1,0:T(8,128)S(1)}, s32[8,24]{1,0:T(8,128)}, u32[]{:S(2)}) copy-start(s32[8,24]{1,0:T(8,128)} %op1.1) | copy-start | bytes 2308
  18.0 28.7 %copy-start.10 = (bf16[64,64,128]{2,1,0:T(8,128)(2,1)}, bf16[64,64,128]{2,1,0:T(8,128)(2,1)S(1)}, u32[]{:S(2)}) copy-start(bf16[64,64,128]{2,1,0:T(8,128)(2,1)S(1)} %collective-permute-done.left) | copy-start | bytes 3145732
  18.1 4.9 %collective-permute-start.3 = (f32[64,64]{1,0:T(8,128)S(1)}, f32[64,64]{1,0:T(8,128)S(1)}, u32[]{:S(2)}, u32[]{:S(2)}) collective-permute-start(f32[64,64]{1,0:T(8,128)S(1)} %get-tuple-element.43), channel_id=1, source_target_pairs={{0,4},{1,5},{2,6},{3,7},{4,0},{5,1},{6,2},{7,3},{8,12},{9,13},{10,... | collective-permute-start | bytes 49160 | tf_op jit(solution)/shard_map/ppermute | solution.py:357
  23.0 23.7 %collective-permute-start.6 = (bf16[36,64,128]{2,1,0:T(8,128)(2,1)S(1)}, bf16[36,64,128]{2,1,0:T(8,128)(2,1)S(1)}, u32[]{:S(2)}, u32[]{:S(2)}) collective-permute-start(bf16[36,64,128]{2,1,0:T(8,128)(2,1)S(1)} %copy-done.11), channel_id=1, source_target_pairs={{0,1},{1,2},{2,3},{3,4},{4,5},{5,6},{6,7},{7,8},{8,9},{9,10},{10,1... | collective-permute-start | bytes 1769480 | tf_op jit(solution)/shard_map/ppermute | solution.py:347
  24.3 22.4 %collective-permute-start.7 = (bf16[36,64,128]{2,1,0:T(8,128)(2,1)S(1)}, bf16[36,64,128]{2,1,0:T(8,128)(2,1)S(1)}, u32[]{:S(2)}, u32[]{:S(2)}) collective-permute-start(bf16[36,64,128]{2,1,0:T(8,128)(2,1)S(1)} %copy-done.11), channel_id=1, source_target_pairs={{1,0},{2,1},{3,2},{4,3},{5,4},{6,5},{7,6},{8,7},{9,8},{10,9},{11,1... | collective-permute-start | bytes 1769480 | tf_op jit(solution)/shard_map/ppermute | solution.py:352
  25.6 16.3 %collective-permute-start.4 = (f32[64,64]{1,0:T(8,128)S(1)}, f32[64,64]{1,0:T(8,128)S(1)}, u32[]{:S(2)}, u32[]{:S(2)}) collective-permute-start(f32[64,64]{1,0:T(8,128)S(1)} %add.27), channel_id=1, source_target_pairs={{0,8},{1,9},{2,10},{3,11},{4,12},{5,13},{6,14},{7,15},{8,0},{9,1},... | collective-permute-start | bytes 49160 | tf_op jit(solution)/shard_map/ppermute | solution.py:357
  41.9 4.8 %collective-permute-start.5 = (f32[64,64]{1,0:T(8,128)S(1)}, f32[64,64]{1,0:T(8,128)S(1)}, u32[]{:S(2)}, u32[]{:S(2)}) collective-permute-start(f32[64,64]{1,0:T(8,128)S(1)} %add.28), channel_id=1, source_target_pairs={{0,16},{1,17},{2,18},{3,19},{4,20},{5,21},{6,22},{7,23},{8,24},{9,... | collective-permute-start | bytes 49160 | tf_op jit(solution)/shard_map/ppermute | solution.py:357
  46.7 0.9 %copy-start.12 = (bf16[36,64,128]{2,1,0:T(8,128)(2,1)}, bf16[36,64,128]{2,1,0:T(8,128)(2,1)S(1)}, u32[]{:S(2)}) copy-start(bf16[36,64,128]{2,1,0:T(8,128)(2,1)S(1)} %collective-permute-done.6.left) | copy-start | bytes 1769476
  47.6 1.3 %copy-start.13 = (bf16[36,64,128]{2,1,0:T(8,128)(2,1)}, bf16[36,64,128]{2,1,0:T(8,128)(2,1)S(1)}, u32[]{:S(2)}) copy-start(bf16[36,64,128]{2,1,0:T(8,128)(2,1)S(1)} %collective-permute-done.7.right) | copy-start | bytes 1769476
  47.6 14.0 %collective-permute-start.8 = (bf16[64,64,128]{2,1,0:T(8,128)(2,1)}, bf16[64,64,128]{2,1,0:T(8,128)(2,1)}, u32[]{:S(2)}, u32[]{:S(2)}) collective-permute-start(bf16[64,64,128]{2,1,0:T(8,128)(2,1)} %own), channel_id=1, source_target_pairs={{1,0},{2,1},{3,2},{4,3},{5,4},{6,5},{7,6},{8,7},{9,8},{10,9},{11,1... | collective-permute-start | bytes 3145736 | tf_op jit(solution)/shard_map/ppermute | solution.py:352
  49.0 12.6 %copy-start.9 = (s32[64,6]{0,1:T(8,128)S(1)}, s32[64,6]{0,1:T(8,128)}, u32[]{:S(2)}) copy-start(s32[64,6]{0,1:T(8,128)} %param.15) | copy-start | bytes 4612

commit v8 on v7

--- a/solution.py
+++ b/solution.py
@@ -382,7 +382,7 @@
             leaf_ops, token = table_call(ops, 0, (), 1)
         if level == 2:
             total = after(total, charges_left)
-        if level == 3:
+        if level == 4:
             total, send, ops = tie((total, send, m2l_ops))
             moments_left = to_right(send)
             moments_right = to_left(send)
@@ -390,7 +390,7 @@
         partner = from_partner(total, level)
         if level == 1:
             partner = after(partner, token)
-        if level == 3:
+        if level == 4:
             partner, chain = tie((partner, chain))
         if level == height - 1:
             partner, charges, moments_left, moments_right = tie(

time: 70.4 us -> 70.4 us (level)
  the two profiles are of different devices: /device:TPU:0 before, /device:TPU:9 now
where the time goes in v8:
time: 70.4 us; the launch traced here: 70 us
  Pallas kernels  36.4 us (52%)
  starting transfers between devices  16.6 us (24%)
  waiting for transfers between devices  16.6 us (24%)
    pallas_call x1, Pallas kernels, far_call(): pl.pallas_call(far_kernel, in_specs=[SMEM] * 5 + [HBM] * 6 + [VMEM] * (4...  12.5 us
    pallas_call x2, Pallas kernels, table_call(): pl.pallas_call(functools.partial(table_kernel, level), in_specs=[HBM] + [...  11.4 us
    ppermute x5, waiting for transfers between devices, from_partner(): lax.ppermute(block, AXES, [(i, i ^ 1 << apart) for i in range(count)])  8.77 us
    ppermute x2, starting transfers between devices, to_right(): return lax.ppermute(block, AXES, [(i, i + 1) for i in range(count - 1)])  7.67 us
    pallas_call x1, Pallas kernels, near_call(): pl.pallas_call(near_kernel, in_specs=[SMEM, SMEM, HBM, HBM, HBM, VMEM, VM...  7.41 us
    ppermute x2, waiting for transfers between devices, to_left(): return lax.ppermute(block, AXES, [(i + 1, i) for i in range(count - 1)])  5.79 us
    pallas_call x1, Pallas kernels, moments_call(): pl.pallas_call(moments_kernel, grid=(steps,), in_specs=[pl.BlockSpec((16,...  5.08 us
    ppermute x2, starting transfers between devices, to_left(): return lax.ppermute(block, AXES, [(i + 1, i) for i in range(count - 1)])  5.06 us
  transfers between devices with their start and end apart: 9, of which 7 were waited for; matrix products, arithmetic and copies ran while one was open for 0% of the time, Pallas kernels for 41%

profile of v8, /device:TPU:9, one launch (start us, length us, event | category | flops | bytes accessed | tf_op | source)
XLA Modules:
  0.0 70.0 jit_solution(6504410844804373926)
XLA Ops:
  0.0 3.8 %collective-permute-start = (bf16[64,64,128]{2,1,0:T(8,128)(2,1)}, bf16[64,64,128]{2,1,0:T(8,128)(2,1)S(1)}, u32[]{:S(2)}, u32[]{:S(2)}) collective-permute-start(bf16[64,64,128]{2,1,0:T(8,128)(2,1)} %own), channel_id=1, source_target_pairs={{0,1},{1,2},{2,3},{3,4},{4,5},{5,6},{6,7},{7,8},{8,9},{9,10},{10,1... | collective-permute-start | bytes 3145736 | tf_op jit(solution)/shard_map/ppermute | solution.py:347
  3.8 5.1 %moments.1 = (bf16[36,64,128]{2,1,0:T(8,128)(2,1)}, f32[64,64]{1,0:T(8,128)S(1)}) custom-call(bf16[64,64,128]{2,1,0:T(8,128)(2,1)} %own, bf16[64,64,128]{2,1,0:T(8,128)(2,1)} %basis.3, bf16[64,64,64]{2,1,0:T(8,128)(2,1)} %child.3, bf16[8,64,64]{2,1,0:T(8,128)(2,1)} %parent.3), custom_call_target="tpu_custom_call" | custom-call | tf_op jit(solution)/shard_map/moments/pallas_call | solution.py:75
  8.9 1.2 %collective-permute-done.1.rest_0_ = f32[64,64]{1,0:T(8,128)S(1)} collective-permute-done((f32[64,64]{1,0:T(8,128)S(1)}, f32[64,64]{1,0:T(8,128)S(1)}, u32[]{:S(2)}, u32[]{:S(2)}) %collective-permute-start.1) | collective-permute-done | bytes 16416 | tf_op jit(solution)/shard_map/ppermute | solution.py:357
  10.1 1.2 %collective-permute-start.2 = (f32[64,64]{1,0:T(8,128)S(1)}, f32[64,64]{1,0:T(8,128)S(1)}, u32[]{:S(2)}, u32[]{:S(2)}) collective-permute-start(f32[64,64]{1,0:T(8,128)S(1)} %add.23), channel_id=1, source_target_pairs={{0,2},{1,3},{2,0},{3,1},{4,6},{5,7},{6,4},{7,5},{8,10},{9,11},{10,... | collective-permute-start | bytes 49160 | tf_op jit(solution)/shard_map/ppermute | solution.py:357
  11.3 0.0 copy-start.6
  11.3 0.0 copy-start.7
  11.3 0.0 copy-start.8
  11.3 5.5 %operator_table.2 = (bf16[316,64,64]{2,1,0:T(8,128)(2,1)}, f32[1,64,64]{2,1,0:T(8,128)S(1)}) custom-call(bf16[2,64,64,316]{3,2,1,0:T(8,128)(2,1)} %bitcast.15), custom_call_target="tpu_custom_call" | custom-call | tf_op jit(solution)/shard_map/operator_table/pallas_call | solution.py:147
  16.8 2.4 %collective-permute-done.2 = f32[64,64]{1,0:T(8,128)S(1)} collective-permute-done((f32[64,64]{1,0:T(8,128)S(1)}, f32[64,64]{1,0:T(8,128)S(1)}, u32[]{:S(2)}, u32[]{:S(2)}) %collective-permute-start.2) | collective-permute-done | bytes 16416 | tf_op jit(solution)/shard_map/ppermute | solution.py:357
  19.2 0.4 collective-permute-start.3
  19.6 2.5 %collective-permute-done.3.rest_2_ = f32[64,64]{1,0:T(8,128)S(1)} collective-permute-done((f32[64,64]{1,0:T(8,128)S(1)}, f32[64,64]{1,0:T(8,128)S(1)}, u32[]{:S(2)}, u32[]{:S(2)}) %collective-permute-start.3) | collective-permute-done | bytes 16416 | tf_op jit(solution)/shard_map/ppermute | solution.py:357
  22.0 2.8 %collective-permute-done.4.rest_3_ = f32[64,64]{1,0:T(8,128)S(1)} collective-permute-done((f32[64,64]{1,0:T(8,128)S(1)}, f32[64,64]{1,0:T(8,128)S(1)}, u32[]{:S(2)}, u32[]{:S(2)}) %collective-permute-start.4) | collective-permute-done | bytes 16416 | tf_op jit(solution)/shard_map/ppermute | solution.py:357
  24.8 3.8 %collective-permute-start.6 = (bf16[36,64,128]{2,1,0:T(8,128)(2,1)S(1)}, bf16[36,64,128]{2,1,0:T(8,128)(2,1)S(1)}, u32[]{:S(2)}, u32[]{:S(2)}) collective-permute-start(bf16[36,64,128]{2,1,0:T(8,128)(2,1)S(1)} %copy-done.11), channel_id=1, source_target_pairs={{0,1},{1,2},{2,3},{3,4},{4,5},{5,6},{6,7},{7,8},{8,9},{9,10},{10,1... | collective-permute-start | bytes 1769480 | tf_op jit(solution)/shard_map/ppermute | solution.py:347
  28.7 2.7 %collective-permute-start.7 = (bf16[36,64,128]{2,1,0:T(8,128)(2,1)S(1)}, bf16[36,64,128]{2,1,0:T(8,128)(2,1)S(1)}, u32[]{:S(2)}, u32[]{:S(2)}) collective-permute-start(bf16[36,64,128]{2,1,0:T(8,128)(2,1)S(1)} %copy-done.11), channel_id=1, source_target_pairs={{1,0},{2,1},{3,2},{4,3},{5,4},{6,5},{7,6},{8,7},{9,8},{10,9},{11,1... | collective-permute-start | bytes 1769480 | tf_op jit(solution)/shard_map/ppermute | solution.py:352
  31.4 2.4 %collective-permute-start.5 = (f32[64,64]{1,0:T(8,128)S(1)}, f32[64,64]{1,0:T(8,128)S(1)}, u32[]{:S(2)}, u32[]{:S(2)}) collective-permute-start(f32[64,64]{1,0:T(8,128)S(1)} %add.28), channel_id=1, source_target_pairs={{0,16},{1,17},{2,18},{3,19},{4,20},{5,21},{6,22},{7,23},{8,24},{9,... | collective-permute-start | bytes 49160 | tf_op jit(solution)/shard_map/ppermute | solution.py:357
  33.8 5.9 %operator_table.3 = (bf16[316,64,64]{2,1,0:T(8,128)(2,1)}, f32[5,64,64]{2,1,0:T(8,128)S(1)}) custom-call(bf16[2,64,64,316]{3,2,1,0:T(8,128)(2,1)} %bitcast.16, f32[64,64]{1,0:T(8,128)S(1)} %copy-done.3, f32[64,64]{1,0:T(8,128)S(1)} %copy-done.4), custom_call_target="tpu_custom_call" | custom-call | tf_op jit(solution)/shard_map/operator_table/pallas_call | solution.py:147
  39.8 2.0 %collective-permute-done.6.left = bf16[36,64,128]{2,1,0:T(8,128)(2,1)S(1)} collective-permute-done((bf16[36,64,128]{2,1,0:T(8,128)(2,1)S(1)}, bf16[36,64,128]{2,1,0:T(8,128)(2,1)S(1)}, u32[]{:S(2)}, u32[]{:S(2)}) %collective-permute-start.6) | collective-permute-done | bytes 589856 | tf_op jit(solution)/shard_map/ppermute | solution.py:347
  41.8 4.4 %collective-permute-done.7.right = bf16[36,64,128]{2,1,0:T(8,128)(2,1)S(1)} collective-permute-done((bf16[36,64,128]{2,1,0:T(8,128)(2,1)S(1)}, bf16[36,64,128]{2,1,0:T(8,128)(2,1)S(1)}, u32[]{:S(2)}, u32[]{:S(2)}) %collective-permute-start.7) | collective-permute-done | bytes 589856 | tf_op jit(solution)/shard_map/ppermute | solution.py:352
  46.2 2.3 %collective-permute-start.8 = (bf16[64,64,128]{2,1,0:T(8,128)(2,1)}, bf16[64,64,128]{2,1,0:T(8,128)(2,1)}, u32[]{:S(2)}, u32[]{:S(2)}) collective-permute-start(bf16[64,64,128]{2,1,0:T(8,128)(2,1)} %own), channel_id=1, source_target_pairs={{1,0},{2,1},{3,2},{4,3},{5,4},{6,5},{7,6},{8,7},{9,8},{10,9},{11,1... | collective-permute-start | bytes 3145736 | tf_op jit(solution)/shard_map/ppermute | solution.py:352
  48.5 0.1 pad_add_fusion.base
  48.7 0.0 copy-start.9
  48.7 12.5 %far.1 = (f32[64,64,128]{2,1,0:T(8,128)S(1)}, bf16[64,6,128,128]{3,2,1,0:T(8,128)(2,1)S(1)}) custom-call(s32[2]{0:T(128)S(1)} %pad_add_fusion.base, s32[24,64]{1,0:T(8,128)S(1)} %bitcast.12, s32[24,64]{1,0:T(8,128)S(1)} %bitcast.13, s32[8,24]{1,0:T(8,128)S(1)} %copy-done.7, s32[8,24]{1,0:T(8,128)S(1)} %copy-done.8, bf16[36,64,128]{2,1,0:T(8,128)(2,1)} %copy-done.12, ...), custom_call_target="tpu_custom_call" | custom-call | tf_op jit(solution)/shard_map/far/pallas_call | solution.py:322
  61.2 1.4 %collective-permute-done.8.right = bf16[64,64,128]{2,1,0:T(8,128)(2,1)} collective-permute-done((bf16[64,64,128]{2,1,0:T(8,128)(2,1)}, bf16[64,64,128]{2,1,0:T(8,128)(2,1)}, u32[]{:S(2)}, u32[]{:S(2)}) %collective-permute-start.8) | collective-permute-done | bytes 1048608 | tf_op jit(solution)/shard_map/ppermute | solution.py:352
  62.6 7.4 %near.1 = f32[64,64,128]{2,1,0:T(8,128)} custom-call(s32[2]{0:T(128)S(1)} %pad_add_fusion.base, s32[6,64]{1,0:T(8,128)S(1)} %bitcast.14, bf16[64,64,128]{2,1,0:T(8,128)(2,1)} %copy-done.10, bf16[64,64,128]{2,1,0:T(8,128)(2,1)} %own, bf16[64,64,128]{2,1,0:T(8,128)(2,1)} %collective-permute-done.8.right, ...), custom_call_target="tpu_custom_call" | custom-call | tf_op jit(solution)/shard_map/near/pallas_call | solution.py:214
  (32 shorter events, 0.1 us)
Async XLA Ops:
  0.0 33.8 %copy-start.3 = (f32[64,64]{1,0:T(8,128)S(1)}, f32[64,64]{1,0:T(8,128)}, u32[]{:S(2)}) copy-start(f32[64,64]{1,0:T(8,128)} %refs_0_.1) | copy-start | bytes 49156
  0.0 33.8 %copy-start.4 = (f32[64,64]{1,0:T(8,128)S(1)}, f32[64,64]{1,0:T(8,128)}, u32[]{:S(2)}) copy-start(f32[64,64]{1,0:T(8,128)} %refs_1_.1) | copy-start | bytes 49156
  0.0 19.2 %collective-permute-start = (bf16[64,64,128]{2,1,0:T(8,128)(2,1)}, bf16[64,64,128]{2,1,0:T(8,128)(2,1)S(1)}, u32[]{:S(2)}, u32[]{:S(2)}) collective-permute-start(bf16[64,64,128]{2,1,0:T(8,128)(2,1)} %own), channel_id=1, source_target_pairs={{0,1},{1,2},{2,3},{3,4},{4,5},{5,6},{6,7},{7,8},{8,9},{9,10},{10,1... | collective-permute-start | bytes 3145736 | tf_op jit(solution)/shard_map/ppermute | solution.py:347
  8.9 15.9 %copy-start.11 = (bf16[36,64,128]{2,1,0:T(8,128)(2,1)S(1)}, bf16[36,64,128]{2,1,0:T(8,128)(2,1)}, u32[]{:S(2)}) copy-start(bf16[36,64,128]{2,1,0:T(8,128)(2,1)} %get-tuple-element.33.own) | copy-start | bytes 1769476
  8.9 1.2 %collective-permute-start.1 = (f32[64,64]{1,0:T(8,128)S(1)}, f32[64,64]{1,0:T(8,128)S(1)}, u32[]{:S(2)}, u32[]{:S(2)}) collective-permute-start(f32[64,64]{1,0:T(8,128)S(1)} %get-tuple-element.24), channel_id=1, source_target_pairs={{0,1},{1,0},{2,3},{3,2},{4,5},{5,4},{6,7},{7,6},{8,9},{9,8},{10,11... | collective-permute-start | bytes 49160 | tf_op jit(solution)/shard_map/ppermute | solution.py:357
  10.1 9.0 %collective-permute-start.2 = (f32[64,64]{1,0:T(8,128)S(1)}, f32[64,64]{1,0:T(8,128)S(1)}, u32[]{:S(2)}, u32[]{:S(2)}) collective-permute-start(f32[64,64]{1,0:T(8,128)S(1)} %add.23), channel_id=1, source_target_pairs={{0,2},{1,3},{2,0},{3,1},{4,6},{5,7},{6,4},{7,5},{8,10},{9,11},{10,... | collective-permute-start | bytes 49160 | tf_op jit(solution)/shard_map/ppermute | solution.py:357
  11.3 37.3 %copy-start = (bf16[64,64,128]{2,1,0:T(8,128)(2,1)S(1)}, bf16[64,64,128]{2,1,0:T(8,128)(2,1)}, u32[]{:S(2)}) copy-start(bf16[64,64,128]{2,1,0:T(8,128)(2,1)} %basis.3) | copy-start | bytes 3145732
  11.3 37.3 %copy-start.1 = (bf16[64,64,64]{2,1,0:T(8,128)(2,1)S(1)}, bf16[64,64,64]{2,1,0:T(8,128)(2,1)}, u32[]{:S(2)}) copy-start(bf16[64,64,64]{2,1,0:T(8,128)(2,1)} %child.3) | copy-start | bytes 1572868
  11.3 37.3 %copy-start.2 = (bf16[8,64,64]{2,1,0:T(8,128)(2,1)S(1)}, bf16[8,64,64]{2,1,0:T(8,128)(2,1)}, u32[]{:S(2)}) copy-start(bf16[8,64,64]{2,1,0:T(8,128)(2,1)} %parent.3) | copy-start | bytes 196612
  11.3 37.3 %copy-start.5 = (s32[64,24]{0,1:T(8,128)S(1)}, s32[64,24]{0,1:T(8,128)}, u32[]{:S(2)}) copy-start(s32[64,24]{0,1:T(8,128)} %param.20) | copy-start | bytes 18436
  11.3 37.3 %copy-start.6 = (s32[64,24]{0,1:T(8,128)S(1)}, s32[64,24]{0,1:T(8,128)}, u32[]{:S(2)}) copy-start(s32[64,24]{0,1:T(8,128)} %param.21) | copy-start | bytes 18436
  11.3 37.3 %copy-start.7 = (s32[8,24]{1,0:T(8,128)S(1)}, s32[8,24]{1,0:T(8,128)}, u32[]{:S(2)}) copy-start(s32[8,24]{1,0:T(8,128)} %list1.1) | copy-start | bytes 2308
  11.3 37.3 %copy-start.8 = (s32[8,24]{1,0:T(8,128)S(1)}, s32[8,24]{1,0:T(8,128)}, u32[]{:S(2)}) copy-start(s32[8,24]{1,0:T(8,128)} %op1.1) | copy-start | bytes 2308
  19.2 20.6 %copy-start.10 = (bf16[64,64,128]{2,1,0:T(8,128)(2,1)}, bf16[64,64,128]{2,1,0:T(8,128)(2,1)S(1)}, u32[]{:S(2)}) copy-start(bf16[64,64,128]{2,1,0:T(8,128)(2,1)S(1)} %collective-permute-done.left) | copy-start | bytes 3145732
  19.2 2.8 %collective-permute-start.3 = (f32[64,64]{1,0:T(8,128)S(1)}, f32[64,64]{1,0:T(8,128)S(1)}, u32[]{:S(2)}, u32[]{:S(2)}) collective-permute-start(f32[64,64]{1,0:T(8,128)S(1)} %get-tuple-element.43), channel_id=1, source_target_pairs={{0,4},{1,5},{2,6},{3,7},{4,0},{5,1},{6,2},{7,3},{8,12},{9,13},{10,... | collective-permute-start | bytes 49160 | tf_op jit(solution)/shard_map/ppermute | solution.py:357
  22.0 2.8 %collective-permute-start.4 = (f32[64,64]{1,0:T(8,128)S(1)}, f32[64,64]{1,0:T(8,128)S(1)}, u32[]{:S(2)}, u32[]{:S(2)}) collective-permute-start(f32[64,64]{1,0:T(8,128)S(1)} %add.27), channel_id=1, source_target_pairs={{0,8},{1,9},{2,10},{3,11},{4,12},{5,13},{6,14},{7,15},{8,0},{9,1},... | collective-permute-start | bytes 49160 | tf_op jit(solution)/shard_map/ppermute | solution.py:357
  24.8 17.0 %collective-permute-start.6 = (bf16[36,64,128]{2,1,0:T(8,128)(2,1)S(1)}, bf16[36,64,128]{2,1,0:T(8,128)(2,1)S(1)}, u32[]{:S(2)}, u32[]{:S(2)}) collective-permute-start(bf16[36,64,128]{2,1,0:T(8,128)(2,1)S(1)} %copy-done.11), channel_id=1, source_target_pairs={{0,1},{1,2},{2,3},{3,4},{4,5},{5,6},{6,7},{7,8},{8,9},{9,10},{10,1... | collective-permute-start | bytes 1769480 | tf_op jit(solution)/shard_map/ppermute | solution.py:347
  28.7 17.5 %collective-permute-start.7 = (bf16[36,64,128]{2,1,0:T(8,128)(2,1)S(1)}, bf16[36,64,128]{2,1,0:T(8,128)(2,1)S(1)}, u32[]{:S(2)}, u32[]{:S(2)}) collective-permute-start(bf16[36,64,128]{2,1,0:T(8,128)(2,1)S(1)} %copy-done.11), channel_id=1, source_target_pairs={{1,0},{2,1},{3,2},{4,3},{5,4},{6,5},{7,6},{8,7},{9,8},{10,9},{11,1... | collective-permute-start | bytes 1769480 | tf_op jit(solution)/shard_map/ppermute | solution.py:352
  31.4 8.3 %collective-permute-start.5 = (f32[64,64]{1,0:T(8,128)S(1)}, f32[64,64]{1,0:T(8,128)S(1)}, u32[]{:S(2)}, u32[]{:S(2)}) collective-permute-start(f32[64,64]{1,0:T(8,128)S(1)} %add.28), channel_id=1, source_target_pairs={{0,16},{1,17},{2,18},{3,19},{4,20},{5,21},{6,22},{7,23},{8,24},{9,... | collective-permute-start | bytes 49160 | tf_op jit(solution)/shard_map/ppermute | solution.py:357
  41.8 4.4 %copy-start.12 = (bf16[36,64,128]{2,1,0:T(8,128)(2,1)}, bf16[36,64,128]{2,1,0:T(8,128)(2,1)S(1)}, u32[]{:S(2)}) copy-start(bf16[36,64,128]{2,1,0:T(8,128)(2,1)S(1)} %collective-permute-done.6.left) | copy-start | bytes 1769476
  46.2 2.3 %copy-start.13 = (bf16[36,64,128]{2,1,0:T(8,128)(2,1)}, bf16[36,64,128]{2,1,0:T(8,128)(2,1)S(1)}, u32[]{:S(2)}) copy-start(bf16[36,64,128]{2,1,0:T(8,128)(2,1)S(1)} %collective-permute-done.7.right) | copy-start | bytes 1769476
  46.2 16.4 %collective-permute-start.8 = (bf16[64,64,128]{2,1,0:T(8,128)(2,1)}, bf16[64,64,128]{2,1,0:T(8,128)(2,1)}, u32[]{:S(2)}, u32[]{:S(2)}) collective-permute-start(bf16[64,64,128]{2,1,0:T(8,128)(2,1)} %own), channel_id=1, source_target_pairs={{1,0},{2,1},{3,2},{4,3},{5,4},{6,5},{7,6},{8,7},{9,8},{10,9},{11,1... | collective-permute-start | bytes 3145736 | tf_op jit(solution)/shard_map/ppermute | solution.py:352
  48.7 14.0 %copy-start.9 = (s32[64,6]{0,1:T(8,128)S(1)}, s32[64,6]{0,1:T(8,128)}, u32[]{:S(2)}) copy-start(s32[64,6]{0,1:T(8,128)} %param.15) | copy-start | bytes 4612

commit v9 on v8

--- a/solution.py
+++ b/solution.py
@@ -130,7 +130,9 @@
         size = min(OPS_BLOCK, count - first)
         for o in range(first, first + size):
             rows = turned[pl.ds(o, half, stride=stride), :]
-            turned_back[o] = jnp.concatenate([rows[:, :rank], rows[:, rank:]], axis=0).astype(bf16)
+            if turned_back.shape[1] == rank:
+                rows = jnp.concatenate([rows[:, :rank], rows[:, rank:]], axis=0)
+            turned_back[o] = rows.astype(bf16)
         block = pl.ds(first, size)
         copies.append(
             pltpu.make_async_copy(turned_back.at[block], table.at[block], out_sems.at[first // OPS_BLOCK])
@@ -140,8 +142,9 @@
         copy.wait()
 
 
-def table_call(ops, level, top, links):
+def table_call(ops, level, packed, top, links):
     _, count, rank, _ = ops.shape
+    shape = (count, rank // 2, 2 * rank) if packed else (count, rank, rank)
     stride = pl.cdiv(count, 8) * 8
     stride += 8 * (stride // 8 % 2 == 0)
     return pl.pallas_call(
@@ -149,13 +152,13 @@
         in_specs=[HBM] + [VMEM for _ in top],
         out_specs=[HBM, VMEM],
         out_shape=[
-            pltpu.HBM((count, rank, rank), bf16),
+            pltpu.HBM(shape, bf16),
             jax.ShapeDtypeStruct((links, rank, rank), f32),
         ],
         scratch_shapes=[
             pltpu.VMEM((rank, rank, count), bf16),
             pltpu.VMEM((rank // 2 * stride, 2 * rank), f32),
-            pltpu.VMEM((count, rank, rank), bf16),
+            pltpu.VMEM(shape, bf16),
             pltpu.SemaphoreType.DMA((4,)),
             pltpu.SemaphoreType.DMA((pl.cdiv(count, OPS_BLOCK),)),
         ],
@@ -239,7 +242,11 @@
         lhs = jnp.concatenate(
             [jnp.where(low, picked[0], picked[1]), jnp.where(low, picked[2], picked[3])], axis=1
         )
-        rhs = jnp.concatenate([table[ops[at[e + i]]] for i in range(4)], axis=0)
+        parts = [table[ops[at[e + i]]] for i in range(4)]
+        rank = acc.shape[1]
+        if parts[0].shape[0] < rank:
+            parts = [half for t in parts for half in (t[:, :rank], t[:, rank:])]
+        rhs = jnp.concatenate(parts, axis=0)
         acc = acc + mm(lhs, rhs)
     return acc
 
@@ -379,14 +386,14 @@
     for level in range(height):
         if level == 1:
             total, ops = tie((total, m2l_ops))
-            leaf_ops, token = table_call(ops, 0, (), 1)
+            parent_ops, token = table_call(ops, 1, True, (), 1)
         if level == 2:
             total = after(total, charges_left)
         if level == 4:
             total, send, ops = tie((total, send, m2l_ops))
             moments_left = to_right(send)
             moments_right = to_left(send)
-            parent_ops, chain = table_call(ops, 1, (top_transfer, top_couple), height)
+            leaf_ops, chain = table_call(ops, 0, False, (top_transfer, top_couple), height)
         partner = from_partner(total, level)
         if level == 1:
             partner = after(partner, token)

time: 70.4 us -> 70.4 us (level)
  waiting for transfers between devices: 16.6 us -> 18.8 us
  Pallas kernels: 36.4 us -> 34.3 us
    pallas_call x2, Pallas kernels: 11.4 us -> 9.92 us  [table_call(): pl.pallas_call(functools.partial(table_kernel, level), in_specs=[HBM] + [...]
    ppermute x5, waiting for transfers between devices: 8.77 us -> 9.71 us  [from_partner(): lax.ppermute(block, AXES, [(i, i ^ 1 << apart) for i in range(count)])]
    ppermute x2, waiting for transfers between devices: 5.79 us -> 6.54 us  [to_left(): return lax.ppermute(block, AXES, [(i + 1, i) for i in range(count - 1)])]
  transfers between devices with their start and end apart: 9 -> 9, of which waited for: 7 -> 7; matrix products, arithmetic and copies ran while one was open for 0% -> 0% of each run, Pallas kernels for 41% -> 38%
where the time goes in v9:
time: 70.4 us; the launch traced here: 70 us
  Pallas kernels  34.3 us (49%)
  waiting for transfers between devices  18.8 us (27%)
  starting transfers between devices  16.6 us (24%)
    pallas_call x1, Pallas kernels, far_call(): pl.pallas_call(far_kernel, in_specs=[SMEM] * 5 + [HBM] * 6 + [VMEM] * (4...  11.8 us
    pallas_call x2, Pallas kernels, table_call(): pl.pallas_call(functools.partial(table_kernel, level), in_specs=[HBM] + [...  9.92 us
    ppermute x5, waiting for transfers between devices, from_partner(): lax.ppermute(block, AXES, [(i, i ^ 1 << apart) for i in range(count)])  9.71 us
    ppermute x2, starting transfers between devices, to_right(): return lax.ppermute(block, AXES, [(i, i + 1) for i in range(count - 1)])  7.67 us
    pallas_call x1, Pallas kernels, near_call(): pl.pallas_call(near_kernel, in_specs=[SMEM, SMEM, HBM, HBM, HBM, VMEM, VM...  7.41 us
    ppermute x2, waiting for transfers between devices, to_left(): return lax.ppermute(block, AXES, [(i + 1, i) for i in range(count - 1)])  6.54 us
    pallas_call x1, Pallas kernels, moments_call(): pl.pallas_call(moments_kernel, grid=(steps,), in_specs=[pl.BlockSpec((16,...  5.08 us
    ppermute x2, starting transfers between devices, to_left(): return lax.ppermute(block, AXES, [(i + 1, i) for i in range(count - 1)])  5.01 us
  transfers between devices with their start and end apart: 9, of which 7 were waited for; matrix products, arithmetic and copies ran while one was open for 0% of the time, Pallas kernels for 38%

profile of v9, /device:TPU:9, one launch (start us, length us, event | category | flops | bytes accessed | tf_op | source)
XLA Modules:
  0.0 70.0 jit_solution(13147384109539851110)
XLA Ops:
  0.0 3.8 %collective-permute-start = (bf16[64,64,128]{2,1,0:T(8,128)(2,1)}, bf16[64,64,128]{2,1,0:T(8,128)(2,1)S(1)}, u32[]{:S(2)}, u32[]{:S(2)}) collective-permute-start(bf16[64,64,128]{2,1,0:T(8,128)(2,1)} %own), channel_id=1, source_target_pairs={{0,1},{1,2},{2,3},{3,4},{4,5},{5,6},{6,7},{7,8},{8,9},{9,10},{10,1... | collective-permute-start | bytes 3145736 | tf_op jit(solution)/shard_map/ppermute | solution.py:354
  3.8 5.1 %moments.1 = (bf16[36,64,128]{2,1,0:T(8,128)(2,1)}, f32[64,64]{1,0:T(8,128)S(1)}) custom-call(bf16[64,64,128]{2,1,0:T(8,128)(2,1)} %own, bf16[64,64,128]{2,1,0:T(8,128)(2,1)} %basis.3, bf16[64,64,64]{2,1,0:T(8,128)(2,1)} %child.3, bf16[8,64,64]{2,1,0:T(8,128)(2,1)} %parent.3), custom_call_target="tpu_custom_call" | custom-call | tf_op jit(solution)/shard_map/moments/pallas_call | solution.py:75
  8.9 1.2 %collective-permute-done.1.rest_0_ = f32[64,64]{1,0:T(8,128)S(1)} collective-permute-done((f32[64,64]{1,0:T(8,128)S(1)}, f32[64,64]{1,0:T(8,128)S(1)}, u32[]{:S(2)}, u32[]{:S(2)}) %collective-permute-start.1) | collective-permute-done | bytes 16416 | tf_op jit(solution)/shard_map/ppermute | solution.py:364
  10.1 1.2 %collective-permute-start.2 = (f32[64,64]{1,0:T(8,128)S(1)}, f32[64,64]{1,0:T(8,128)S(1)}, u32[]{:S(2)}, u32[]{:S(2)}) collective-permute-start(f32[64,64]{1,0:T(8,128)S(1)} %add.23), channel_id=1, source_target_pairs={{0,2},{1,3},{2,0},{3,1},{4,6},{5,7},{6,4},{7,5},{8,10},{9,11},{10,... | collective-permute-start | bytes 49160 | tf_op jit(solution)/shard_map/ppermute | solution.py:364
  11.3 0.0 copy-start.6
  11.3 0.0 copy-start.8
  11.3 0.0 copy-start.9
  11.3 4.5 %operator_table.2 = (bf16[316,32,128]{2,1,0:T(8,128)(2,1)}, f32[1,64,64]{2,1,0:T(8,128)S(1)}) custom-call(bf16[2,64,64,316]{3,2,1,0:T(8,128)(2,1)} %bitcast.15), custom_call_target="tpu_custom_call" | custom-call | tf_op jit(solution)/shard_map/operator_table/pallas_call | solution.py:150
  15.9 3.3 %collective-permute-done.2 = f32[64,64]{1,0:T(8,128)S(1)} collective-permute-done((f32[64,64]{1,0:T(8,128)S(1)}, f32[64,64]{1,0:T(8,128)S(1)}, u32[]{:S(2)}, u32[]{:S(2)}) %collective-permute-start.2) | collective-permute-done | bytes 16416 | tf_op jit(solution)/shard_map/ppermute | solution.py:364
  19.2 0.4 collective-permute-start.3
  19.6 2.5 %collective-permute-done.3.rest_2_ = f32[64,64]{1,0:T(8,128)S(1)} collective-permute-done((f32[64,64]{1,0:T(8,128)S(1)}, f32[64,64]{1,0:T(8,128)S(1)}, u32[]{:S(2)}, u32[]{:S(2)}) %collective-permute-start.3) | collective-permute-done | bytes 16416 | tf_op jit(solution)/shard_map/ppermute | solution.py:364
  22.0 2.8 %collective-permute-done.4.rest_3_ = f32[64,64]{1,0:T(8,128)S(1)} collective-permute-done((f32[64,64]{1,0:T(8,128)S(1)}, f32[64,64]{1,0:T(8,128)S(1)}, u32[]{:S(2)}, u32[]{:S(2)}) %collective-permute-start.4) | collective-permute-done | bytes 16416 | tf_op jit(solution)/shard_map/ppermute | solution.py:364
  24.8 3.8 %collective-permute-start.6 = (bf16[36,64,128]{2,1,0:T(8,128)(2,1)S(1)}, bf16[36,64,128]{2,1,0:T(8,128)(2,1)S(1)}, u32[]{:S(2)}, u32[]{:S(2)}) collective-permute-start(bf16[36,64,128]{2,1,0:T(8,128)(2,1)S(1)} %copy-done.11), channel_id=1, source_target_pairs={{0,1},{1,2},{2,3},{3,4},{4,5},{5,6},{6,7},{7,8},{8,9},{9,10},{10,1... | collective-permute-start | bytes 1769480 | tf_op jit(solution)/shard_map/ppermute | solution.py:354
  28.7 2.7 %collective-permute-start.7 = (bf16[36,64,128]{2,1,0:T(8,128)(2,1)S(1)}, bf16[36,64,128]{2,1,0:T(8,128)(2,1)S(1)}, u32[]{:S(2)}, u32[]{:S(2)}) collective-permute-start(bf16[36,64,128]{2,1,0:T(8,128)(2,1)S(1)} %copy-done.11), channel_id=1, source_target_pairs={{1,0},{2,1},{3,2},{4,3},{5,4},{6,5},{7,6},{8,7},{9,8},{10,9},{11,1... | collective-permute-start | bytes 1769480 | tf_op jit(solution)/shard_map/ppermute | solution.py:359
  31.4 2.4 %collective-permute-start.5 = (f32[64,64]{1,0:T(8,128)S(1)}, f32[64,64]{1,0:T(8,128)S(1)}, u32[]{:S(2)}, u32[]{:S(2)}) collective-permute-start(f32[64,64]{1,0:T(8,128)S(1)} %add.28), channel_id=1, source_target_pairs={{0,16},{1,17},{2,18},{3,19},{4,20},{5,21},{6,22},{7,23},{8,24},{9,... | collective-permute-start | bytes 49160 | tf_op jit(solution)/shard_map/ppermute | solution.py:364
  33.8 5.4 %operator_table.3 = (bf16[316,64,64]{2,1,0:T(8,128)(2,1)}, f32[5,64,64]{2,1,0:T(8,128)S(1)}) custom-call(bf16[2,64,64,316]{3,2,1,0:T(8,128)(2,1)} %bitcast.16, f32[64,64]{1,0:T(8,128)S(1)} %copy-done.3, f32[64,64]{1,0:T(8,128)S(1)} %copy-done.4), custom_call_target="tpu_custom_call" | custom-call | tf_op jit(solution)/shard_map/operator_table/pallas_call | solution.py:150
  39.2 2.6 %collective-permute-done.6.left = bf16[36,64,128]{2,1,0:T(8,128)(2,1)S(1)} collective-permute-done((bf16[36,64,128]{2,1,0:T(8,128)(2,1)S(1)}, bf16[36,64,128]{2,1,0:T(8,128)(2,1)S(1)}, u32[]{:S(2)}, u32[]{:S(2)}) %collective-permute-start.6) | collective-permute-done | bytes 589856 | tf_op jit(solution)/shard_map/ppermute | solution.py:354
  41.8 4.4 %collective-permute-done.7.right = bf16[36,64,128]{2,1,0:T(8,128)(2,1)S(1)} collective-permute-done((bf16[36,64,128]{2,1,0:T(8,128)(2,1)S(1)}, bf16[36,64,128]{2,1,0:T(8,128)(2,1)S(1)}, u32[]{:S(2)}, u32[]{:S(2)}) %collective-permute-start.7) | collective-permute-done | bytes 589856 | tf_op jit(solution)/shard_map/ppermute | solution.py:359
  46.2 2.3 %collective-permute-start.8 = (bf16[64,64,128]{2,1,0:T(8,128)(2,1)}, bf16[64,64,128]{2,1,0:T(8,128)(2,1)}, u32[]{:S(2)}, u32[]{:S(2)}) collective-permute-start(bf16[64,64,128]{2,1,0:T(8,128)(2,1)} %own), channel_id=1, source_target_pairs={{1,0},{2,1},{3,2},{4,3},{5,4},{6,5},{7,6},{8,7},{9,8},{10,9},{11,1... | collective-permute-start | bytes 3145736 | tf_op jit(solution)/shard_map/ppermute | solution.py:359
  48.5 0.1 pad_add_fusion.base
  48.6 0.0 copy-start.7
  48.6 11.8 %far.1 = (f32[64,64,128]{2,1,0:T(8,128)S(1)}, bf16[64,6,128,128]{3,2,1,0:T(8,128)(2,1)S(1)}) custom-call(s32[2]{0:T(128)S(1)} %pad_add_fusion.base, s32[24,64]{1,0:T(8,128)S(1)} %bitcast.12, s32[24,64]{1,0:T(8,128)S(1)} %bitcast.13, s32[8,24]{1,0:T(8,128)S(1)} %copy-done.8, s32[8,24]{1,0:T(8,128)S(1)} %copy-done.9, bf16[36,64,128]{2,1,0:T(8,128)(2,1)} %copy-done.12, ...), custom_call_target="tpu_custom_call" | custom-call | tf_op jit(solution)/shard_map/far/pallas_call | solution.py:329
  60.5 2.1 %collective-permute-done.8.right = bf16[64,64,128]{2,1,0:T(8,128)(2,1)} collective-permute-done((bf16[64,64,128]{2,1,0:T(8,128)(2,1)}, bf16[64,64,128]{2,1,0:T(8,128)(2,1)}, u32[]{:S(2)}, u32[]{:S(2)}) %collective-permute-start.8) | collective-permute-done | bytes 1048608 | tf_op jit(solution)/shard_map/ppermute | solution.py:359
  62.6 7.4 %near.1 = f32[64,64,128]{2,1,0:T(8,128)} custom-call(s32[2]{0:T(128)S(1)} %pad_add_fusion.base, s32[6,64]{1,0:T(8,128)S(1)} %bitcast.14, bf16[64,64,128]{2,1,0:T(8,128)(2,1)} %copy-done.10, bf16[64,64,128]{2,1,0:T(8,128)(2,1)} %own, bf16[64,64,128]{2,1,0:T(8,128)(2,1)} %collective-permute-done.8.right, ...), custom_call_target="tpu_custom_call" | custom-call | tf_op jit(solution)/shard_map/near/pallas_call | solution.py:217
  (32 shorter events, 0.1 us)
Async XLA Ops:
  0.0 33.8 %copy-start.3 = (f32[64,64]{1,0:T(8,128)S(1)}, f32[64,64]{1,0:T(8,128)}, u32[]{:S(2)}) copy-start(f32[64,64]{1,0:T(8,128)} %refs_0_.1) | copy-start | bytes 49156
  0.0 33.8 %copy-start.4 = (f32[64,64]{1,0:T(8,128)S(1)}, f32[64,64]{1,0:T(8,128)}, u32[]{:S(2)}) copy-start(f32[64,64]{1,0:T(8,128)} %refs_1_.1) | copy-start | bytes 49156
  0.0 19.2 %collective-permute-start = (bf16[64,64,128]{2,1,0:T(8,128)(2,1)}, bf16[64,64,128]{2,1,0:T(8,128)(2,1)S(1)}, u32[]{:S(2)}, u32[]{:S(2)}) collective-permute-start(bf16[64,64,128]{2,1,0:T(8,128)(2,1)} %own), channel_id=1, source_target_pairs={{0,1},{1,2},{2,3},{3,4},{4,5},{5,6},{6,7},{7,8},{8,9},{9,10},{10,1... | collective-permute-start | bytes 3145736 | tf_op jit(solution)/shard_map/ppermute | solution.py:354
  8.9 15.9 %copy-start.11 = (bf16[36,64,128]{2,1,0:T(8,128)(2,1)S(1)}, bf16[36,64,128]{2,1,0:T(8,128)(2,1)}, u32[]{:S(2)}) copy-start(bf16[36,64,128]{2,1,0:T(8,128)(2,1)} %get-tuple-element.33.own) | copy-start | bytes 1769476
  8.9 1.2 %collective-permute-start.1 = (f32[64,64]{1,0:T(8,128)S(1)}, f32[64,64]{1,0:T(8,128)S(1)}, u32[]{:S(2)}, u32[]{:S(2)}) collective-permute-start(f32[64,64]{1,0:T(8,128)S(1)} %get-tuple-element.24), channel_id=1, source_target_pairs={{0,1},{1,0},{2,3},{3,2},{4,5},{5,4},{6,7},{7,6},{8,9},{9,8},{10,11... | collective-permute-start | bytes 49160 | tf_op jit(solution)/shard_map/ppermute | solution.py:364
  10.1 9.0 %collective-permute-start.2 = (f32[64,64]{1,0:T(8,128)S(1)}, f32[64,64]{1,0:T(8,128)S(1)}, u32[]{:S(2)}, u32[]{:S(2)}) collective-permute-start(f32[64,64]{1,0:T(8,128)S(1)} %add.23), channel_id=1, source_target_pairs={{0,2},{1,3},{2,0},{3,1},{4,6},{5,7},{6,4},{7,5},{8,10},{9,11},{10,... | collective-permute-start | bytes 49160 | tf_op jit(solution)/shard_map/ppermute | solution.py:364
  11.3 37.3 %copy-start = (bf16[64,64,128]{2,1,0:T(8,128)(2,1)S(1)}, bf16[64,64,128]{2,1,0:T(8,128)(2,1)}, u32[]{:S(2)}) copy-start(bf16[64,64,128]{2,1,0:T(8,128)(2,1)} %basis.3) | copy-start | bytes 3145732
  11.3 37.3 %copy-start.1 = (bf16[64,64,64]{2,1,0:T(8,128)(2,1)S(1)}, bf16[64,64,64]{2,1,0:T(8,128)(2,1)}, u32[]{:S(2)}) copy-start(bf16[64,64,64]{2,1,0:T(8,128)(2,1)} %child.3) | copy-start | bytes 1572868
  11.3 37.3 %copy-start.2 = (bf16[8,64,64]{2,1,0:T(8,128)(2,1)S(1)}, bf16[8,64,64]{2,1,0:T(8,128)(2,1)}, u32[]{:S(2)}) copy-start(bf16[8,64,64]{2,1,0:T(8,128)(2,1)} %parent.3) | copy-start | bytes 196612
  11.3 37.3 %copy-start.5 = (s32[64,24]{0,1:T(8,128)S(1)}, s32[64,24]{0,1:T(8,128)}, u32[]{:S(2)}) copy-start(s32[64,24]{0,1:T(8,128)} %param.20) | copy-start | bytes 18436
  11.3 37.3 %copy-start.6 = (s32[64,24]{0,1:T(8,128)S(1)}, s32[64,24]{0,1:T(8,128)}, u32[]{:S(2)}) copy-start(s32[64,24]{0,1:T(8,128)} %param.21) | copy-start | bytes 18436
  11.3 37.3 %copy-start.8 = (s32[8,24]{1,0:T(8,128)S(1)}, s32[8,24]{1,0:T(8,128)}, u32[]{:S(2)}) copy-start(s32[8,24]{1,0:T(8,128)} %list1.1) | copy-start | bytes 2308
  11.3 37.3 %copy-start.9 = (s32[8,24]{1,0:T(8,128)S(1)}, s32[8,24]{1,0:T(8,128)}, u32[]{:S(2)}) copy-start(s32[8,24]{1,0:T(8,128)} %op1.1) | copy-start | bytes 2308
  19.2 20.0 %copy-start.10 = (bf16[64,64,128]{2,1,0:T(8,128)(2,1)}, bf16[64,64,128]{2,1,0:T(8,128)(2,1)S(1)}, u32[]{:S(2)}) copy-start(bf16[64,64,128]{2,1,0:T(8,128)(2,1)S(1)} %collective-permute-done.left) | copy-start | bytes 3145732
  19.2 2.8 %collective-permute-start.3 = (f32[64,64]{1,0:T(8,128)S(1)}, f32[64,64]{1,0:T(8,128)S(1)}, u32[]{:S(2)}, u32[]{:S(2)}) collective-permute-start(f32[64,64]{1,0:T(8,128)S(1)} %get-tuple-element.43), channel_id=1, source_target_pairs={{0,4},{1,5},{2,6},{3,7},{4,0},{5,1},{6,2},{7,3},{8,12},{9,13},{10,... | collective-permute-start | bytes 49160 | tf_op jit(solution)/shard_map/ppermute | solution.py:364
  22.0 2.8 %collective-permute-start.4 = (f32[64,64]{1,0:T(8,128)S(1)}, f32[64,64]{1,0:T(8,128)S(1)}, u32[]{:S(2)}, u32[]{:S(2)}) collective-permute-start(f32[64,64]{1,0:T(8,128)S(1)} %add.27), channel_id=1, source_target_pairs={{0,8},{1,9},{2,10},{3,11},{4,12},{5,13},{6,14},{7,15},{8,0},{9,1},... | collective-permute-start | bytes 49160 | tf_op jit(solution)/shard_map/ppermute | solution.py:364
  24.8 17.0 %collective-permute-start.6 = (bf16[36,64,128]{2,1,0:T(8,128)(2,1)S(1)}, bf16[36,64,128]{2,1,0:T(8,128)(2,1)S(1)}, u32[]{:S(2)}, u32[]{:S(2)}) collective-permute-start(bf16[36,64,128]{2,1,0:T(8,128)(2,1)S(1)} %copy-done.11), channel_id=1, source_target_pairs={{0,1},{1,2},{2,3},{3,4},{4,5},{5,6},{6,7},{7,8},{8,9},{9,10},{10,1... | collective-permute-start | bytes 1769480 | tf_op jit(solution)/shard_map/ppermute | solution.py:354
  28.7 17.5 %collective-permute-start.7 = (bf16[36,64,128]{2,1,0:T(8,128)(2,1)S(1)}, bf16[36,64,128]{2,1,0:T(8,128)(2,1)S(1)}, u32[]{:S(2)}, u32[]{:S(2)}) collective-permute-start(bf16[36,64,128]{2,1,0:T(8,128)(2,1)S(1)} %copy-done.11), channel_id=1, source_target_pairs={{1,0},{2,1},{3,2},{4,3},{5,4},{6,5},{7,6},{8,7},{9,8},{10,9},{11,1... | collective-permute-start | bytes 1769480 | tf_op jit(solution)/shard_map/ppermute | solution.py:359
  31.4 7.8 %collective-permute-start.5 = (f32[64,64]{1,0:T(8,128)S(1)}, f32[64,64]{1,0:T(8,128)S(1)}, u32[]{:S(2)}, u32[]{:S(2)}) collective-permute-start(f32[64,64]{1,0:T(8,128)S(1)} %add.28), channel_id=1, source_target_pairs={{0,16},{1,17},{2,18},{3,19},{4,20},{5,21},{6,22},{7,23},{8,24},{9,... | collective-permute-start | bytes 49160 | tf_op jit(solution)/shard_map/ppermute | solution.py:364
  41.8 4.4 %copy-start.12 = (bf16[36,64,128]{2,1,0:T(8,128)(2,1)}, bf16[36,64,128]{2,1,0:T(8,128)(2,1)S(1)}, u32[]{:S(2)}) copy-start(bf16[36,64,128]{2,1,0:T(8,128)(2,1)S(1)} %collective-permute-done.6.left) | copy-start | bytes 1769476
  46.2 2.3 %copy-start.13 = (bf16[36,64,128]{2,1,0:T(8,128)(2,1)}, bf16[36,64,128]{2,1,0:T(8,128)(2,1)S(1)}, u32[]{:S(2)}) copy-start(bf16[36,64,128]{2,1,0:T(8,128)(2,1)S(1)} %collective-permute-done.7.right) | copy-start | bytes 1769476
  46.2 16.4 %collective-permute-start.8 = (bf16[64,64,128]{2,1,0:T(8,128)(2,1)}, bf16[64,64,128]{2,1,0:T(8,128)(2,1)}, u32[]{:S(2)}, u32[]{:S(2)}) collective-permute-start(bf16[64,64,128]{2,1,0:T(8,128)(2,1)} %own), channel_id=1, source_target_pairs={{1,0},{2,1},{3,2},{4,3},{5,4},{6,5},{7,6},{8,7},{9,8},{10,9},{11,1... | collective-permute-start | bytes 3145736 | tf_op jit(solution)/shard_map/ppermute | solution.py:359
  48.6 14.0 %copy-start.7 = (s32[64,6]{0,1:T(8,128)S(1)}, s32[64,6]{0,1:T(8,128)}, u32[]{:S(2)}) copy-start(s32[64,6]{0,1:T(8,128)} %param.15) | copy-start | bytes 4612
